TPU v7x, 128 devices: a whole 4x4x4 slice. The times are simulated.
128 devices in a mesh: seq: 16 (over y, z_lo, core), vis: 8 (over z_hi, x).
Axes of the slice: x: 4, y: 4, z: 4 (z_hi: 2, z_lo: 2; z = z_hi * 2 + z_lo), core: 2. Of those that a mesh axis runs over, the one named last changes fastest.
Arguments:
- text: bfloat16 [4096, 8192], P('seq'), may hold values from -6 to 6
- frames: bfloat16 [4096, 8192], P(('seq', 'vis')), may hold values from -60 to 60
- tile_pos: int32 [4096], P(('seq', 'vis')), may hold values from 0 to 4095, as said below
- frame_count: int32 [128], P(('seq', 'vis')), may hold values from 2 to 32
- doc_ids: int32 [4096], replicated, may hold values from 0 to 3, never falling along the last dimension, each value on 1 to 2048 neighbouring positions
- norm_gain: float32 [8192], replicated, may hold values from 0.1 to 1.9
- w_query: bfloat16 [8192, 8192], P(None, 'vis'), may hold values from -4 to 4
- q_bias: float32 [8192], P('vis'), may hold values from -3 to 3
- w_key: bfloat16 [8192, 1024], P(None, 'vis'), may hold values from -4 to 4
- w_value: bfloat16 [8192, 1024], P(None, 'vis'), may hold values from -0.0625 to 0.0625
- v_bias: float32 [1024], P('vis'), may hold values from -3 to 3
Outputs:
- attended: bfloat16 [4096, 8192], P('seq', 'vis')
Inputs may be any that keep to these rules, and one draw needn't show every extreme that they name: `tile_pos`: all entries together name every position of the window once. Of one device's 32 rows, at most 2 of those below its frame_count fall into one shard of 256 positions, and in every draw one shard receives exactly 2 usable rows from every device. Rows at or beyond the count are unused. `doc_ids`: never falling along the window.
All inputs are finite; a program needn't handle non-finite values.
Results may differ from a plain program's by a relative error of at most 0.0069.
Values may be sent and summed in bfloat16 or wider, within the bound.
A program may use at most 128 MiB of HBM per device.

v0:
```python
import jax
import jax.numpy as jnp
from jax import lax
from jax.sharding import PartitionSpec as P

HEAD_DIM = 128


epsilon = 1e-06
negative = -1e30


def frame_slots(frames, tile_pos, frame_count, shard_rows, owners, capacity):
    row_count = frames.shape[0]
    row_ids = jnp.arange(row_count, dtype=jnp.int32)
    usable = row_ids < frame_count[0]
    owner = jnp.where(usable, tile_pos // shard_rows, owners)
    hits = (owner[:, None] == jnp.arange(owners, dtype=jnp.int32)[None, :]).astype(jnp.int32)
    earlier = (row_ids[:, None] > row_ids[None, :]).astype(jnp.int32)
    before = jnp.dot(earlier, hits, preferred_element_type=jnp.int32)
    rank = jnp.sum(before * hits, axis=1)
    slot_index = owner * capacity + rank
    slot_ids = jnp.arange(owners * capacity, dtype=jnp.int32)
    match = usable[:, None] & (slot_index[:, None] == slot_ids[None, :])
    filled = jnp.any(match, axis=0)
    source = jnp.sum(jnp.where(match, row_ids[:, None], 0), axis=0)
    slot_rows = jnp.where(filled[:, None], frames[source], jnp.zeros((), frames.dtype))
    slot_place = jnp.where(filled, tile_pos[source], -1)
    return (
        slot_rows.reshape(owners, capacity, frames.shape[1]),
        slot_place.reshape(owners, capacity),
    )


def place_frames(text, incoming, incoming_place, first_row):
    local_place = incoming_place - first_row
    lookup = local_place[None, :] == jnp.arange(text.shape[0], dtype=jnp.int32)[:, None]
    covered = jnp.any(lookup, axis=1)
    source = jnp.sum(
        jnp.where(lookup, jnp.arange(local_place.shape[0], dtype=jnp.int32)[None, :], 0), axis=1
    )
    return jnp.where(covered[:, None], incoming[source], text)


def attend_block(
    block_state, query_rows, query_place, query_docs, key_block, key_place, key_docs, kv_heads
):
    row_peak, row_total, summed = block_state
    row_count = query_rows.shape[0]
    grouped = query_rows.reshape(row_count, kv_heads, -1, HEAD_DIM)
    key_width = kv_heads * HEAD_DIM
    key_part = key_block[:, :key_width].reshape(-1, kv_heads, HEAD_DIM)
    value_part = key_block[:, key_width:].reshape(-1, kv_heads, HEAD_DIM)
    scores = jnp.einsum(
        "qgjd,kgd->qgjk", grouped, key_part, preferred_element_type=jnp.float32
    ) * HEAD_DIM ** (-0.5)
    allowed = (key_place[None, :] <= query_place[:, None]) & (
        key_docs[None, :] == query_docs[:, None]
    )
    allowed = allowed[:, None, None, :]
    block_peak = jnp.max(jnp.where(allowed, scores, negative), axis=3)
    new_peak = jnp.maximum(row_peak, block_peak)
    raised = jnp.where(allowed, jnp.exp(scores - new_peak[..., None]), 0.0)
    factor = jnp.exp(row_peak - new_peak)
    new_total = row_total * factor + jnp.sum(raised, axis=3)
    product = jnp.einsum(
        "qgjk,kgd->qgjd",
        raised.astype(jnp.bfloat16),
        value_part,
        preferred_element_type=jnp.float32,
    )
    return (new_peak, new_total, summed * factor[..., None] + product)


def on_device(
    text, frames, tile_pos, frame_count, doc_ids, norm_gain, w_query, q_bias, w_key, w_value, v_bias
):
    seq_count = lax.axis_size("seq")
    vis_count = lax.axis_size("vis")
    shard_index = lax.axis_index("seq")
    shard_rows = text.shape[0]
    capacity = shard_rows // (seq_count * vis_count)
    first_row = shard_index * shard_rows
    slot_rows, slot_place = frame_slots(
        frames, tile_pos, frame_count, shard_rows, seq_count, capacity
    )
    wide_rows = jnp.broadcast_to(slot_rows[:, None], (seq_count, vis_count) + slot_rows.shape[1:])
    wide_rows = wide_rows.reshape(seq_count * vis_count, capacity, slot_rows.shape[2])
    wide_place = jnp.broadcast_to(slot_place[:, None], (seq_count, vis_count, capacity))
    wide_place = wide_place.reshape(seq_count * vis_count, capacity)
    incoming, incoming_place = (
        lax.all_to_all(wide_rows, ("seq", "vis"), split_axis=0, concat_axis=0, tiled=True),
        lax.all_to_all(wide_place, ("seq", "vis"), split_axis=0, concat_axis=0, tiled=True),
    )
    incoming = incoming.reshape(-1, incoming.shape[-1])
    incoming_place = incoming_place.reshape(-1)
    merged = place_frames(text, incoming, incoming_place, first_row)
    widened = merged.astype(jnp.float32)
    mean_square = jnp.mean(widened * widened, axis=1, keepdims=True)
    normed = (widened * lax.rsqrt(mean_square + epsilon) * norm_gain).astype(jnp.bfloat16)
    queries = (jnp.dot(normed, w_query, preferred_element_type=jnp.float32) + q_bias).astype(
        jnp.bfloat16
    )
    key_rows = jnp.dot(normed, w_key, preferred_element_type=jnp.float32).astype(jnp.bfloat16)
    value_rows = (jnp.dot(normed, w_value, preferred_element_type=jnp.float32) + v_bias).astype(
        jnp.bfloat16
    )
    keyval = jnp.concatenate([key_rows, value_rows], axis=1)
    kv_heads = w_key.shape[1] // HEAD_DIM
    per_group = w_query.shape[1] // HEAD_DIM // kv_heads
    own_place = first_row + jnp.arange(shard_rows, dtype=jnp.int32)
    own_docs = lax.dynamic_slice_in_dim(doc_ids, first_row, shard_rows)
    blocks = [(queries, own_place, own_docs)]
    initial = tuple(
        (
            (
                jnp.full((entry[0].shape[0], kv_heads, per_group), negative, jnp.float32),
                jnp.zeros((entry[0].shape[0], kv_heads, per_group), jnp.float32),
                jnp.zeros((entry[0].shape[0], kv_heads, per_group, HEAD_DIM), jnp.float32),
            )
            for entry in blocks
        )
    )
    incoming_keys = lax.all_gather(keyval, "seq", axis=0, tiled=True)
    piece_rows = incoming_keys.shape[0]
    step_rows = 512

    def one_step(step_index, current):
        key_first = step_index * step_rows
        key_block = lax.dynamic_slice_in_dim(incoming_keys, step_index * step_rows, step_rows)
        key_place = key_first + jnp.arange(step_rows, dtype=jnp.int32)
        key_docs = lax.dynamic_slice_in_dim(doc_ids, key_first, step_rows)
        updated = []
        for entry, block_state in zip(blocks, current):
            query_rows, query_place, query_docs = entry

            def compute(
                operand, query_rows=query_rows, query_place=query_place, query_docs=query_docs
            ):
                return attend_block(
                    operand,
                    query_rows,
                    query_place,
                    query_docs,
                    key_block,
                    key_place,
                    key_docs,
                    kv_heads,
                )

            def unchanged(operand):
                return operand

            updated.append(lax.cond(key_first <= query_place[-1], compute, unchanged, block_state))
        return tuple(updated)

    finals = lax.fori_loop(0, piece_rows // step_rows, one_step, initial)
    outputs = [
        (summed / row_total[..., None]).reshape(summed.shape[0], -1).astype(jnp.bfloat16)
        for row_peak, row_total, summed in finals
    ]
    return outputs[0]


def solution(mesh):
    in_specs = (
        P("seq", None),
        P(("seq", "vis"), None),
        P(("seq", "vis")),
        P(("seq", "vis")),
        P(),
        P(),
        P(None, "vis"),
        P("vis"),
        P(None, "vis"),
        P(None, "vis"),
        P("vis"),
    )
    out_specs = P("seq", "vis")
    return jax.shard_map(
        on_device, mesh=mesh, in_specs=in_specs, out_specs=out_specs, check_vma=False
    )
```

profile of v0, /device:TPU:57, one launch (start us, length us, event | category | flops | bytes accessed | tf_op | source)
XLA Modules:
  0.0 259.8 jit_solution(562289550122915700)
XLA Ops:
  11.2 10.4 %all-to-all-start = ((s32[128,1,2]{2,1,0:T(1,128)}), s32[128,1,2]{2,1,0:T(1,128)S(1)}, u32[]{:S(2)}, u32[]{:S(2)}) async-start(s32[128,1,2]{2,1,0:T(1,128)} %bitcast.16), calls=%async_computation | async-start | bytes 131072 | tf_op jit(solution)/shard_map/all_to_all | solution.py:93
  25.0 3.7 %all-to-all-done = s32[128,1,2]{2,1,0:T(1,128)S(1)} async-done(((s32[128,1,2]{2,1,0:T(1,128)}), s32[128,1,2]{2,1,0:T(1,128)S(1)}, u32[]{:S(2)}, u32[]{:S(2)}) %all-to-all-start) | async-done | bytes 1056 | tf_op jit(solution)/shard_map/all_to_all | solution.py:93
  28.7 6.1 %broadcast_in_dim.133 = bf16[16,8,2,8192]{3,2,1,0:T(2,128)(2,1)} broadcast(bf16[16,2,8192]{2,1,0:T(2,128)(2,1)S(1)} %broadcast_select_fusion.1), dimensions={0,2,3} | broadcast | bytes 4718592 | tf_op jit(solution)/shard_map/broadcast_in_dim | solution.py:87
  34.8 8.2 %all-to-all-start.1 = ((bf16[128,2,8192]{2,1,0:T(2,128)(2,1)}), bf16[128,2,8192]{2,1,0:T(2,128)(2,1)}, u32[]{:S(2)}, u32[]{:S(2)}) async-start(bf16[128,2,8192]{2,1,0:T(2,128)(2,1)} %bitcast.83), calls=%async_computation.1 | async-start | bytes 8388608 | tf_op jit(solution)/shard_map/all_to_all | solution.py:92
  43.6 48.8 %all-to-all-done.1 = bf16[128,2,8192]{2,1,0:T(2,128)(2,1)} async-done(((bf16[128,2,8192]{2,1,0:T(2,128)(2,1)}), bf16[128,2,8192]{2,1,0:T(2,128)(2,1)}, u32[]{:S(2)}, u32[]{:S(2)}) %all-to-all-start.1) | async-done | bytes 4194336 | tf_op jit(solution)/shard_map/all_to_all | solution.py:92
  92.5 7.2 %reshape.191 = bf16[256,8192]{1,0:T(8,128)(2,1)} reshape(bf16[128,2,8192]{2,1,0:T(2,128)(2,1)} %all-to-all-done.1) | data formatting | bytes 8388608 | tf_op jit(solution)/shard_map/reshape | solution.py:95
  99.7 11.7 %gather_fusion.2 = bf16[256,8192]{1,0:T(8,128)(2,1)} fusion(bf16[256,8192]{1,0:T(8,128)(2,1)} %reshape.191, s32[1024]{0:T(1024)S(1)} %pad_clamp_fusion), kind=kCustom, calls=%fused_computation.2 | custom fusion | bytes 8389632 | tf_op jit(solution)/shard_map/gather | solution.py:42
  111.3 5.1 %fusion.22 = f32[256]{0:T(256)S(1)} fusion(bf16[256,8192]{1,0:T(8,128)(2,1)} %gather_fusion.2, bf16[256,8192]{1,0:T(8,128)(2,1)} %param.15, pred[256]{0:T(512)(128)(4,1)S(1)} %fusion.28), kind=kLoop, calls=%fused_computation.31 | loop fusion | flops 8388352 | bytes 8389888 | tf_op jit(solution)/shard_map/reduce_sum | solution.py:99
  126.2 12.3 %fusion.25 = bf16[256,1024]{1,0:T(8,128)(2,1)} fusion(bf16[256,8192]{1,0:T(8,128)(2,1)} %copy-done.2, bf16[8192,1024]{1,0:T(8,128)(2,1)} %param.21, f32[1024]{0:T(1024)S(1)} %copy-done.8), kind=kOutput, calls=%fused_computation.36 | convolution fusion | flops 4295491584 | bytes 21499904 | tf_op jit(solution)/shard_map/dot_general | solution.py:101
  138.5 22.6 %all-gather.2.cloned.1.call-done = bf16[4096,256]{0,1:T(8,128)(2,1)} async-done(((bf16[256,256]{0,1:T(8,128)(2,1)}), bf16[4096,256]{0,1:T(8,128)(2,1)}) %all-gather.2.cloned.1.call-update) | async-done | bytes 2097168 | tf_op jit(solution)/shard_map/all_gather | solution.py:124
  161.1 4.1 %copy.30 = bf16[4096,256]{1,0:T(8,128)(2,1)} copy(bf16[4096,256]{0,1:T(8,128)(2,1)} %all-gather.2.cloned.1.call-done) | data formatting | bytes 4194304 | tf_op jit(solution)/shard_map/while | solution.py:157
  165.3 84.8 %while.17 = (s32[]{:T(128)}, f32[256,1,8]{0,2,1:T(8,128)S(1)}, f32[256,1,8]{0,2,1:T(8,128)S(1)}, f32[256,1,8,128]{0,3,2,1:T(8,128)S(1)}, s32[256]{0:T(256)S(1)},...) while((s32[]{:T(128)}, f32[256,1,8]{0,2,1:T(8,128)S(1)}, ...), condition=%wide.region_11.12_spmd, body=%wide.region_6.11_spmd.sunk | while | flops 549329408 | bytes 32915828 | solution.py:157
  166.6 9.3 %conditional.2 = ((f32[256,1,8]{0,2,1:T(8,128)S(1)}, f32[256,1,8]{0,2,1:T(8,128)S(1)}, f32[256,1,8,128]{0,3,2,1:T(8,128)S(1)})) conditional(s32[]{:T(128)} %convert_element_type.65, (f32[256,1,8]{0,2,1:T(8,128)S(1)}, f32[256,1,8]{0,2,1:T(8,128)S(1)}, f32[256,1,8,128]{0,3,2,1:T(8,128)S(1)}) %tuple.52, (s32[]{:T(128)}, s32[512]{0:T(512)S(1)}, ...), branch_computations={%region_7.7_spmd, %region_8.10_spmd} | conditional | flops 549329408 | bytes 32913534 | solution.py:154
  167.6 3.8 %fusion = (f32[256,8]{0,1:T(8,128)S(1)}, f32[512,256,8]{1,0,2:T(8,128)}) fusion(pred[256,512]{0,1:T(8,128)(4,1)S(1)} %compare_and_fusion, bf16[4096,256]{1,0:T(8,128)(2,1)} %get-tuple-element.272, s32[]{:T(128)S(6)} %select_n.70, bf16[256,1024]{1,0:T(8,128)(2,1)} %get-tuple-element.273), kind=kOutput, calls=%fused_computation.5 | convolution fusion | flops 271579136 | bytes 4988932 | tf_op jit(solution)/shard_map/while/body/eval_jaxpr/cond/branch_1_fun/qgjd,kgd->qgjk/dot_general | solution.py:54
  177.2 9.3 %conditional.2 = ((f32[256,1,8]{0,2,1:T(8,128)S(1)}, f32[256,1,8]{0,2,1:T(8,128)S(1)}, f32[256,1,8,128]{0,3,2,1:T(8,128)S(1)})) conditional(s32[]{:T(128)} %convert_element_type.65, (f32[256,1,8]{0,2,1:T(8,128)S(1)}, f32[256,1,8]{0,2,1:T(8,128)S(1)}, f32[256,1,8,128]{0,3,2,1:T(8,128)S(1)}) %tuple.52, (s32[]{:T(128)}, s32[512]{0:T(512)S(1)}, ...), branch_computations={%region_7.7_spmd, %region_8.10_spmd} | conditional | flops 549329408 | bytes 32913534 | solution.py:154
  178.2 3.8 %fusion = (f32[256,8]{0,1:T(8,128)S(1)}, f32[512,256,8]{1,0,2:T(8,128)}) fusion(pred[256,512]{0,1:T(8,128)(4,1)S(1)} %compare_and_fusion, bf16[4096,256]{1,0:T(8,128)(2,1)} %get-tuple-element.272, s32[]{:T(128)S(6)} %select_n.70, bf16[256,1024]{1,0:T(8,128)(2,1)} %get-tuple-element.273), kind=kOutput, calls=%fused_computation.5 | convolution fusion | flops 271579136 | bytes 4988932 | tf_op jit(solution)/shard_map/while/body/eval_jaxpr/cond/branch_1_fun/qgjd,kgd->qgjk/dot_general | solution.py:54
  182.0 3.6 %fusion.12 = f32[256,1,8,128]{0,3,2,1:T(8,128)S(1)} fusion(f32[512,256,8]{1,0,2:T(8,128)} %get-tuple-element.350, f32[256,8]{0,1:T(8,128)S(1)} %bitcast.84, pred[256,512]{0,1:T(8,128)(4,1)S(1)} %compare_and_fusion, f32[256,1,8,128]{0,3,2,1:T(8,128)S(1)} %get-tuple-element.275, f32[256,8]{0,1:T(8,128)S(1)} %get-tuple-element.347, ...), kind=kOutput, calls=%fused_computation.14 | convolution fusion | flops 273154048 | bytes 6569992 | tf_op jit(solution)/shard_map/while/body/eval_jaxpr/cond/branch_1_fun/qgjk,kgd->qgjd/dot_general | solution.py:66
  187.7 9.3 %conditional.2 = ((f32[256,1,8]{0,2,1:T(8,128)S(1)}, f32[256,1,8]{0,2,1:T(8,128)S(1)}, f32[256,1,8,128]{0,3,2,1:T(8,128)S(1)})) conditional(s32[]{:T(128)} %convert_element_type.65, (f32[256,1,8]{0,2,1:T(8,128)S(1)}, f32[256,1,8]{0,2,1:T(8,128)S(1)}, f32[256,1,8,128]{0,3,2,1:T(8,128)S(1)}) %tuple.52, (s32[]{:T(128)}, s32[512]{0:T(512)S(1)}, ...), branch_computations={%region_7.7_spmd, %region_8.10_spmd} | conditional | flops 549329408 | bytes 32913534 | solution.py:154
  188.8 3.8 %fusion = (f32[256,8]{0,1:T(8,128)S(1)}, f32[512,256,8]{1,0,2:T(8,128)}) fusion(pred[256,512]{0,1:T(8,128)(4,1)S(1)} %compare_and_fusion, bf16[4096,256]{1,0:T(8,128)(2,1)} %get-tuple-element.272, s32[]{:T(128)S(6)} %select_n.70, bf16[256,1024]{1,0:T(8,128)(2,1)} %get-tuple-element.273), kind=kOutput, calls=%fused_computation.5 | convolution fusion | flops 271579136 | bytes 4988932 | tf_op jit(solution)/shard_map/while/body/eval_jaxpr/cond/branch_1_fun/qgjd,kgd->qgjk/dot_general | solution.py:54
  192.6 3.6 %fusion.12 = f32[256,1,8,128]{0,3,2,1:T(8,128)S(1)} fusion(f32[512,256,8]{1,0,2:T(8,128)} %get-tuple-element.350, f32[256,8]{0,1:T(8,128)S(1)} %bitcast.84, pred[256,512]{0,1:T(8,128)(4,1)S(1)} %compare_and_fusion, f32[256,1,8,128]{0,3,2,1:T(8,128)S(1)} %get-tuple-element.275, f32[256,8]{0,1:T(8,128)S(1)} %get-tuple-element.347, ...), kind=kOutput, calls=%fused_computation.14 | convolution fusion | flops 273154048 | bytes 6569992 | tf_op jit(solution)/shard_map/while/body/eval_jaxpr/cond/branch_1_fun/qgjk,kgd->qgjd/dot_general | solution.py:66
  198.3 9.3 %conditional.2 = ((f32[256,1,8]{0,2,1:T(8,128)S(1)}, f32[256,1,8]{0,2,1:T(8,128)S(1)}, f32[256,1,8,128]{0,3,2,1:T(8,128)S(1)})) conditional(s32[]{:T(128)} %convert_element_type.65, (f32[256,1,8]{0,2,1:T(8,128)S(1)}, f32[256,1,8]{0,2,1:T(8,128)S(1)}, f32[256,1,8,128]{0,3,2,1:T(8,128)S(1)}) %tuple.52, (s32[]{:T(128)}, s32[512]{0:T(512)S(1)}, ...), branch_computations={%region_7.7_spmd, %region_8.10_spmd} | conditional | flops 549329408 | bytes 32913534 | solution.py:154
  199.3 3.8 %fusion = (f32[256,8]{0,1:T(8,128)S(1)}, f32[512,256,8]{1,0,2:T(8,128)}) fusion(pred[256,512]{0,1:T(8,128)(4,1)S(1)} %compare_and_fusion, bf16[4096,256]{1,0:T(8,128)(2,1)} %get-tuple-element.272, s32[]{:T(128)S(6)} %select_n.70, bf16[256,1024]{1,0:T(8,128)(2,1)} %get-tuple-element.273), kind=kOutput, calls=%fused_computation.5 | convolution fusion | flops 271579136 | bytes 4988932 | tf_op jit(solution)/shard_map/while/body/eval_jaxpr/cond/branch_1_fun/qgjd,kgd->qgjk/dot_general | solution.py:54
  203.2 3.6 %fusion.12 = f32[256,1,8,128]{0,3,2,1:T(8,128)S(1)} fusion(f32[512,256,8]{1,0,2:T(8,128)} %get-tuple-element.350, f32[256,8]{0,1:T(8,128)S(1)} %bitcast.84, pred[256,512]{0,1:T(8,128)(4,1)S(1)} %compare_and_fusion, f32[256,1,8,128]{0,3,2,1:T(8,128)S(1)} %get-tuple-element.275, f32[256,8]{0,1:T(8,128)S(1)} %get-tuple-element.347, ...), kind=kOutput, calls=%fused_computation.14 | convolution fusion | flops 273154048 | bytes 6569992 | tf_op jit(solution)/shard_map/while/body/eval_jaxpr/cond/branch_1_fun/qgjk,kgd->qgjd/dot_general | solution.py:66
  208.9 9.3 %conditional.2 = ((f32[256,1,8]{0,2,1:T(8,128)S(1)}, f32[256,1,8]{0,2,1:T(8,128)S(1)}, f32[256,1,8,128]{0,3,2,1:T(8,128)S(1)})) conditional(s32[]{:T(128)} %convert_element_type.65, (f32[256,1,8]{0,2,1:T(8,128)S(1)}, f32[256,1,8]{0,2,1:T(8,128)S(1)}, f32[256,1,8,128]{0,3,2,1:T(8,128)S(1)}) %tuple.52, (s32[]{:T(128)}, s32[512]{0:T(512)S(1)}, ...), branch_computations={%region_7.7_spmd, %region_8.10_spmd} | conditional | flops 549329408 | bytes 32913534 | solution.py:154
  209.9 3.8 %fusion = (f32[256,8]{0,1:T(8,128)S(1)}, f32[512,256,8]{1,0,2:T(8,128)}) fusion(pred[256,512]{0,1:T(8,128)(4,1)S(1)} %compare_and_fusion, bf16[4096,256]{1,0:T(8,128)(2,1)} %get-tuple-element.272, s32[]{:T(128)S(6)} %select_n.70, bf16[256,1024]{1,0:T(8,128)(2,1)} %get-tuple-element.273), kind=kOutput, calls=%fused_computation.5 | convolution fusion | flops 271579136 | bytes 4988932 | tf_op jit(solution)/shard_map/while/body/eval_jaxpr/cond/branch_1_fun/qgjd,kgd->qgjk/dot_general | solution.py:54
  219.5 9.3 %conditional.2 = ((f32[256,1,8]{0,2,1:T(8,128)S(1)}, f32[256,1,8]{0,2,1:T(8,128)S(1)}, f32[256,1,8,128]{0,3,2,1:T(8,128)S(1)})) conditional(s32[]{:T(128)} %convert_element_type.65, (f32[256,1,8]{0,2,1:T(8,128)S(1)}, f32[256,1,8]{0,2,1:T(8,128)S(1)}, f32[256,1,8,128]{0,3,2,1:T(8,128)S(1)}) %tuple.52, (s32[]{:T(128)}, s32[512]{0:T(512)S(1)}, ...), branch_computations={%region_7.7_spmd, %region_8.10_spmd} | conditional | flops 549329408 | bytes 32913534 | solution.py:154
  220.5 3.8 %fusion = (f32[256,8]{0,1:T(8,128)S(1)}, f32[512,256,8]{1,0,2:T(8,128)}) fusion(pred[256,512]{0,1:T(8,128)(4,1)S(1)} %compare_and_fusion, bf16[4096,256]{1,0:T(8,128)(2,1)} %get-tuple-element.272, s32[]{:T(128)S(6)} %select_n.70, bf16[256,1024]{1,0:T(8,128)(2,1)} %get-tuple-element.273), kind=kOutput, calls=%fused_computation.5 | convolution fusion | flops 271579136 | bytes 4988932 | tf_op jit(solution)/shard_map/while/body/eval_jaxpr/cond/branch_1_fun/qgjd,kgd->qgjk/dot_general | solution.py:54
  230.1 9.3 %conditional.2 = ((f32[256,1,8]{0,2,1:T(8,128)S(1)}, f32[256,1,8]{0,2,1:T(8,128)S(1)}, f32[256,1,8,128]{0,3,2,1:T(8,128)S(1)})) conditional(s32[]{:T(128)} %convert_element_type.65, (f32[256,1,8]{0,2,1:T(8,128)S(1)}, f32[256,1,8]{0,2,1:T(8,128)S(1)}, f32[256,1,8,128]{0,3,2,1:T(8,128)S(1)}) %tuple.52, (s32[]{:T(128)}, s32[512]{0:T(512)S(1)}, ...), branch_computations={%region_7.7_spmd, %region_8.10_spmd} | conditional | flops 549329408 | bytes 32913534 | solution.py:154
  231.1 3.8 %fusion = (f32[256,8]{0,1:T(8,128)S(1)}, f32[512,256,8]{1,0,2:T(8,128)}) fusion(pred[256,512]{0,1:T(8,128)(4,1)S(1)} %compare_and_fusion, bf16[4096,256]{1,0:T(8,128)(2,1)} %get-tuple-element.272, s32[]{:T(128)S(6)} %select_n.70, bf16[256,1024]{1,0:T(8,128)(2,1)} %get-tuple-element.273), kind=kOutput, calls=%fused_computation.5 | convolution fusion | flops 271579136 | bytes 4988932 | tf_op jit(solution)/shard_map/while/body/eval_jaxpr/cond/branch_1_fun/qgjd,kgd->qgjk/dot_general | solution.py:54
  235.0 3.6 %fusion.12 = f32[256,1,8,128]{0,3,2,1:T(8,128)S(1)} fusion(f32[512,256,8]{1,0,2:T(8,128)} %get-tuple-element.350, f32[256,8]{0,1:T(8,128)S(1)} %bitcast.84, pred[256,512]{0,1:T(8,128)(4,1)S(1)} %compare_and_fusion, f32[256,1,8,128]{0,3,2,1:T(8,128)S(1)} %get-tuple-element.275, f32[256,8]{0,1:T(8,128)S(1)} %get-tuple-element.347, ...), kind=kOutput, calls=%fused_computation.14 | convolution fusion | flops 273154048 | bytes 6569992 | tf_op jit(solution)/shard_map/while/body/eval_jaxpr/cond/branch_1_fun/qgjk,kgd->qgjd/dot_general | solution.py:66
  240.7 9.3 %conditional.2 = ((f32[256,1,8]{0,2,1:T(8,128)S(1)}, f32[256,1,8]{0,2,1:T(8,128)S(1)}, f32[256,1,8,128]{0,3,2,1:T(8,128)S(1)})) conditional(s32[]{:T(128)} %convert_element_type.65, (f32[256,1,8]{0,2,1:T(8,128)S(1)}, f32[256,1,8]{0,2,1:T(8,128)S(1)}, f32[256,1,8,128]{0,3,2,1:T(8,128)S(1)}) %tuple.52, (s32[]{:T(128)}, s32[512]{0:T(512)S(1)}, ...), branch_computations={%region_7.7_spmd, %region_8.10_spmd} | conditional | flops 549329408 | bytes 32913534 | solution.py:154
  241.7 3.8 %fusion = (f32[256,8]{0,1:T(8,128)S(1)}, f32[512,256,8]{1,0,2:T(8,128)}) fusion(pred[256,512]{0,1:T(8,128)(4,1)S(1)} %compare_and_fusion, bf16[4096,256]{1,0:T(8,128)(2,1)} %get-tuple-element.272, s32[]{:T(128)S(6)} %select_n.70, bf16[256,1024]{1,0:T(8,128)(2,1)} %get-tuple-element.273), kind=kOutput, calls=%fused_computation.5 | convolution fusion | flops 271579136 | bytes 4988932 | tf_op jit(solution)/shard_map/while/body/eval_jaxpr/cond/branch_1_fun/qgjd,kgd->qgjk/dot_general | solution.py:54
  (144 shorter events, 54.4 us)
Async XLA Ops:
  6.5 113.5 %copy-start = (bf16[8192,128]{1,0:T(8,128)(2,1)S(1)}, bf16[8192,128]{1,0:T(8,128)(2,1)}, u32[]{:S(2)}) copy-start(bf16[8192,128]{1,0:T(8,128)(2,1)} %param.23) | copy-start | bytes 6291460
  11.2 17.4 %all-to-all-start = ((s32[128,1,2]{2,1,0:T(1,128)}), s32[128,1,2]{2,1,0:T(1,128)S(1)}, u32[]{:S(2)}, u32[]{:S(2)}) async-start(s32[128,1,2]{2,1,0:T(1,128)} %bitcast.16), calls=%async_computation | async-start | bytes 131072 | tf_op jit(solution)/shard_map/all_to_all | solution.py:93
  34.8 57.7 %all-to-all-start.1 = ((bf16[128,2,8192]{2,1,0:T(2,128)(2,1)}), bf16[128,2,8192]{2,1,0:T(2,128)(2,1)}, u32[]{:S(2)}, u32[]{:S(2)}) async-start(bf16[128,2,8192]{2,1,0:T(2,128)(2,1)} %bitcast.83), calls=%async_computation.1 | async-start | bytes 8388608 | tf_op jit(solution)/shard_map/all_to_all | solution.py:92
  43.0 118.1 %all-gather.2.cloned.1.call-start = ((), (), s32[]{:S(2)}) async-start(), calls=%async_computation.2 | async-start | bytes 2228224 | tf_op jit(solution)/shard_map/all_gather | solution.py:124
  99.7 16.8 %copy-start.6 = (f32[8192]{0:T(1024)S(1)}, f32[8192]{0:T(1024)}, u32[]{:S(2)}) copy-start(f32[8192]{0:T(1024)} %param.20) | copy-start | bytes 98308
  111.3 5.2 %copy-start.3 = (bf16[256,8192]{1,0:T(8,128)(2,1)S(1)}, bf16[256,8192]{1,0:T(8,128)(2,1)}, u32[]{:S(2)}) copy-start(bf16[256,8192]{1,0:T(8,128)(2,1)} %gather_fusion.2) | copy-start | bytes 12582916
  111.3 5.9 %copy-start.4 = (bf16[256,8192]{1,0:T(8,128)(2,1)S(1)}, bf16[256,8192]{1,0:T(8,128)(2,1)}, u32[]{:S(2)}) copy-start(bf16[256,8192]{1,0:T(8,128)(2,1)} %param.15) | copy-start | bytes 12582916
  120.1 4.7 %copy-start.2 = (bf16[256,8192]{1,0:T(8,128)(2,1)}, bf16[256,8192]{1,0:T(8,128)(2,1)S(1)}, u32[]{:S(2)}) copy-start(bf16[256,8192]{1,0:T(8,128)(2,1)S(1)} %fusion.24) | copy-start | bytes 12582916
  120.1 3.1 %copy-start.5 = (bf16[8192,128]{1,0:T(8,128)(2,1)S(1)}, bf16[8192,128]{1,0:T(8,128)(2,1)}, u32[]{:S(2)}) copy-start(bf16[8192,128]{1,0:T(8,128)(2,1)} %param.24) | copy-start | bytes 6291460
  120.1 3.1 %copy-start.7 = (f32[128]{0:T(128)S(1)}, f32[128]{0:T(128)}, u32[]{:S(2)}) copy-start(f32[128]{0:T(128)} %param.25) | copy-start | bytes 1540
  123.2 3.0 %copy-start.8 = (f32[1024]{0:T(1024)S(1)}, f32[1024]{0:T(1024)}, u32[]{:S(2)}) copy-start(f32[1024]{0:T(1024)} %param.22) | copy-start | bytes 12292
  171.4 3.6 %copy-start.1 = (f32[512,256,8]{1,0,2:T(8,128)S(1)}, f32[512,256,8]{1,0,2:T(8,128)}, u32[]{:S(2)}) copy-start(f32[512,256,8]{1,0,2:T(8,128)} %get-tuple-element.350) | copy-start | bytes 12582916 | tf_op jit(solution)/shard_map/while/body/eval_jaxpr/cond
  182.0 3.6 %copy-start.1 = (f32[512,256,8]{1,0,2:T(8,128)S(1)}, f32[512,256,8]{1,0,2:T(8,128)}, u32[]{:S(2)}) copy-start(f32[512,256,8]{1,0,2:T(8,128)} %get-tuple-element.350) | copy-start | bytes 12582916 | tf_op jit(solution)/shard_map/while/body/eval_jaxpr/cond
  192.6 3.6 %copy-start.1 = (f32[512,256,8]{1,0,2:T(8,128)S(1)}, f32[512,256,8]{1,0,2:T(8,128)}, u32[]{:S(2)}) copy-start(f32[512,256,8]{1,0,2:T(8,128)} %get-tuple-element.350) | copy-start | bytes 12582916 | tf_op jit(solution)/shard_map/while/body/eval_jaxpr/cond
  203.2 3.6 %copy-start.1 = (f32[512,256,8]{1,0,2:T(8,128)S(1)}, f32[512,256,8]{1,0,2:T(8,128)}, u32[]{:S(2)}) copy-start(f32[512,256,8]{1,0,2:T(8,128)} %get-tuple-element.350) | copy-start | bytes 12582916 | tf_op jit(solution)/shard_map/while/body/eval_jaxpr/cond
  213.8 3.6 %copy-start.1 = (f32[512,256,8]{1,0,2:T(8,128)S(1)}, f32[512,256,8]{1,0,2:T(8,128)}, u32[]{:S(2)}) copy-start(f32[512,256,8]{1,0,2:T(8,128)} %get-tuple-element.350) | copy-start | bytes 12582916 | tf_op jit(solution)/shard_map/while/body/eval_jaxpr/cond
  224.4 3.6 %copy-start.1 = (f32[512,256,8]{1,0,2:T(8,128)S(1)}, f32[512,256,8]{1,0,2:T(8,128)}, u32[]{:S(2)}) copy-start(f32[512,256,8]{1,0,2:T(8,128)} %get-tuple-element.350) | copy-start | bytes 12582916 | tf_op jit(solution)/shard_map/while/body/eval_jaxpr/cond
  235.0 3.6 %copy-start.1 = (f32[512,256,8]{1,0,2:T(8,128)S(1)}, f32[512,256,8]{1,0,2:T(8,128)}, u32[]{:S(2)}) copy-start(f32[512,256,8]{1,0,2:T(8,128)} %get-tuple-element.350) | copy-start | bytes 12582916 | tf_op jit(solution)/shard_map/while/body/eval_jaxpr/cond
  245.5 3.6 %copy-start.1 = (f32[512,256,8]{1,0,2:T(8,128)S(1)}, f32[512,256,8]{1,0,2:T(8,128)}, u32[]{:S(2)}) copy-start(f32[512,256,8]{1,0,2:T(8,128)} %get-tuple-element.350) | copy-start | bytes 12582916 | tf_op jit(solution)/shard_map/while/body/eval_jaxpr/cond
Sparse Core Ops, SparseCore 0:
  125.5 35.5 all-gather.1
where the time goes:
time: 261 us; the launch traced here: 260 us
  waiting for transfers between devices  75.1 us (29%)
  matrix products  74.8 us (29%)
  local copies, waits for them, and re-layouts  50.3 us (19%)
  other arithmetic  20.7 us (8%)
  starting transfers between devices  18.6 us (7%)
  between operations  14.4 us (6%)
  loops' own time  5.92 us (2%)
    all_to_all x1, waiting for transfers between devices, on_device(): lax.all_to_all(wide_rows, ('seq', 'vis'), split_axis=0, concat_axis=0, ti...  48.8 us
    dot_general x8, matrix products, attend_block(): jnp.einsum('qgjd,kgd->qgjk', grouped, key_part, preferred_element_type=jn...  30.6 us
    dot_general x8, matrix products, attend_block(): jnp.einsum('qgjk,kgd->qgjd', raised.astype(jnp.bfloat16), value_part, pre...  28.5 us
    all_gather x1, waiting for transfers between devices, on_device(): incoming_keys = lax.all_gather(keyval, 'seq', axis=0, tiled=True)  22.6 us
    dot_general x1, matrix products, on_device(): jnp.dot(normed, w_query, preferred_element_type=jnp.float32) + q_bias  12.3 us
    gather x1, local copies, waits for them, and re-layouts, place_frames(): return jnp.where(covered[:, None], incoming[source], text)  11.7 us
    all_to_all x1, starting transfers between devices, on_device(): lax.all_to_all(wide_place, ('seq', 'vis'), split_axis=0, concat_axis=0, t...  10.4 us
    all_to_all x1, starting transfers between devices, on_device(): lax.all_to_all(wide_rows, ('seq', 'vis'), split_axis=0, concat_axis=0, ti...  8.19 us
  transfers between devices with their start and end apart: 3, of which 3 were waited for; matrix products, arithmetic and copies ran while one was open for 7% of the time, Pallas kernels for 0%

commit v1 on v0

--- a/solution.py
+++ b/solution.py
@@ -2,6 +2,8 @@
 import jax.numpy as jnp
 from jax import lax
 from jax.sharding import PartitionSpec as P
+from jax.experimental import pallas as pl
+from jax.experimental.pallas import tpu as pltpu
 
 HEAD_DIM = 128
 
@@ -42,36 +44,6 @@
     return jnp.where(covered[:, None], incoming[source], text)
 
 
-def attend_block(
-    block_state, query_rows, query_place, query_docs, key_block, key_place, key_docs, kv_heads
-):
-    row_peak, row_total, summed = block_state
-    row_count = query_rows.shape[0]
-    grouped = query_rows.reshape(row_count, kv_heads, -1, HEAD_DIM)
-    key_width = kv_heads * HEAD_DIM
-    key_part = key_block[:, :key_width].reshape(-1, kv_heads, HEAD_DIM)
-    value_part = key_block[:, key_width:].reshape(-1, kv_heads, HEAD_DIM)
-    scores = jnp.einsum(
-        "qgjd,kgd->qgjk", grouped, key_part, preferred_element_type=jnp.float32
-    ) * HEAD_DIM ** (-0.5)
-    allowed = (key_place[None, :] <= query_place[:, None]) & (
-        key_docs[None, :] == query_docs[:, None]
-    )
-    allowed = allowed[:, None, None, :]
-    block_peak = jnp.max(jnp.where(allowed, scores, negative), axis=3)
-    new_peak = jnp.maximum(row_peak, block_peak)
-    raised = jnp.where(allowed, jnp.exp(scores - new_peak[..., None]), 0.0)
-    factor = jnp.exp(row_peak - new_peak)
-    new_total = row_total * factor + jnp.sum(raised, axis=3)
-    product = jnp.einsum(
-        "qgjk,kgd->qgjd",
-        raised.astype(jnp.bfloat16),
-        value_part,
-        preferred_element_type=jnp.float32,
-    )
-    return (new_peak, new_total, summed * factor[..., None] + product)
-
-
 def on_device(
     text, frames, tile_pos, frame_count, doc_ids, norm_gain, w_query, q_bias, w_key, w_value, v_bias
 ):
@@ -108,58 +80,104 @@
     keyval = jnp.concatenate([key_rows, value_rows], axis=1)
     kv_heads = w_key.shape[1] // HEAD_DIM
     per_group = w_query.shape[1] // HEAD_DIM // kv_heads
-    own_place = first_row + jnp.arange(shard_rows, dtype=jnp.int32)
     own_docs = lax.dynamic_slice_in_dim(doc_ids, first_row, shard_rows)
-    blocks = [(queries, own_place, own_docs)]
-    initial = tuple(
-        (
-            (
-                jnp.full((entry[0].shape[0], kv_heads, per_group), negative, jnp.float32),
-                jnp.zeros((entry[0].shape[0], kv_heads, per_group), jnp.float32),
-                jnp.zeros((entry[0].shape[0], kv_heads, per_group, HEAD_DIM), jnp.float32),
-            )
-            for entry in blocks
-        )
-    )
     incoming_keys = lax.all_gather(keyval, "seq", axis=0, tiled=True)
-    piece_rows = incoming_keys.shape[0]
-    step_rows = 512
-
-    def one_step(step_index, current):
-        key_first = step_index * step_rows
-        key_block = lax.dynamic_slice_in_dim(incoming_keys, step_index * step_rows, step_rows)
-        key_place = key_first + jnp.arange(step_rows, dtype=jnp.int32)
-        key_docs = lax.dynamic_slice_in_dim(doc_ids, key_first, step_rows)
-        updated = []
-        for entry, block_state in zip(blocks, current):
-            query_rows, query_place, query_docs = entry
-
-            def compute(
-                operand, query_rows=query_rows, query_place=query_place, query_docs=query_docs
-            ):
-                return attend_block(
-                    operand,
-                    query_rows,
-                    query_place,
-                    query_docs,
-                    key_block,
-                    key_place,
-                    key_docs,
-                    kv_heads,
-                )
-
-            def unchanged(operand):
-                return operand
-
-            updated.append(lax.cond(key_first <= query_place[-1], compute, unchanged, block_state))
-        return tuple(updated)
-
-    finals = lax.fori_loop(0, piece_rows // step_rows, one_step, initial)
-    outputs = [
-        (summed / row_total[..., None]).reshape(summed.shape[0], -1).astype(jnp.bfloat16)
-        for row_peak, row_total, summed in finals
-    ]
-    return outputs[0]
+    doc_start = jnp.sum((doc_ids < own_docs[0]).astype(jnp.int32))
+    last_row = first_row + shard_rows - 1
+    block_range = jnp.stack([doc_start // KEY_BLOCK, last_row // KEY_BLOCK, first_row]).astype(jnp.int32)
+    return flash_attention(block_range, queries, incoming_keys, own_docs, doc_ids, kv_heads)
+
+
+KEY_BLOCK = 512
+
+
+def flash_kernel(
+    range_ref, q_ref, k_ref, v_ref, qdoc_ref, kdoc_ref, out_ref, peak_ref, total_ref, acc_ref
+):
+    step = pl.program_id(0)
+    block = range_ref[0] + step
+    rows = q_ref.shape[0]
+    heads = q_ref.shape[1] // HEAD_DIM
+
+    @pl.when(step == 0)
+    def _():
+        peak_ref[...] = jnp.full(peak_ref.shape, negative, jnp.float32)
+        total_ref[...] = jnp.zeros(total_ref.shape, jnp.float32)
+        acc_ref[...] = jnp.zeros(acc_ref.shape, jnp.float32)
+
+    @pl.when(block <= range_ref[1])
+    def _():
+        key_place = block * KEY_BLOCK + lax.broadcasted_iota(jnp.int32, (1, KEY_BLOCK), 1)
+        query_place = range_ref[2] + lax.broadcasted_iota(jnp.int32, (rows, 1), 0)
+        allowed = (key_place <= query_place) & (kdoc_ref[...] == qdoc_ref[...])
+        keys = k_ref[...]
+        vals = v_ref[...]
+        for h in range(heads):
+            cols = slice(h * HEAD_DIM, (h + 1) * HEAD_DIM)
+            scores = lax.dot_general(
+                q_ref[:, cols], keys, (((1,), (1,)), ((), ())),
+                preferred_element_type=jnp.float32,
+            ) * HEAD_DIM ** (-0.5)
+            scores = jnp.where(allowed, scores, negative)
+            old_peak = peak_ref[h]
+            new_peak = jnp.maximum(old_peak, jnp.max(scores, axis=1, keepdims=True))
+            raised = jnp.where(allowed, jnp.exp(scores - new_peak[:, :1]), 0.0)
+            factor = jnp.exp(old_peak - new_peak)
+            total_ref[h] = total_ref[h] * factor + jnp.sum(raised, axis=1, keepdims=True)
+            peak_ref[h] = new_peak
+            product = jnp.dot(raised.astype(jnp.bfloat16), vals, preferred_element_type=jnp.float32)
+            acc_ref[:, cols] = acc_ref[:, cols] * factor[:, :1] + product
+
+    @pl.when(step == pl.num_programs(0) - 1)
+    def _():
+        for h in range(heads):
+            cols = slice(h * HEAD_DIM, (h + 1) * HEAD_DIM)
+            out_ref[:, cols] = (acc_ref[:, cols] / total_ref[h][:, :1]).astype(out_ref.dtype)
+
+
+def flash_attention(block_range, queries, keyval, own_docs, doc_ids, kv_heads):
+    rows, width = queries.shape
+    key_rows = keyval.shape[0]
+    steps = key_rows // KEY_BLOCK
+    heads = width // HEAD_DIM
+
+    def key_block(j, r):
+        return (jnp.minimum(r[0] + j, r[1]), 0)
+
+    def value_block(j, r):
+        return (jnp.minimum(r[0] + j, r[1]), 1)
+
+    def doc_block(j, r):
+        return (0, jnp.minimum(r[0] + j, r[1]))
+
+    grid_spec = pltpu.PrefetchScalarGridSpec(
+        num_scalar_prefetch=1,
+        grid=(steps,),
+        in_specs=[
+            pl.BlockSpec((rows, width), lambda j, r: (0, 0)),
+            pl.BlockSpec((KEY_BLOCK, HEAD_DIM), key_block),
+            pl.BlockSpec((KEY_BLOCK, HEAD_DIM), value_block),
+            pl.BlockSpec((rows, 1), lambda j, r: (0, 0)),
+            pl.BlockSpec((1, KEY_BLOCK), doc_block),
+        ],
+        out_specs=pl.BlockSpec((rows, width), lambda j, r: (0, 0)),
+        scratch_shapes=[
+            pltpu.VMEM((heads, rows, 1), jnp.float32),
+            pltpu.VMEM((heads, rows, 1), jnp.float32),
+            pltpu.VMEM((rows, width), jnp.float32),
+        ],
+    )
+    flops = 4 * rows * width * key_rows // 2
+    return pl.pallas_call(
+        flash_kernel,
+        out_shape=jax.ShapeDtypeStruct((rows, width), jnp.bfloat16),
+        grid_spec=grid_spec,
+        compiler_params=pltpu.CompilerParams(dimension_semantics=("arbitrary",)),
+        cost_estimate=pl.CostEstimate(
+            flops=flops, transcendentals=rows * heads * key_rows // 2,
+            bytes_accessed=2 * (2 * rows * width + key_rows * 2 * HEAD_DIM),
+        ),
+    )(block_range, queries, keyval, keyval, own_docs.reshape(rows, 1), doc_ids.reshape(1, -1))
 
 
 def solution(mesh):

time: 261 us -> 188 us (0.72)
  the two profiles are of different devices: /device:TPU:57 before, /device:TPU:19 now
where the time goes in v1:
time: 188 us; the launch traced here: 187 us
  waiting for transfers between devices  67 us (36%)
  local copies, waits for them, and re-layouts  33.8 us (18%)
  Pallas kernels  21.9 us (12%)
  starting transfers between devices  19.4 us (10%)
  between operations  17 us (9%)
  matrix products  15.4 us (8%)
  other arithmetic  12.9 us (7%)
    all_to_all x1, waiting for transfers between devices, on_device(): lax.all_to_all(wide_rows, ('seq', 'vis'), split_axis=0, concat_axis=0, ti...  49.7 us
    pallas_call x1, Pallas kernels, flash_attention(): pl.pallas_call(flash_kernel, out_shape=jax.ShapeDtypeStruct((rows, width)...  21.9 us
    all_gather x1, waiting for transfers between devices, on_device(): incoming_keys = lax.all_gather(keyval, 'seq', axis=0, tiled=True)  14.1 us
    dot_general x1, matrix products, on_device(): jnp.dot(normed, w_query, preferred_element_type=jnp.float32) + q_bias  12.5 us
    gather x1, local copies, waits for them, and re-layouts, place_frames(): return jnp.where(covered[:, None], incoming[source], text)  11.7 us
    all_to_all x1, starting transfers between devices, on_device(): lax.all_to_all(wide_place, ('seq', 'vis'), split_axis=0, concat_axis=0, t...  10.6 us
    all_to_all x1, starting transfers between devices, on_device(): lax.all_to_all(wide_rows, ('seq', 'vis'), split_axis=0, concat_axis=0, ti...  8.76 us
    reshape x1, local copies, waits for them, and re-layouts, on_device(): incoming = incoming.reshape(-1, incoming.shape[-1])  7.2 us
  transfers between devices with their start and end apart: 3, of which 3 were waited for; matrix products, arithmetic and copies ran while one was open for 10% of the time, Pallas kernels for 0%

profile of v1, /device:TPU:19, one launch (start us, length us, event | category | flops | bytes accessed | tf_op | source)
XLA Modules:
  0.0 187.4 jit_solution(4197653167987235396)
XLA Ops:
  7.3 0.7 fusion.11
  8.0 0.1 fusion.5
  8.2 0.7 multiply_add_fusion
  9.0 1.4 gather_fusion
  10.6 0.6 broadcast_in_dim.56
  11.2 10.6 %all-to-all-start = ((s32[128,1,2]{2,1,0:T(1,128)}), s32[128,1,2]{2,1,0:T(1,128)S(1)}, u32[]{:S(2)}, u32[]{:S(2)}) async-start(s32[128,1,2]{2,1,0:T(1,128)} %bitcast.7), calls=%async_computation | async-start | bytes 131072 | tf_op jit(solution)/shard_map/all_to_all | solution.py:65
  21.9 2.5 %gather_fusion.1 = bf16[32,8192]{1,0:T(8,128)(2,1)S(1)} fusion(bf16[32,8192]{1,0:T(8,128)(2,1)} %param.12, s32[1024]{0:T(1024)S(1)} %pad_clamp_fusion.1), kind=kCustom, calls=%fused_computation.1 | custom fusion | bytes 1048704 | tf_op jit(solution)/shard_map/gather | solution.py:29
  24.3 0.3 gather.16
  24.7 0.5 broadcast_select_fusion.1
  25.2 3.1 %all-to-all-done = s32[128,1,2]{2,1,0:T(1,128)S(1)} async-done(((s32[128,1,2]{2,1,0:T(1,128)}), s32[128,1,2]{2,1,0:T(1,128)S(1)}, u32[]{:S(2)}, u32[]{:S(2)}) %all-to-all-start) | async-done | bytes 1056 | tf_op jit(solution)/shard_map/all_to_all | solution.py:65
  28.3 6.1 %broadcast_in_dim.86 = bf16[16,8,2,8192]{3,2,1,0:T(2,128)(2,1)} broadcast(bf16[16,2,8192]{2,1,0:T(2,128)(2,1)S(1)} %broadcast_select_fusion.1), dimensions={0,2,3} | broadcast | bytes 4718592 | tf_op jit(solution)/shard_map/broadcast_in_dim | solution.py:59
  34.5 8.8 %all-to-all-start.1 = ((bf16[128,2,8192]{2,1,0:T(2,128)(2,1)}), bf16[128,2,8192]{2,1,0:T(2,128)(2,1)}, u32[]{:S(2)}, u32[]{:S(2)}) async-start(bf16[128,2,8192]{2,1,0:T(2,128)(2,1)} %bitcast.24), calls=%async_computation.1 | async-start | bytes 8388608 | tf_op jit(solution)/shard_map/all_to_all | solution.py:64
  43.3 0.2 subtract_reduce_fusion
  43.5 0.1 sub.35
  43.6 0.1 select_reduce_fusion
  43.9 49.7 %all-to-all-done.1 = bf16[128,2,8192]{2,1,0:T(2,128)(2,1)} async-done(((bf16[128,2,8192]{2,1,0:T(2,128)(2,1)}), bf16[128,2,8192]{2,1,0:T(2,128)(2,1)}, u32[]{:S(2)}, u32[]{:S(2)}) %all-to-all-start.1) | async-done | bytes 4194336 | tf_op jit(solution)/shard_map/all_to_all | solution.py:64
  93.6 7.2 %reshape.92 = bf16[256,8192]{1,0:T(8,128)(2,1)} reshape(bf16[128,2,8192]{2,1,0:T(2,128)(2,1)} %all-to-all-done.1) | data formatting | bytes 8388608 | tf_op jit(solution)/shard_map/reshape | solution.py:67
  100.8 11.7 %gather_fusion.2 = bf16[256,8192]{1,0:T(8,128)(2,1)} fusion(bf16[256,8192]{1,0:T(8,128)(2,1)} %reshape.92, s32[1024]{0:T(1024)S(1)} %pad_clamp_fusion), kind=kCustom, calls=%fused_computation.2 | custom fusion | bytes 8389632 | tf_op jit(solution)/shard_map/gather | solution.py:44
  112.5 5.1 %fusion = f32[256]{0:T(256)S(1)} fusion(bf16[256,8192]{1,0:T(8,128)(2,1)} %gather_fusion.2, bf16[256,8192]{1,0:T(8,128)(2,1)} %param.11, pred[256]{0:T(512)(128)(4,1)S(1)} %fusion.6), kind=kLoop, calls=%fused_computation.5 | loop fusion | flops 8388352 | bytes 8389888 | tf_op jit(solution)/shard_map/reduce_sum | solution.py:71
  117.6 0.8 copy-done.3
  118.4 2.8 %fusion.2 = bf16[256,8192]{1,0:T(8,128)(2,1)S(1)} fusion(f32[8192]{0:T(1024)S(1)} %copy-done.5, f32[256]{0:T(256)S(1)} %add_rsqrt_fusion, bf16[256,8192]{1,0:T(8,128)(2,1)S(1)} %copy-done.2, bf16[256,8192]{1,0:T(8,128)(2,1)S(1)} %copy-done.3, pred[256]{0:T(512)(128)(4,1)S(1)} %fusion.6), kind=kLoop, calls=%fused_computation.7 | loop fusion | flops 10485760 | bytes 12616960 | tf_op jit(solution)/shard_map/convert_element_type | solution.py:72
  121.2 1.5 convolution_convert_fusion
  122.7 1.6 copy-done.4
  124.3 1.2 fusion.4
  125.5 0.7 pad_maximum_fusion
  126.3 0.5 slice.3
  126.9 1.2 convert_reduce_fusion
  130.6 0.8 copy.22.qdoc_ref
  131.4 0.6 pad_add_fusion.range_ref
  132.0 12.5 %fusion.3.q_ref = bf16[256,1024]{1,0:T(8,128)(2,1)} fusion(bf16[256,8192]{1,0:T(8,128)(2,1)} %copy-done.1, bf16[8192,1024]{1,0:T(8,128)(2,1)} %param.17, f32[1024]{0:T(1024)S(1)} %copy-done.8), kind=kOutput, calls=%fused_computation.10 | convolution fusion | flops 4295491584 | bytes 21499904 | tf_op jit(solution)/shard_map/dot_general | solution.py:73
  144.6 14.1 %all-gather.2.cloned.1.call-done.k_ref.v_ref = bf16[4096,256]{1,0:T(8,128)(2,1)} async-done(((bf16[256,256]{1,0:T(8,128)(2,1)}), bf16[4096,256]{1,0:T(8,128)(2,1)}) %all-gather.2.cloned.1.call-update) | async-done | bytes 2097168 | tf_op jit(solution)/shard_map/all_gather | solution.py:84
  158.7 21.9 %shard_map.109 = bf16[256,1024]{1,0:T(8,128)(2,1)} custom-call(s32[3]{0:T(128)} %pad_add_fusion.range_ref, bf16[256,1024]{1,0:T(8,128)(2,1)} %fusion.3.q_ref, bf16[4096,256]{1,0:T(8,128)(2,1)} %all-gather.2.cloned.1.call-done.k_ref.v_ref, bf16[4096,256]{1,0:T(8,128)(2,1)} %all-gather.2.cloned.1.call-done.k_ref.v_ref, s32[256,1]{1,0:T(8,128)} %copy.22.qdoc_ref, ...), custom_call_target="tpu_custom_call" | custom-call | flops 2147483648 | bytes 3145728 | tf_op jit(solution)/shard_map/pallas_call | solution.py:171
  (31 shorter events, 0.7 us)
Async XLA Ops:
  6.5 114.6 %copy-start = (bf16[8192,128]{1,0:T(8,128)(2,1)S(1)}, bf16[8192,128]{1,0:T(8,128)(2,1)}, u32[]{:S(2)}) copy-start(bf16[8192,128]{1,0:T(8,128)(2,1)} %param.19) | copy-start | bytes 6291460
  11.2 17.1 %all-to-all-start = ((s32[128,1,2]{2,1,0:T(1,128)}), s32[128,1,2]{2,1,0:T(1,128)S(1)}, u32[]{:S(2)}, u32[]{:S(2)}) async-start(s32[128,1,2]{2,1,0:T(1,128)} %bitcast.7), calls=%async_computation | async-start | bytes 131072 | tf_op jit(solution)/shard_map/all_to_all | solution.py:65
  34.5 59.1 %all-to-all-start.1 = ((bf16[128,2,8192]{2,1,0:T(2,128)(2,1)}), bf16[128,2,8192]{2,1,0:T(2,128)(2,1)}, u32[]{:S(2)}, u32[]{:S(2)}) async-start(bf16[128,2,8192]{2,1,0:T(2,128)(2,1)} %bitcast.24), calls=%async_computation.1 | async-start | bytes 8388608 | tf_op jit(solution)/shard_map/all_to_all | solution.py:64
  43.2 115.5 %all-gather.2.cloned.1.call-start = ((), (), s32[]{:S(2)}) async-start(), calls=%async_computation.2 | async-start | bytes 2228224 | tf_op jit(solution)/shard_map/all_gather | solution.py:84
  100.8 16.8 %copy-start.5 = (f32[8192]{0:T(1024)S(1)}, f32[8192]{0:T(1024)}, u32[]{:S(2)}) copy-start(f32[8192]{0:T(1024)} %param.16) | copy-start | bytes 98308
  112.4 5.2 %copy-start.2 = (bf16[256,8192]{1,0:T(8,128)(2,1)S(1)}, bf16[256,8192]{1,0:T(8,128)(2,1)}, u32[]{:S(2)}) copy-start(bf16[256,8192]{1,0:T(8,128)(2,1)} %gather_fusion.2) | copy-start | bytes 12582916
  112.4 5.9 %copy-start.3 = (bf16[256,8192]{1,0:T(8,128)(2,1)S(1)}, bf16[256,8192]{1,0:T(8,128)(2,1)}, u32[]{:S(2)}) copy-start(bf16[256,8192]{1,0:T(8,128)(2,1)} %param.11) | copy-start | bytes 12582916
  121.2 4.4 %copy-start.1 = (bf16[256,8192]{1,0:T(8,128)(2,1)}, bf16[256,8192]{1,0:T(8,128)(2,1)S(1)}, u32[]{:S(2)}) copy-start(bf16[256,8192]{1,0:T(8,128)(2,1)S(1)} %fusion.2) | copy-start | bytes 12582916
  121.2 3.1 %copy-start.4 = (bf16[8192,128]{1,0:T(8,128)(2,1)S(1)}, bf16[8192,128]{1,0:T(8,128)(2,1)}, u32[]{:S(2)}) copy-start(bf16[8192,128]{1,0:T(8,128)(2,1)} %param.20) | copy-start | bytes 6291460
  121.2 3.1 %copy-start.7 = (f32[128]{0:T(128)S(1)}, f32[128]{0:T(128)}, u32[]{:S(2)}) copy-start(f32[128]{0:T(128)} %param.21) | copy-start | bytes 1540
  124.3 2.0 %copy-start.6 = (s32[4096]{0:T(1024)S(1)}, s32[4096]{0:T(1024)}, u32[]{:S(2)}) copy-start(s32[4096]{0:T(1024)} %param.15) | copy-start | bytes 49156
  124.3 7.8 %copy-start.8 = (f32[1024]{0:T(1024)S(1)}, f32[1024]{0:T(1024)}, u32[]{:S(2)}) copy-start(f32[1024]{0:T(1024)} %param.18) | copy-start | bytes 12292
Sparse Core Ops, SparseCore 0:
  126.4 32.2 all-gather.1

commit v2 on v1

--- a/solution.py
+++ b/solution.py
@@ -25,23 +25,24 @@
     slot_ids = jnp.arange(owners * capacity, dtype=jnp.int32)
     match = usable[:, None] & (slot_index[:, None] == slot_ids[None, :])
     filled = jnp.any(match, axis=0)
-    source = jnp.sum(jnp.where(match, row_ids[:, None], 0), axis=0)
-    slot_rows = jnp.where(filled[:, None], frames[source], jnp.zeros((), frames.dtype))
-    slot_place = jnp.where(filled, tile_pos[source], -1)
-    return (
-        slot_rows.reshape(owners, capacity, frames.shape[1]),
-        slot_place.reshape(owners, capacity),
-    )
+    local = tile_pos - owner * shard_rows
+    slot_local = jnp.sum(jnp.where(match, local[:, None], 0), axis=0)
+    slot_local = jnp.where(filled, slot_local, -1)
+    slot_rows = jnp.dot(
+        match.T.astype(frames.dtype), frames, preferred_element_type=jnp.float32
+    ).astype(frames.dtype)
+    place_col = jnp.broadcast_to(slot_local[:, None], (slot_local.shape[0], 128)).astype(frames.dtype)
+    payload = jnp.concatenate([slot_rows, place_col], axis=1)
+    return payload.reshape(owners, capacity, payload.shape[1])
 
 
-def place_frames(text, incoming, incoming_place, first_row):
-    local_place = incoming_place - first_row
-    lookup = local_place[None, :] == jnp.arange(text.shape[0], dtype=jnp.int32)[:, None]
+def place_frames(text, incoming, incoming_place):
+    lookup = incoming_place[None, :] == jnp.arange(text.shape[0], dtype=jnp.int32)[:, None]
     covered = jnp.any(lookup, axis=1)
-    source = jnp.sum(
-        jnp.where(lookup, jnp.arange(local_place.shape[0], dtype=jnp.int32)[None, :], 0), axis=1
-    )
-    return jnp.where(covered[:, None], incoming[source], text)
+    placed = jnp.dot(
+        lookup.astype(incoming.dtype), incoming, preferred_element_type=jnp.float32
+    ).astype(text.dtype)
+    return jnp.where(covered[:, None], placed, text)
 
 
 def on_device(
@@ -53,20 +54,13 @@
     shard_rows = text.shape[0]
     capacity = shard_rows // (seq_count * vis_count)
     first_row = shard_index * shard_rows
-    slot_rows, slot_place = frame_slots(
-        frames, tile_pos, frame_count, shard_rows, seq_count, capacity
-    )
-    wide_rows = jnp.broadcast_to(slot_rows[:, None], (seq_count, vis_count) + slot_rows.shape[1:])
-    wide_rows = wide_rows.reshape(seq_count * vis_count, capacity, slot_rows.shape[2])
-    wide_place = jnp.broadcast_to(slot_place[:, None], (seq_count, vis_count, capacity))
-    wide_place = wide_place.reshape(seq_count * vis_count, capacity)
-    incoming, incoming_place = (
-        lax.all_to_all(wide_rows, ("seq", "vis"), split_axis=0, concat_axis=0, tiled=True),
-        lax.all_to_all(wide_place, ("seq", "vis"), split_axis=0, concat_axis=0, tiled=True),
-    )
-    incoming = incoming.reshape(-1, incoming.shape[-1])
-    incoming_place = incoming_place.reshape(-1)
-    merged = place_frames(text, incoming, incoming_place, first_row)
+    payload = frame_slots(frames, tile_pos, frame_count, shard_rows, seq_count, capacity)
+    arrived = lax.all_to_all(payload, "seq", split_axis=0, concat_axis=0, tiled=True)
+    gathered = lax.all_gather(arrived, "vis", axis=0, tiled=True)
+    gathered = gathered.reshape(-1, gathered.shape[-1])
+    width = text.shape[1]
+    incoming_place = gathered[:, width].astype(jnp.int32)
+    merged = place_frames(text, gathered[:, :width], incoming_place)
     widened = merged.astype(jnp.float32)
     mean_square = jnp.mean(widened * widened, axis=1, keepdims=True)
     normed = (widened * lax.rsqrt(mean_square + epsilon) * norm_gain).astype(jnp.bfloat16)

time: 188 us -> 174 us (0.926)
  the two profiles are of different devices: /device:TPU:19 before, /device:TPU:57 now
where the time goes in v2:
time: 174 us; the launch traced here: 173 us
  waiting for transfers between devices  86.7 us (50%)
  matrix products  22.3 us (13%)
  Pallas kernels  18.4 us (11%)
  between operations  16.9 us (10%)
  blocking collectives  13.8 us (8%)
  local copies, waits for them, and re-layouts  10.6 us (6%)
  other arithmetic  4.6 us (3%)
    all_gather x1, waiting for transfers between devices, on_device(): gathered = lax.all_gather(arrived, 'vis', axis=0, tiled=True)  73.4 us
    pallas_call x1, Pallas kernels, flash_attention(): pl.pallas_call(flash_kernel, out_shape=jax.ShapeDtypeStruct((rows, width)...  18.4 us
    all_to_all x1, blocking collectives, on_device(): lax.all_to_all(payload, 'seq', split_axis=0, concat_axis=0, tiled=True)  13.8 us
    all_gather x1, waiting for transfers between devices, on_device(): incoming_keys = lax.all_gather(keyval, 'seq', axis=0, tiled=True)  13.3 us
    dot_general x1, matrix products, on_device(): jnp.dot(normed, w_query, preferred_element_type=jnp.float32) + q_bias  12.6 us
    reshape x1, local copies, waits for them, and re-layouts, on_device(): gathered = gathered.reshape(-1, gathered.shape[-1])  7.3 us
    dot_general x1, matrix products, place_frames(): jnp.dot(lookup.astype(incoming.dtype), incoming, preferred_element_type=j...  5.16 us
  transfers between devices with their start and end apart: 2, of which 2 were waited for; matrix products, arithmetic and copies ran while one was open for 9% of the time, Pallas kernels for 0%

profile of v2, /device:TPU:57, one launch (start us, length us, event | category | flops | bytes accessed | tf_op | source)
XLA Modules:
  0.0 173.3 jit_solution(14406501808136138515)
XLA Ops:
  7.3 0.7 multiply_subtract_fusion
  8.0 0.1 fusion.7
  8.2 0.1 fusion.11
  8.3 0.1 select_reduce_fusion
  8.4 1.5 convolution_convert_fusion.1
  9.8 0.1 broadcast_in_dim.27
  10.0 0.2 reshape.43
  10.2 13.8 %all_to_all.5 = bf16[16,2,8320]{2,1,0:T(2,128)(2,1)} all-to-all(bf16[16,2,8320]{2,1,0:T(2,128)(2,1)S(1)} %reshape.43), channel_id=1, replica_groups=mesh['seq'=16,'vis'=8] {'seq'}, dimensions={0} | all-to-all | bytes 1064960 | tf_op jit(solution)/shard_map/all_to_all | solution.py:58
  24.0 0.0 all-gather.3.cloned.1.call-update
  24.0 0.0 all-gather.5.cloned.1.call-start
  24.1 73.4 %all-gather.3.cloned.1.call-done = bf16[128,2,8320]{2,1,0:T(2,128)(2,1)} async-done(((bf16[16,2,8320]{2,1,0:T(2,128)(2,1)}), bf16[128,2,8320]{2,1,0:T(2,128)(2,1)}) %all-gather.3.cloned.1.call-update) | async-done | bytes 4259856 | tf_op jit(solution)/shard_map/all_gather | solution.py:59
  97.5 7.3 %reshape.44 = bf16[256,8320]{1,0:T(8,128)(2,1)} reshape(bf16[128,2,8320]{2,1,0:T(2,128)(2,1)} %all-gather.3.cloned.1.call-done) | data formatting | bytes 8519680 | tf_op jit(solution)/shard_map/reshape | solution.py:60
  104.8 1.0 convert_reduce_fusion
  105.7 0.1 fusion.8
  105.8 5.2 %fusion.1 = (f32[256]{0:T(256)S(1)}, bf16[256,8192]{1,0:T(8,128)(2,1)S(1)}) fusion(bf16[256,8192]{1,0:T(8,128)(2,1)} %param.11, bf16[256,8320]{1,0:T(8,128)(2,1)} %reshape.44, s32[256]{0:T(256)S(1)} %convert_reduce_fusion, pred[256]{0:T(512)(128)(4,1)S(1)} %fusion.8), kind=kOutput, calls=%fused_computation.5 | convolution fusion | flops 1084292864 | bytes 12585216 | tf_op jit(solution)/shard_map/dot_general | solution.py:42
  111.0 0.0 copy-start.2
  111.0 0.0 copy-start.5
  111.1 1.4 convolution_convert_fusion.2
  112.5 0.6 copy-done.6
  113.1 1.0 copy-done.2
  114.1 1.5 fusion.6
  115.6 0.7 pad_maximum_fusion.1
  116.3 0.0 all-gather.5.cloned.1.call-update
  116.3 0.1 dynamic_slice.3
  116.4 0.5 slice.9
  116.9 1.3 convert_reduce_fusion.1
  120.8 0.8 copy.26.qdoc_ref
  121.6 0.6 pad_add_fusion.range_ref
  122.2 0.0 copy-done.4
  122.2 12.6 %fusion.5.q_ref = bf16[256,1024]{1,0:T(8,128)(2,1)} fusion(bf16[8192,1024]{1,0:T(8,128)(2,1)} %param.17, f32[1024]{0:T(1024)S(1)} %copy-done.4, bf16[256,8192]{1,0:T(8,128)(2,1)} %copy-done.6, f32[8192]{0:T(1024)S(1)} %copy-done.3, f32[256]{0:T(256)S(1)} %add_rsqrt_fusion), kind=kOutput, calls=%fused_computation.10 | convolution fusion | flops 4303880192 | bytes 21533696 | tf_op jit(solution)/shard_map/dot_general | solution.py:67
  134.8 13.3 %all-gather.5.cloned.1.call-done.k_ref.v_ref = bf16[4096,256]{1,0:T(8,128)(2,1)} async-done(((bf16[256,256]{1,0:T(8,128)(2,1)}), bf16[4096,256]{1,0:T(8,128)(2,1)}) %all-gather.5.cloned.1.call-update) | async-done | bytes 2097168 | tf_op jit(solution)/shard_map/all_gather | solution.py:78
  148.1 18.4 %shard_map.109 = bf16[256,1024]{1,0:T(8,128)(2,1)} custom-call(s32[3]{0:T(128)} %pad_add_fusion.range_ref, bf16[256,1024]{1,0:T(8,128)(2,1)} %fusion.5.q_ref, bf16[4096,256]{1,0:T(8,128)(2,1)} %all-gather.5.cloned.1.call-done.k_ref.v_ref, bf16[4096,256]{1,0:T(8,128)(2,1)} %all-gather.5.cloned.1.call-done.k_ref.v_ref, s32[256,1]{1,0:T(8,128)} %copy.26.qdoc_ref, ...), custom_call_target="tpu_custom_call" | custom-call | flops 2147483648 | bytes 3145728 | tf_op jit(solution)/shard_map/pallas_call | solution.py:165
  (15 shorter events, 0.1 us)
Async XLA Ops:
  6.5 104.5 %copy-start = (bf16[8192,128]{1,0:T(8,128)(2,1)S(1)}, bf16[8192,128]{1,0:T(8,128)(2,1)}, u32[]{:S(2)}) copy-start(bf16[8192,128]{1,0:T(8,128)(2,1)} %param.19) | copy-start | bytes 6291460
  6.5 90.9 %all-gather.3.cloned.1.call-start = ((), (), s32[]{:S(2)}) async-start(), calls=%async_computation.1 | async-start | bytes 4792320 | tf_op jit(solution)/shard_map/all_gather | solution.py:59
  24.0 124.1 %all-gather.5.cloned.1.call-start = ((), (), s32[]{:S(2)}) async-start(), calls=%async_computation.2 | async-start | bytes 2228224 | tf_op jit(solution)/shard_map/all_gather | solution.py:78
  105.8 5.2 %copy-start.3 = (f32[8192]{0:T(1024)S(1)}, f32[8192]{0:T(1024)}, u32[]{:S(2)}) copy-start(f32[8192]{0:T(1024)} %param.16) | copy-start | bytes 98308
  111.0 2.1 %copy-start.6 = (bf16[256,8192]{1,0:T(8,128)(2,1)}, bf16[256,8192]{1,0:T(8,128)(2,1)S(1)}, u32[]{:S(2)}) copy-start(bf16[256,8192]{1,0:T(8,128)(2,1)S(1)} %get-tuple-element.8) | copy-start | bytes 12582916
  111.0 3.1 %copy-start.2 = (bf16[8192,128]{1,0:T(8,128)(2,1)S(1)}, bf16[8192,128]{1,0:T(8,128)(2,1)}, u32[]{:S(2)}) copy-start(bf16[8192,128]{1,0:T(8,128)(2,1)} %param.20) | copy-start | bytes 6291460
  111.0 3.1 %copy-start.5 = (f32[128]{0:T(128)S(1)}, f32[128]{0:T(128)}, u32[]{:S(2)}) copy-start(f32[128]{0:T(128)} %param.21) | copy-start | bytes 1540
  114.1 2.2 %copy-start.1 = (s32[4096]{0:T(1024)S(1)}, s32[4096]{0:T(1024)}, u32[]{:S(2)}) copy-start(s32[4096]{0:T(1024)} %param.15) | copy-start | bytes 49156
  114.1 8.1 %copy-start.4 = (f32[1024]{0:T(1024)S(1)}, f32[1024]{0:T(1024)}, u32[]{:S(2)}) copy-start(f32[1024]{0:T(1024)} %param.18) | copy-start | bytes 12292
Sparse Core Ops, SparseCore 0:
  24.1 73.2 all-gather.2
  116.4 31.5 all-gather.4

commit v3 on v2

--- a/solution.py
+++ b/solution.py
@@ -45,6 +45,101 @@
     return jnp.where(covered[:, None], placed, text)
 
 
+def exchange_kernel(payload_ref, out_ref, send_a, recv_a, send_b, recv_b, local_sem):
+    seq_count = lax.axis_size("seq")
+    vis_count = lax.axis_size("vis")
+    me_seq = lax.axis_index("seq")
+    me_vis = lax.axis_index("vis")
+    barrier = pltpu.get_barrier_semaphore()
+    for k in range(1, seq_count):
+        pl.semaphore_signal(
+            barrier, inc=1, device_id=(lax.rem(me_seq + k, seq_count), me_vis),
+            device_id_type=pl.DeviceIdType.MESH,
+        )
+    for k in range(1, vis_count):
+        pl.semaphore_signal(
+            barrier, inc=1, device_id=(me_seq, lax.rem(me_vis + k, vis_count)),
+            device_id_type=pl.DeviceIdType.MESH,
+        )
+    pl.semaphore_wait(barrier, seq_count + vis_count - 2)
+    base = me_vis * seq_count
+    local = pltpu.make_async_copy(payload_ref.at[me_seq], out_ref.at[base + me_seq], local_sem.at[0])
+    local.start()
+    first = []
+    for k in range(1, seq_count):
+        target = lax.rem(me_seq + k, seq_count)
+        copy = pltpu.make_async_remote_copy(
+            src_ref=payload_ref.at[target],
+            dst_ref=out_ref.at[base + me_seq],
+            send_sem=send_a.at[k],
+            recv_sem=recv_a.at[k],
+            device_id=(target, me_vis),
+            device_id_type=pl.DeviceIdType.MESH,
+        )
+        copy.start()
+        first.append(copy)
+    local.wait()
+    for k in range(1, seq_count):
+        source = lax.rem(me_seq + seq_count - k, seq_count)
+        incoming = pltpu.make_async_remote_copy(
+            src_ref=payload_ref.at[source],
+            dst_ref=out_ref.at[base + source],
+            send_sem=send_a.at[k],
+            recv_sem=recv_a.at[k],
+            device_id=(source, me_vis),
+            device_id_type=pl.DeviceIdType.MESH,
+        )
+        incoming.wait_recv()
+    for copy in first:
+        copy.wait_send()
+    block = out_ref.at[pl.ds(base, seq_count)]
+    second = []
+    for k in range(1, vis_count):
+        target = lax.rem(me_vis + k, vis_count)
+        copy = pltpu.make_async_remote_copy(
+            src_ref=block,
+            dst_ref=block,
+            send_sem=send_b.at[k],
+            recv_sem=recv_b.at[k],
+            device_id=(me_seq, target),
+            device_id_type=pl.DeviceIdType.MESH,
+        )
+        copy.start()
+        second.append(copy)
+    for k in range(1, vis_count):
+        source = lax.rem(me_vis + vis_count - k, vis_count)
+        landing = out_ref.at[pl.ds(source * seq_count, seq_count)]
+        incoming = pltpu.make_async_remote_copy(
+            src_ref=landing,
+            dst_ref=landing,
+            send_sem=send_b.at[k],
+            recv_sem=recv_b.at[k],
+            device_id=(me_seq, source),
+            device_id_type=pl.DeviceIdType.MESH,
+        )
+        incoming.wait_recv()
+    for copy in second:
+        copy.wait_send()
+
+
+def exchange_frames(payload, vis_count):
+    owners, capacity, width = payload.shape
+    return pl.pallas_call(
+        exchange_kernel,
+        out_shape=jax.ShapeDtypeStruct((vis_count * owners, capacity, width), payload.dtype),
+        in_specs=[pl.BlockSpec(memory_space=pl.ANY)],
+        out_specs=pl.BlockSpec(memory_space=pl.ANY),
+        scratch_shapes=[
+            pltpu.SemaphoreType.DMA((owners,)),
+            pltpu.SemaphoreType.DMA((owners,)),
+            pltpu.SemaphoreType.DMA((vis_count,)),
+            pltpu.SemaphoreType.DMA((vis_count,)),
+            pltpu.SemaphoreType.DMA((1,)),
+        ],
+        compiler_params=pltpu.CompilerParams(collective_id=1, has_side_effects=True),
+    )(payload)
+
+
 def on_device(
     text, frames, tile_pos, frame_count, doc_ids, norm_gain, w_query, q_bias, w_key, w_value, v_bias
 ):
@@ -55,8 +150,7 @@
     capacity = shard_rows // (seq_count * vis_count)
     first_row = shard_index * shard_rows
     payload = frame_slots(frames, tile_pos, frame_count, shard_rows, seq_count, capacity)
-    arrived = lax.all_to_all(payload, "seq", split_axis=0, concat_axis=0, tiled=True)
-    gathered = lax.all_gather(arrived, "vis", axis=0, tiled=True)
+    gathered = exchange_frames(payload, vis_count)
     gathered = gathered.reshape(-1, gathered.shape[-1])
     width = text.shape[1]
     incoming_place = gathered[:, width].astype(jnp.int32)

time: 174 us -> 172 us (0.989)
  the two profiles are of different devices: /device:TPU:57 before, /device:TPU:43 now
where the time goes in v3:
time: 172 us
  Pallas kernels  95.8 us (56%)
  matrix products  22.1 us (13%)
  waiting for transfers between devices  20.9 us (12%)
  between operations  16.9 us (10%)
  local copies, waits for them, and re-layouts  11.5 us (7%)
  other arithmetic  4.51 us (3%)
    pallas_call x1, Pallas kernels, exchange_frames(): pl.pallas_call(exchange_kernel, out_shape=jax.ShapeDtypeStruct((vis_count...  77.3 us
    all_gather x1, waiting for transfers between devices, on_device(): incoming_keys = lax.all_gather(keyval, 'seq', axis=0, tiled=True)  20.8 us
    pallas_call x1, Pallas kernels, flash_attention(): pl.pallas_call(flash_kernel, out_shape=jax.ShapeDtypeStruct((rows, width)...  18.5 us
    dot_general x1, matrix products, on_device(): jnp.dot(normed, w_query, preferred_element_type=jnp.float32) + q_bias  12.4 us
    reshape x1, local copies, waits for them, and re-layouts, on_device(): gathered = gathered.reshape(-1, gathered.shape[-1])  7.3 us
    dot_general x1, matrix products, place_frames(): jnp.dot(lookup.astype(incoming.dtype), incoming, preferred_element_type=j...  5.16 us
  transfers between devices with their start and end apart: 1, of which 1 were waited for; matrix products, arithmetic and copies ran while one was open for 9% of the time, Pallas kernels for 0%

profile of v3, /device:TPU:43, one launch (start us, length us, event | category | flops | bytes accessed | tf_op | source)
XLA Modules:
  0.0 171.6 jit_solution(7973237047569678814)
XLA Ops:
  6.5 0.0 copy-start
  6.5 0.0 all-gather.2.cloned.1.call-start
  7.3 0.7 multiply_subtract_fusion
  8.0 0.1 fusion.7
  8.2 0.1 fusion.11
  8.3 0.1 select_reduce_fusion
  8.4 1.4 convolution_convert_fusion.1
  9.8 0.1 broadcast_in_dim.27
  10.0 1.0 reshape.43.payload_ref
  11.0 77.3 %shard_map.109 = bf16[128,2,8320]{2,1,0:T(2,128)(2,1)} custom-call(bf16[16,2,8320]{2,1,0:T(2,128)(2,1)} %reshape.43.payload_ref), custom_call_target="tpu_custom_call" | custom-call | tf_op jit(solution)/shard_map/pallas_call | solution.py:127
  88.3 7.3 %reshape.44 = bf16[256,8320]{1,0:T(8,128)(2,1)} reshape(bf16[128,2,8320]{2,1,0:T(2,128)(2,1)} %shard_map.109) | data formatting | bytes 8519680 | tf_op jit(solution)/shard_map/reshape | solution.py:154
  95.6 0.9 slice_convert_fusion
  96.4 0.1 copy.25
  96.5 0.1 fusion.8
  96.7 5.2 %fusion.1 = (f32[256]{0:T(256)S(1)}, bf16[256,8192]{1,0:T(8,128)(2,1)S(1)}) fusion(bf16[256,8192]{1,0:T(8,128)(2,1)} %param.11, bf16[256,8320]{1,0:T(8,128)(2,1)} %reshape.44, s32[256]{0:T(256)S(1)} %bitcast.17, pred[256]{0:T(512)(128)(4,1)S(1)} %fusion.8), kind=kOutput, calls=%fused_computation.5 | convolution fusion | flops 1084292864 | bytes 12585216 | tf_op jit(solution)/shard_map/dot_general | solution.py:42
  101.9 0.0 copy-start.2
  101.9 0.0 copy-start.5
  101.9 1.4 convolution_convert_fusion.2
  103.3 0.6 copy-done.6
  104.0 1.0 copy-done.2
  105.0 1.5 fusion.6
  106.4 0.7 pad_maximum_fusion.1
  107.1 0.0 all-gather.2.cloned.1.call-update
  107.2 0.1 dynamic_slice.3
  107.2 0.5 slice.9
  107.8 1.3 convert_reduce_fusion
  111.7 0.8 copy.21.qdoc_ref
  112.4 0.6 pad_add_fusion.range_ref
  113.0 0.0 copy-done.4
  113.0 12.4 %fusion.5.q_ref = bf16[256,1024]{1,0:T(8,128)(2,1)} fusion(bf16[8192,1024]{1,0:T(8,128)(2,1)} %param.17, f32[1024]{0:T(1024)S(1)} %copy-done.4, bf16[256,8192]{1,0:T(8,128)(2,1)} %copy-done.6, f32[8192]{0:T(1024)S(1)} %copy-done.3, f32[256]{0:T(256)S(1)} %add_rsqrt_fusion), kind=kOutput, calls=%fused_computation.10 | convolution fusion | flops 4303880192 | bytes 21533696 | tf_op jit(solution)/shard_map/dot_general | solution.py:161
  125.5 20.8 %all-gather.2.cloned.1.call-done.k_ref.v_ref = bf16[4096,256]{1,0:T(8,128)(2,1)} async-done(((bf16[256,256]{1,0:T(8,128)(2,1)}), bf16[4096,256]{1,0:T(8,128)(2,1)}) %all-gather.2.cloned.1.call-update) | async-done | bytes 2097168 | tf_op jit(solution)/shard_map/all_gather | solution.py:172
  146.3 18.5 %shard_map.110 = bf16[256,1024]{1,0:T(8,128)(2,1)} custom-call(s32[3]{0:T(128)} %pad_add_fusion.range_ref, bf16[256,1024]{1,0:T(8,128)(2,1)} %fusion.5.q_ref, bf16[4096,256]{1,0:T(8,128)(2,1)} %all-gather.2.cloned.1.call-done.k_ref.v_ref, bf16[4096,256]{1,0:T(8,128)(2,1)} %all-gather.2.cloned.1.call-done.k_ref.v_ref, s32[256,1]{1,0:T(8,128)} %copy.21.qdoc_ref, ...), custom_call_target="tpu_custom_call" | custom-call | flops 2147483648 | bytes 3145728 | tf_op jit(solution)/shard_map/pallas_call | solution.py:259
  (13 shorter events, 0.1 us)
Async XLA Ops:
  6.5 95.3 %copy-start = (bf16[8192,128]{1,0:T(8,128)(2,1)S(1)}, bf16[8192,128]{1,0:T(8,128)(2,1)}, u32[]{:S(2)}) copy-start(bf16[8192,128]{1,0:T(8,128)(2,1)} %param.19) | copy-start | bytes 6291460
  6.5 139.8 %all-gather.2.cloned.1.call-start = ((), (), s32[]{:S(2)}) async-start(), calls=%async_computation | async-start | bytes 2228224 | tf_op jit(solution)/shard_map/all_gather | solution.py:172
  96.7 5.2 %copy-start.3 = (f32[8192]{0:T(1024)S(1)}, f32[8192]{0:T(1024)}, u32[]{:S(2)}) copy-start(f32[8192]{0:T(1024)} %param.16) | copy-start | bytes 98308
  101.8 2.1 %copy-start.6 = (bf16[256,8192]{1,0:T(8,128)(2,1)}, bf16[256,8192]{1,0:T(8,128)(2,1)S(1)}, u32[]{:S(2)}) copy-start(bf16[256,8192]{1,0:T(8,128)(2,1)S(1)} %get-tuple-element.8) | copy-start | bytes 12582916
  101.9 3.1 %copy-start.2 = (bf16[8192,128]{1,0:T(8,128)(2,1)S(1)}, bf16[8192,128]{1,0:T(8,128)(2,1)}, u32[]{:S(2)}) copy-start(bf16[8192,128]{1,0:T(8,128)(2,1)} %param.20) | copy-start | bytes 6291460
  101.9 3.1 %copy-start.5 = (f32[128]{0:T(128)S(1)}, f32[128]{0:T(128)}, u32[]{:S(2)}) copy-start(f32[128]{0:T(128)} %param.21) | copy-start | bytes 1540
  105.0 2.2 %copy-start.1 = (s32[4096]{0:T(1024)S(1)}, s32[4096]{0:T(1024)}, u32[]{:S(2)}) copy-start(s32[4096]{0:T(1024)} %param.15) | copy-start | bytes 49156
  105.0 8.1 %copy-start.4 = (f32[1024]{0:T(1024)S(1)}, f32[1024]{0:T(1024)}, u32[]{:S(2)}) copy-start(f32[1024]{0:T(1024)} %param.18) | copy-start | bytes 12292
Sparse Core Ops, SparseCore 0:
  107.3 38.9 all-gather.1

commit v4 on v3

--- a/solution.py
+++ b/solution.py
@@ -48,20 +48,29 @@
 def exchange_kernel(payload_ref, out_ref, send_a, recv_a, send_b, recv_b, local_sem):
     seq_count = lax.axis_size("seq")
     vis_count = lax.axis_size("vis")
+    ring = vis_count // 2
     me_seq = lax.axis_index("seq")
     me_vis = lax.axis_index("vis")
+    ring_pos = lax.rem(me_vis, ring)
+    ring_id = me_vis // ring
+
+    def vis_of(ring_index, position):
+        return ring_index * ring + lax.rem(position + ring, ring)
+
+    right = vis_of(ring_id, ring_pos + 1)
+    left = vis_of(ring_id, ring_pos - 1)
+    partner = vis_of(1 - ring_id, ring_pos)
     barrier = pltpu.get_barrier_semaphore()
     for k in range(1, seq_count):
         pl.semaphore_signal(
             barrier, inc=1, device_id=(lax.rem(me_seq + k, seq_count), me_vis),
             device_id_type=pl.DeviceIdType.MESH,
         )
-    for k in range(1, vis_count):
+    for peer in (left, right, partner):
         pl.semaphore_signal(
-            barrier, inc=1, device_id=(me_seq, lax.rem(me_vis + k, vis_count)),
-            device_id_type=pl.DeviceIdType.MESH,
-        )
-    pl.semaphore_wait(barrier, seq_count + vis_count - 2)
+            barrier, inc=1, device_id=(me_seq, peer), device_id_type=pl.DeviceIdType.MESH
+        )
+    pl.semaphore_wait(barrier, seq_count + 2)
     base = me_vis * seq_count
     local = pltpu.make_async_copy(payload_ref.at[me_seq], out_ref.at[base + me_seq], local_sem.at[0])
     local.start()
@@ -92,33 +101,56 @@
         incoming.wait_recv()
     for copy in first:
         copy.wait_send()
-    block = out_ref.at[pl.ds(base, seq_count)]
-    second = []
-    for k in range(1, vis_count):
-        target = lax.rem(me_vis + k, vis_count)
-        copy = pltpu.make_async_remote_copy(
-            src_ref=block,
-            dst_ref=block,
-            send_sem=send_b.at[k],
-            recv_sem=recv_b.at[k],
-            device_id=(me_seq, target),
+
+    half = seq_count // 2
+
+    def region(owner, part):
+        if part == 0:
+            return out_ref.at[pl.ds(owner * seq_count, seq_count)]
+        start = owner * seq_count + (part - 1) * half
+        return out_ref.at[pl.ds(start, half)]
+
+    def link(owner, part, peer, index):
+        piece = region(owner, part)
+        return pltpu.make_async_remote_copy(
+            src_ref=piece,
+            dst_ref=piece,
+            send_sem=send_b.at[index],
+            recv_sem=recv_b.at[index],
+            device_id=(me_seq, peer),
             device_id_type=pl.DeviceIdType.MESH,
         )
+
+    far = vis_of(ring_id, ring_pos + 2)
+    left_partner = vis_of(1 - ring_id, ring_pos - 1)
+    right_partner = vis_of(1 - ring_id, ring_pos + 1)
+    far_partner = vis_of(1 - ring_id, ring_pos + 2)
+    sent = []
+
+    def send(owner, part, peer, index):
+        copy = link(owner, part, peer, index)
         copy.start()
-        second.append(copy)
-    for k in range(1, vis_count):
-        source = lax.rem(me_vis + vis_count - k, vis_count)
-        landing = out_ref.at[pl.ds(source * seq_count, seq_count)]
-        incoming = pltpu.make_async_remote_copy(
-            src_ref=landing,
-            dst_ref=landing,
-            send_sem=send_b.at[k],
-            recv_sem=recv_b.at[k],
-            device_id=(me_seq, source),
-            device_id_type=pl.DeviceIdType.MESH,
-        )
-        incoming.wait_recv()
-    for copy in second:
+        sent.append(copy)
+
+    send(me_vis, 0, right, 1)
+    send(me_vis, 0, left, 2)
+    send(me_vis, 0, partner, 3)
+    link(partner, 0, partner, 3).wait_recv()
+    send(partner, 0, right, 4)
+    send(partner, 0, left, 5)
+    link(left, 0, left, 1).wait_recv()
+    send(left, 1, right, 6)
+    link(right, 0, right, 2).wait_recv()
+    send(right, 2, left, 7)
+    link(left_partner, 0, left, 4).wait_recv()
+    send(left_partner, 1, right, 8)
+    link(right_partner, 0, right, 5).wait_recv()
+    send(right_partner, 2, left, 9)
+    link(far, 1, left, 6).wait_recv()
+    link(far, 2, right, 7).wait_recv()
+    link(far_partner, 1, left, 8).wait_recv()
+    link(far_partner, 2, right, 9).wait_recv()
+    for copy in sent:
         copy.wait_send()
 
 
@@ -132,8 +164,8 @@
         scratch_shapes=[
             pltpu.SemaphoreType.DMA((owners,)),
             pltpu.SemaphoreType.DMA((owners,)),
-            pltpu.SemaphoreType.DMA((vis_count,)),
-            pltpu.SemaphoreType.DMA((vis_count,)),
+            pltpu.SemaphoreType.DMA((10,)),
+            pltpu.SemaphoreType.DMA((10,)),
             pltpu.SemaphoreType.DMA((1,)),
         ],
         compiler_params=pltpu.CompilerParams(collective_id=1, has_side_effects=True),

time: 172 us -> 142 us (0.83)
  the two profiles are of different devices: /device:TPU:43 before, /device:TPU:57 now
where the time goes in v4:
time: 142 us; the launch traced here: 140 us
  Pallas kernels  71.8 us (51%)
  matrix products  22.3 us (16%)
  between operations  16.9 us (12%)
  waiting for transfers between devices  13.3 us (9%)
  local copies, waits for them, and re-layouts  11.5 us (8%)
  other arithmetic  4.51 us (3%)
    pallas_call x1, Pallas kernels, exchange_frames(): pl.pallas_call(exchange_kernel, out_shape=jax.ShapeDtypeStruct((vis_count...  53.3 us
    pallas_call x1, Pallas kernels, flash_attention(): pl.pallas_call(flash_kernel, out_shape=jax.ShapeDtypeStruct((rows, width)...  18.4 us
    all_gather x1, waiting for transfers between devices, on_device(): incoming_keys = lax.all_gather(keyval, 'seq', axis=0, tiled=True)  13.3 us
    dot_general x1, matrix products, on_device(): jnp.dot(normed, w_query, preferred_element_type=jnp.float32) + q_bias  12.6 us
    reshape x1, local copies, waits for them, and re-layouts, on_device(): gathered = gathered.reshape(-1, gathered.shape[-1])  7.3 us
    dot_general x1, matrix products, place_frames(): jnp.dot(lookup.astype(incoming.dtype), incoming, preferred_element_type=j...  5.16 us
  transfers between devices with their start and end apart: 1, of which 1 were waited for; matrix products, arithmetic and copies ran while one was open for 11% of the time, Pallas kernels for 0%

profile of v4, /device:TPU:57, one launch (start us, length us, event | category | flops | bytes accessed | tf_op | source)
XLA Modules:
  0.0 140.3 jit_solution(908107946746760540)
XLA Ops:
  6.5 0.0 copy-start
  6.5 0.0 all-gather.2.cloned.1.call-start
  7.3 0.7 multiply_subtract_fusion
  8.0 0.1 fusion.7
  8.2 0.1 fusion.11
  8.3 0.1 select_reduce_fusion
  8.4 1.5 %convolution_convert_fusion.1 = bf16[32,8192]{1,0:T(8,128)(2,1)S(1)} fusion(bf16[32,8192]{1,0:T(8,128)(2,1)} %param.12, s32[32]{0:T(128)S(1)} %multiply_add_fusion, pred[32]{0:T(512)(128)(4,1)S(1)} %iota_compare_fusion.7), kind=kOutput, calls=%fused_computation.4 | convolution fusion | flops 17041408 | bytes 1048736 | tf_op jit(solution)/shard_map/dot_general | solution.py:31
  9.8 0.1 broadcast_in_dim.27
  10.0 1.0 reshape.43.payload_ref
  11.0 53.3 %shard_map.109 = bf16[128,2,8320]{2,1,0:T(2,128)(2,1)} custom-call(bf16[16,2,8320]{2,1,0:T(2,128)(2,1)} %reshape.43.payload_ref), custom_call_target="tpu_custom_call" | custom-call | tf_op jit(solution)/shard_map/pallas_call | solution.py:159
  64.3 7.3 %reshape.44 = bf16[256,8320]{1,0:T(8,128)(2,1)} reshape(bf16[128,2,8320]{2,1,0:T(2,128)(2,1)} %shard_map.109) | data formatting | bytes 8519680 | tf_op jit(solution)/shard_map/reshape | solution.py:186
  71.6 0.9 slice_convert_fusion
  72.5 0.1 copy.25
  72.6 0.1 fusion.8
  72.7 5.2 %fusion.1 = (f32[256]{0:T(256)S(1)}, bf16[256,8192]{1,0:T(8,128)(2,1)S(1)}) fusion(bf16[256,8192]{1,0:T(8,128)(2,1)} %param.11, bf16[256,8320]{1,0:T(8,128)(2,1)} %reshape.44, s32[256]{0:T(256)S(1)} %bitcast.17, pred[256]{0:T(512)(128)(4,1)S(1)} %fusion.8), kind=kOutput, calls=%fused_computation.5 | convolution fusion | flops 1084292864 | bytes 12585216 | tf_op jit(solution)/shard_map/dot_general | solution.py:42
  77.9 0.0 copy-start.2
  77.9 0.0 copy-start.5
  77.9 1.4 %convolution_convert_fusion.2 = bf16[256,128]{1,0:T(8,128)(2,1)S(1)} fusion(bf16[8192,128]{1,0:T(8,128)(2,1)S(1)} %copy-done, bf16[256,8192]{1,0:T(8,128)(2,1)S(1)} %get-tuple-element.8, f32[8192]{0:T(1024)S(1)} %copy-done.3, f32[256]{0:T(256)S(1)} %add_rsqrt_fusion), kind=kOutput, calls=%fused_computation.13 | convolution fusion | flops 545292288 | bytes 6390784 | tf_op jit(solution)/shard_map/dot_general | solution.py:196
  79.3 0.6 copy-done.6
  80.0 1.0 copy-done.2
  81.0 1.5 %fusion.6 = bf16[256,128]{1,0:T(8,128)(2,1)S(1)} fusion(bf16[8192,128]{1,0:T(8,128)(2,1)S(1)} %copy-done.2, f32[128]{0:T(128)S(1)} %copy-done.5, bf16[256,8192]{1,0:T(8,128)(2,1)S(1)} %get-tuple-element.8, f32[8192]{0:T(1024)S(1)} %copy-done.3, f32[256]{0:T(256)S(1)} %add_rsqrt_fusion), kind=kOutput, calls=%fused_computation.12 | convolution fusion | flops 545325056 | bytes 6391296 | tf_op jit(solution)/shard_map/dot_general | solution.py:197
  82.5 0.7 pad_maximum_fusion.1
  83.2 0.0 all-gather.2.cloned.1.call-update
  83.2 0.0 copy-done.1
  83.2 0.1 dynamic_slice.3
  83.3 0.5 slice.9
  83.8 1.3 convert_reduce_fusion
  87.7 0.8 copy.21.qdoc_ref
  88.5 0.6 pad_add_fusion.range_ref
  89.1 12.6 %fusion.5.q_ref = bf16[256,1024]{1,0:T(8,128)(2,1)} fusion(bf16[8192,1024]{1,0:T(8,128)(2,1)} %param.17, f32[1024]{0:T(1024)S(1)} %copy-done.4, bf16[256,8192]{1,0:T(8,128)(2,1)} %copy-done.6, f32[8192]{0:T(1024)S(1)} %copy-done.3, f32[256]{0:T(256)S(1)} %add_rsqrt_fusion), kind=kOutput, calls=%fused_computation.10 | convolution fusion | flops 4303880192 | bytes 21533696 | tf_op jit(solution)/shard_map/dot_general | solution.py:193
  101.7 13.3 %all-gather.2.cloned.1.call-done.k_ref.v_ref = bf16[4096,256]{1,0:T(8,128)(2,1)} async-done(((bf16[256,256]{1,0:T(8,128)(2,1)}), bf16[4096,256]{1,0:T(8,128)(2,1)}) %all-gather.2.cloned.1.call-update) | async-done | bytes 2097168 | tf_op jit(solution)/shard_map/all_gather | solution.py:204
  115.0 18.4 %shard_map.110 = bf16[256,1024]{1,0:T(8,128)(2,1)} custom-call(s32[3]{0:T(128)} %pad_add_fusion.range_ref, bf16[256,1024]{1,0:T(8,128)(2,1)} %fusion.5.q_ref, bf16[4096,256]{1,0:T(8,128)(2,1)} %all-gather.2.cloned.1.call-done.k_ref.v_ref, bf16[4096,256]{1,0:T(8,128)(2,1)} %all-gather.2.cloned.1.call-done.k_ref.v_ref, s32[256,1]{1,0:T(8,128)} %copy.21.qdoc_ref, ...), custom_call_target="tpu_custom_call" | custom-call | flops 2147483648 | bytes 3145728 | tf_op jit(solution)/shard_map/pallas_call | solution.py:291
  (13 shorter events, 0.1 us)
Async XLA Ops:
  6.5 71.3 %copy-start = (bf16[8192,128]{1,0:T(8,128)(2,1)S(1)}, bf16[8192,128]{1,0:T(8,128)(2,1)}, u32[]{:S(2)}) copy-start(bf16[8192,128]{1,0:T(8,128)(2,1)} %param.19) | copy-start | bytes 6291460
  6.5 108.5 %all-gather.2.cloned.1.call-start = ((), (), s32[]{:S(2)}) async-start(), calls=%async_computation | async-start | bytes 2228224 | tf_op jit(solution)/shard_map/all_gather | solution.py:204
  72.7 5.2 %copy-start.3 = (f32[8192]{0:T(1024)S(1)}, f32[8192]{0:T(1024)}, u32[]{:S(2)}) copy-start(f32[8192]{0:T(1024)} %param.16) | copy-start | bytes 98308
  77.9 2.1 %copy-start.6 = (bf16[256,8192]{1,0:T(8,128)(2,1)}, bf16[256,8192]{1,0:T(8,128)(2,1)S(1)}, u32[]{:S(2)}) copy-start(bf16[256,8192]{1,0:T(8,128)(2,1)S(1)} %get-tuple-element.8) | copy-start | bytes 12582916
  77.9 3.1 %copy-start.2 = (bf16[8192,128]{1,0:T(8,128)(2,1)S(1)}, bf16[8192,128]{1,0:T(8,128)(2,1)}, u32[]{:S(2)}) copy-start(bf16[8192,128]{1,0:T(8,128)(2,1)} %param.20) | copy-start | bytes 6291460
  77.9 3.1 %copy-start.5 = (f32[128]{0:T(128)S(1)}, f32[128]{0:T(128)}, u32[]{:S(2)}) copy-start(f32[128]{0:T(128)} %param.21) | copy-start | bytes 1540
  81.0 2.2 %copy-start.1 = (s32[4096]{0:T(1024)S(1)}, s32[4096]{0:T(1024)}, u32[]{:S(2)}) copy-start(s32[4096]{0:T(1024)} %param.15) | copy-start | bytes 49156
  81.0 8.1 %copy-start.4 = (f32[1024]{0:T(1024)S(1)}, f32[1024]{0:T(1024)}, u32[]{:S(2)}) copy-start(f32[1024]{0:T(1024)} %param.18) | copy-start | bytes 12292
Sparse Core Ops, SparseCore 0:
  83.3 31.6 all-gather.1

commit v5 on v4

--- a/solution.py
+++ b/solution.py
@@ -36,12 +36,13 @@
     return payload.reshape(owners, capacity, payload.shape[1])
 
 
-def place_frames(text, incoming, incoming_place):
-    lookup = incoming_place[None, :] == jnp.arange(text.shape[0], dtype=jnp.int32)[:, None]
-    covered = jnp.any(lookup, axis=1)
-    placed = jnp.dot(
-        lookup.astype(incoming.dtype), incoming, preferred_element_type=jnp.float32
-    ).astype(text.dtype)
+def place_frames(text, incoming, incoming_place, width):
+    lookup = incoming_place[None] == jnp.arange(text.shape[0], dtype=jnp.int32)[:, None, None]
+    covered = jnp.any(lookup, axis=(1, 2))
+    placed = lax.dot_general(
+        lookup.astype(incoming.dtype), incoming, (((1, 2), (0, 1)), ((), ())),
+        preferred_element_type=jnp.float32,
+    )[:, :width].astype(text.dtype)
     return jnp.where(covered[:, None], placed, text)
 
 
@@ -183,10 +184,9 @@
     first_row = shard_index * shard_rows
     payload = frame_slots(frames, tile_pos, frame_count, shard_rows, seq_count, capacity)
     gathered = exchange_frames(payload, vis_count)
-    gathered = gathered.reshape(-1, gathered.shape[-1])
     width = text.shape[1]
-    incoming_place = gathered[:, width].astype(jnp.int32)
-    merged = place_frames(text, gathered[:, :width], incoming_place)
+    incoming_place = gathered[:, :, width].astype(jnp.int32)
+    merged = place_frames(text, gathered, incoming_place, width)
     widened = merged.astype(jnp.float32)
     mean_square = jnp.mean(widened * widened, axis=1, keepdims=True)
     normed = (widened * lax.rsqrt(mean_square + epsilon) * norm_gain).astype(jnp.bfloat16)

time: 142 us -> 138 us (0.972)
  the two profiles are of different devices: /device:TPU:57 before, /device:TPU:48 now
where the time goes in v5:
time: 138 us
  Pallas kernels  76.2 us (55%)
  matrix products  20.9 us (15%)
  between operations  16.9 us (12%)
  waiting for transfers between devices  12.7 us (9%)
  other arithmetic  6.83 us (5%)
  local copies, waits for them, and re-layouts  4.16 us (3%)
    pallas_call x1, Pallas kernels, exchange_frames(): pl.pallas_call(exchange_kernel, out_shape=jax.ShapeDtypeStruct((vis_count...  54.3 us
    pallas_call x1, Pallas kernels, flash_attention(): pl.pallas_call(flash_kernel, out_shape=jax.ShapeDtypeStruct((rows, width)...  21.9 us
    all_gather x1, waiting for transfers between devices, on_device(): incoming_keys = lax.all_gather(keyval, 'seq', axis=0, tiled=True)  12.7 us
    dot_general x1, matrix products, on_device(): jnp.dot(normed, w_query, preferred_element_type=jnp.float32) + q_bias  12.6 us
    dot_general x1, matrix products, place_frames(): lax.dot_general(lookup.astype(incoming.dtype), incoming, (((1, 2), (0, 1)...  3.67 us
  transfers between devices with their start and end apart: 1, of which 1 were waited for; matrix products, arithmetic and copies ran while one was open for 12% of the time, Pallas kernels for 0%

profile of v5, /device:TPU:48, one launch (start us, length us, event | category | flops | bytes accessed | tf_op | source)
XLA Modules:
  0.0 137.6 jit_solution(13166760934423856309)
XLA Ops:
  6.5 0.0 all-gather.2.cloned.1.call-start
  7.3 0.7 multiply_subtract_fusion
  8.0 0.1 fusion.7
  8.2 0.1 fusion.11
  8.3 0.1 select_reduce_fusion
  8.4 1.5 %convolution_convert_fusion = bf16[32,8192]{1,0:T(8,128)(2,1)S(1)} fusion(bf16[32,8192]{1,0:T(8,128)(2,1)} %param.12, s32[32]{0:T(128)S(1)} %multiply_add_fusion, pred[32]{0:T(512)(128)(4,1)S(1)} %iota_compare_fusion.7), kind=kOutput, calls=%fused_computation.3 | convolution fusion | flops 17041408 | bytes 1048736 | tf_op jit(solution)/shard_map/dot_general | solution.py:31
  9.8 0.1 broadcast_in_dim.27
  10.0 1.0 reshape.40.payload_ref
  11.0 54.3 %shard_map.109 = bf16[128,2,8320]{2,1,0:T(2,128)(2,1)} custom-call(bf16[16,2,8320]{2,1,0:T(2,128)(2,1)} %reshape.40.payload_ref), custom_call_target="tpu_custom_call" | custom-call | tf_op jit(solution)/shard_map/pallas_call | solution.py:160
  65.3 0.9 slice_convert_fusion.1
  66.2 0.1 copy.26
  66.3 3.7 %convolution_bitcast_fusion = bf16[256,8320]{1,0:T(8,128)(2,1)S(1)} fusion(bf16[128,2,8320]{2,1,0:T(2,128)(2,1)} %shard_map.109, s32[128,2]{0,1:T(2,128)S(1)} %bitcast.17), kind=kOutput, calls=%fused_computation | convolution fusion | flops 1090584576 | bytes 8520704 | tf_op jit(solution)/shard_map/dot_general | solution.py:42
  69.9 0.1 fusion.8
  70.1 0.0 copy-done.1
  70.1 0.0 copy-start.5
  70.1 2.3 %fusion = (f32[256]{0:T(256)S(1)}, bf16[256,8192]{1,0:T(8,128)(2,1)S(1)}) fusion(bf16[256,8192]{1,0:T(8,128)(2,1)S(1)} %copy-done.1, bf16[256,8320]{1,0:T(8,128)(2,1)S(1)} %convolution_bitcast_fusion, pred[256]{0:T(512)(128)(4,1)S(1)} %fusion.8), kind=kLoop, calls=%fused_computation.4 | loop fusion | flops 8388352 | bytes 12584192 | tf_op jit(solution)/shard_map/reduce_sum | solution.py:191
  72.4 0.0 copy-start.4
  72.4 0.0 copy-start.7
  72.4 1.5 %convolution_convert_fusion.1 = bf16[256,128]{1,0:T(8,128)(2,1)S(1)} fusion(bf16[8192,128]{1,0:T(8,128)(2,1)S(1)} %copy-done, bf16[256,8192]{1,0:T(8,128)(2,1)S(1)} %get-tuple-element.6, f32[8192]{0:T(1024)S(1)} %copy-done.5, f32[256]{0:T(256)S(1)} %add_rsqrt_fusion), kind=kOutput, calls=%fused_computation.14 | convolution fusion | flops 545292288 | bytes 6390784 | tf_op jit(solution)/shard_map/dot_general | solution.py:196
  74.0 0.5 copy-done.2
  74.5 1.0 copy-done.4
  75.5 1.5 %fusion.6 = bf16[256,128]{1,0:T(8,128)(2,1)S(1)} fusion(bf16[8192,128]{1,0:T(8,128)(2,1)S(1)} %copy-done.4, f32[128]{0:T(128)S(1)} %copy-done.7, bf16[256,8192]{1,0:T(8,128)(2,1)S(1)} %get-tuple-element.6, f32[8192]{0:T(1024)S(1)} %copy-done.5, f32[256]{0:T(256)S(1)} %add_rsqrt_fusion), kind=kOutput, calls=%fused_computation.13 | convolution fusion | flops 545325056 | bytes 6391296 | tf_op jit(solution)/shard_map/dot_general | solution.py:197
  77.0 0.7 pad_maximum_fusion.1
  77.7 0.0 all-gather.2.cloned.1.call-update
  77.8 0.1 dynamic_slice.3
  77.8 0.5 slice.10
  78.4 1.3 convert_reduce_fusion
  82.2 0.8 copy.30.qdoc_ref
  83.0 0.6 pad_add_fusion.range_ref
  83.6 12.6 %fusion.5.q_ref = bf16[256,1024]{1,0:T(8,128)(2,1)} fusion(bf16[8192,1024]{1,0:T(8,128)(2,1)} %param.17, f32[1024]{0:T(1024)S(1)} %copy-done.6, bf16[256,8192]{1,0:T(8,128)(2,1)} %copy-done.2, f32[8192]{0:T(1024)S(1)} %copy-done.5, f32[256]{0:T(256)S(1)} %add_rsqrt_fusion), kind=kOutput, calls=%fused_computation.11 | convolution fusion | flops 4303880192 | bytes 21533696 | tf_op jit(solution)/shard_map/dot_general | solution.py:193
  96.2 12.7 %all-gather.2.cloned.1.call-done.k_ref.v_ref = bf16[4096,256]{1,0:T(8,128)(2,1)} async-done(((bf16[256,256]{1,0:T(8,128)(2,1)}), bf16[4096,256]{1,0:T(8,128)(2,1)}) %all-gather.2.cloned.1.call-update) | async-done | bytes 2097168 | tf_op jit(solution)/shard_map/all_gather | solution.py:204
  108.9 21.9 %shard_map.110 = bf16[256,1024]{1,0:T(8,128)(2,1)} custom-call(s32[3]{0:T(128)} %pad_add_fusion.range_ref, bf16[256,1024]{1,0:T(8,128)(2,1)} %fusion.5.q_ref, bf16[4096,256]{1,0:T(8,128)(2,1)} %all-gather.2.cloned.1.call-done.k_ref.v_ref, bf16[4096,256]{1,0:T(8,128)(2,1)} %all-gather.2.cloned.1.call-done.k_ref.v_ref, s32[256,1]{1,0:T(8,128)} %copy.30.qdoc_ref, ...), custom_call_target="tpu_custom_call" | custom-call | flops 2147483648 | bytes 3145728 | tf_op jit(solution)/shard_map/pallas_call | solution.py:291
  (15 shorter events, 0.1 us)
Async XLA Ops:
  6.5 65.9 %copy-start = (bf16[8192,128]{1,0:T(8,128)(2,1)S(1)}, bf16[8192,128]{1,0:T(8,128)(2,1)}, u32[]{:S(2)}) copy-start(bf16[8192,128]{1,0:T(8,128)(2,1)} %param.19) | copy-start | bytes 6291460
  6.5 102.4 %all-gather.2.cloned.1.call-start = ((), (), s32[]{:S(2)}) async-start(), calls=%async_computation | async-start | bytes 2228224 | tf_op jit(solution)/shard_map/all_gather | solution.py:204
  66.3 3.8 %copy-start.1 = (bf16[256,8192]{1,0:T(8,128)(2,1)S(1)}, bf16[256,8192]{1,0:T(8,128)(2,1)}, u32[]{:S(2)}) copy-start(bf16[256,8192]{1,0:T(8,128)(2,1)} %param.11) | copy-start | bytes 12582916
  70.1 2.3 %copy-start.5 = (f32[8192]{0:T(1024)S(1)}, f32[8192]{0:T(1024)}, u32[]{:S(2)}) copy-start(f32[8192]{0:T(1024)} %param.16) | copy-start | bytes 98308
  72.4 2.1 %copy-start.2 = (bf16[256,8192]{1,0:T(8,128)(2,1)}, bf16[256,8192]{1,0:T(8,128)(2,1)S(1)}, u32[]{:S(2)}) copy-start(bf16[256,8192]{1,0:T(8,128)(2,1)S(1)} %get-tuple-element.6) | copy-start | bytes 12582916
  72.4 3.1 %copy-start.4 = (bf16[8192,128]{1,0:T(8,128)(2,1)S(1)}, bf16[8192,128]{1,0:T(8,128)(2,1)}, u32[]{:S(2)}) copy-start(bf16[8192,128]{1,0:T(8,128)(2,1)} %param.20) | copy-start | bytes 6291460
  72.4 3.1 %copy-start.7 = (f32[128]{0:T(128)S(1)}, f32[128]{0:T(128)}, u32[]{:S(2)}) copy-start(f32[128]{0:T(128)} %param.21) | copy-start | bytes 1540
  75.5 2.2 %copy-start.3 = (s32[4096]{0:T(1024)S(1)}, s32[4096]{0:T(1024)}, u32[]{:S(2)}) copy-start(s32[4096]{0:T(1024)} %param.15) | copy-start | bytes 49156
  75.5 8.1 %copy-start.6 = (f32[1024]{0:T(1024)S(1)}, f32[1024]{0:T(1024)}, u32[]{:S(2)}) copy-start(f32[1024]{0:T(1024)} %param.18) | copy-start | bytes 12292
Sparse Core Ops, SparseCore 0:
  77.9 31.0 all-gather.1

commit v6 on v5

--- a/solution.py
+++ b/solution.py
@@ -190,6 +190,7 @@
     widened = merged.astype(jnp.float32)
     mean_square = jnp.mean(widened * widened, axis=1, keepdims=True)
     normed = (widened * lax.rsqrt(mean_square + epsilon) * norm_gain).astype(jnp.bfloat16)
+    normed = lax.optimization_barrier(normed)
     queries = (jnp.dot(normed, w_query, preferred_element_type=jnp.float32) + q_bias).astype(
         jnp.bfloat16
     )

time: 138 us -> 139 us (level)
  the two profiles are of different devices: /device:TPU:48 before, /device:TPU:49 now
where the time goes in v6:
time: 139 us
  Pallas kernels  75.6 us (54%)
  matrix products  20.3 us (15%)
  between operations  16.9 us (12%)
  waiting for transfers between devices  13.9 us (10%)
  other arithmetic  7.95 us (6%)
  local copies, waits for them, and re-layouts  4.4 us (3%)
    pallas_call x1, Pallas kernels, exchange_frames(): pl.pallas_call(exchange_kernel, out_shape=jax.ShapeDtypeStruct((vis_count...  53.5 us
    pallas_call x1, Pallas kernels, flash_attention(): pl.pallas_call(flash_kernel, out_shape=jax.ShapeDtypeStruct((rows, width)...  22 us
    all_gather x1, waiting for transfers between devices, on_device(): incoming_keys = lax.all_gather(keyval, 'seq', axis=0, tiled=True)  13.9 us
    dot_general x1, matrix products, on_device(): jnp.dot(normed, w_query, preferred_element_type=jnp.float32) + q_bias  12.5 us
    dot_general x1, matrix products, place_frames(): lax.dot_general(lookup.astype(incoming.dtype), incoming, (((1, 2), (0, 1)...  3.67 us
  transfers between devices with their start and end apart: 1, of which 1 were waited for; matrix products, arithmetic and copies ran while one was open for 11% of the time, Pallas kernels for 0%

profile of v6, /device:TPU:49, one launch (start us, length us, event | category | flops | bytes accessed | tf_op | source)
XLA Modules:
  0.0 139.1 jit_solution(7274966530465580031)
XLA Ops:
  6.5 0.0 copy-start
  6.5 0.0 all-gather.2.cloned.1.call-start
  7.3 0.7 multiply_subtract_fusion
  8.0 0.1 fusion.7
  8.2 0.1 fusion.11
  8.3 0.1 select_reduce_fusion
  8.4 1.5 %convolution_convert_fusion = bf16[32,8192]{1,0:T(8,128)(2,1)S(1)} fusion(bf16[32,8192]{1,0:T(8,128)(2,1)} %param.12, s32[32]{0:T(128)S(1)} %multiply_add_fusion, pred[32]{0:T(512)(128)(4,1)S(1)} %iota_compare_fusion.7), kind=kOutput, calls=%fused_computation.3 | convolution fusion | flops 17041408 | bytes 1048736 | tf_op jit(solution)/shard_map/dot_general | solution.py:31
  9.8 0.1 broadcast_in_dim.27
  10.0 1.0 reshape.40.payload_ref
  11.0 53.5 %shard_map.109 = bf16[128,2,8320]{2,1,0:T(2,128)(2,1)} custom-call(bf16[16,2,8320]{2,1,0:T(2,128)(2,1)} %reshape.40.payload_ref), custom_call_target="tpu_custom_call" | custom-call | tf_op jit(solution)/shard_map/pallas_call | solution.py:160
  64.5 0.9 slice_convert_fusion.1
  65.4 0.1 copy.26
  65.5 3.7 %convolution_bitcast_fusion = bf16[256,8320]{1,0:T(8,128)(2,1)S(1)} fusion(bf16[128,2,8320]{2,1,0:T(2,128)(2,1)} %shard_map.109, s32[128,2]{0,1:T(2,128)S(1)} %bitcast.20), kind=kOutput, calls=%fused_computation | convolution fusion | flops 1090584576 | bytes 8520704 | tf_op jit(solution)/shard_map/dot_general | solution.py:42
  69.2 0.1 fusion.8
  69.3 0.0 copy-start.4
  69.3 2.2 %fusion = (f32[256]{0:T(256)S(1)}, bf16[256,8192]{1,0:T(8,128)(2,1)S(1)}) fusion(bf16[256,8192]{1,0:T(8,128)(2,1)S(1)} %copy-done.2, bf16[256,8320]{1,0:T(8,128)(2,1)S(1)} %convolution_bitcast_fusion, pred[256]{0:T(512)(128)(4,1)S(1)} %fusion.8), kind=kLoop, calls=%fused_computation.4 | loop fusion | flops 8388352 | bytes 12584192 | tf_op jit(solution)/shard_map/reduce_sum | solution.py:191
  71.6 1.2 fusion.2
  72.8 0.0 copy-start.3
  72.8 0.0 copy-start.6
  72.8 1.3 convolution_convert_fusion.1
  74.1 1.8 %copy-done.3 = bf16[8192,128]{1,0:T(8,128)(2,1)S(1)} copy-done((bf16[8192,128]{1,0:T(8,128)(2,1)S(1)}, bf16[8192,128]{1,0:T(8,128)(2,1)}, u32[]{:S(2)}) %copy-start.3) | copy-done | bytes 2097176
  75.9 1.2 fusion.6
  77.2 0.7 pad_maximum_fusion.1
  77.8 0.0 all-gather.2.cloned.1.call-update
  77.9 0.1 dynamic_slice.3
  78.0 0.5 slice.10
  78.5 1.3 convert_reduce_fusion
  82.4 0.8 copy.30.qdoc_ref
  83.2 0.6 pad_add_fusion.range_ref
  83.8 12.5 %fusion.5.q_ref = bf16[256,1024]{1,0:T(8,128)(2,1)} fusion(bf16[256,8192]{1,0:T(8,128)(2,1)} %copy-done.1, bf16[8192,1024]{1,0:T(8,128)(2,1)} %param.17, f32[1024]{0:T(1024)S(1)} %copy-done.7), kind=kOutput, calls=%fused_computation.11 | convolution fusion | flops 4295491584 | bytes 21499904 | tf_op jit(solution)/shard_map/dot_general | solution.py:194
  96.3 13.9 %all-gather.2.cloned.1.call-done.k_ref.v_ref = bf16[4096,256]{1,0:T(8,128)(2,1)} async-done(((bf16[256,256]{1,0:T(8,128)(2,1)}), bf16[4096,256]{1,0:T(8,128)(2,1)}) %all-gather.2.cloned.1.call-update) | async-done | bytes 2097168 | tf_op jit(solution)/shard_map/all_gather | solution.py:205
  110.2 22.0 %shard_map.110 = bf16[256,1024]{1,0:T(8,128)(2,1)} custom-call(s32[3]{0:T(128)} %pad_add_fusion.range_ref, bf16[256,1024]{1,0:T(8,128)(2,1)} %fusion.5.q_ref, bf16[4096,256]{1,0:T(8,128)(2,1)} %all-gather.2.cloned.1.call-done.k_ref.v_ref, bf16[4096,256]{1,0:T(8,128)(2,1)} %all-gather.2.cloned.1.call-done.k_ref.v_ref, s32[256,1]{1,0:T(8,128)} %copy.30.qdoc_ref, ...), custom_call_target="tpu_custom_call" | custom-call | flops 2147483648 | bytes 3145728 | tf_op jit(solution)/shard_map/pallas_call | solution.py:292
  (16 shorter events, 0.1 us)
Async XLA Ops:
  6.5 66.2 %copy-start = (bf16[8192,128]{1,0:T(8,128)(2,1)S(1)}, bf16[8192,128]{1,0:T(8,128)(2,1)}, u32[]{:S(2)}) copy-start(bf16[8192,128]{1,0:T(8,128)(2,1)} %param.19) | copy-start | bytes 6291460
  6.5 103.6 %all-gather.2.cloned.1.call-start = ((), (), s32[]{:S(2)}) async-start(), calls=%async_computation | async-start | bytes 2228224 | tf_op jit(solution)/shard_map/all_gather | solution.py:205
  65.5 3.8 %copy-start.2 = (bf16[256,8192]{1,0:T(8,128)(2,1)S(1)}, bf16[256,8192]{1,0:T(8,128)(2,1)}, u32[]{:S(2)}) copy-start(bf16[256,8192]{1,0:T(8,128)(2,1)} %param.11) | copy-start | bytes 12582916
  69.3 2.2 %copy-start.4 = (f32[8192]{0:T(1024)S(1)}, f32[8192]{0:T(1024)}, u32[]{:S(2)}) copy-start(f32[8192]{0:T(1024)} %param.16) | copy-start | bytes 98308
  72.8 4.4 %copy-start.1 = (bf16[256,8192]{1,0:T(8,128)(2,1)}, bf16[256,8192]{1,0:T(8,128)(2,1)S(1)}, u32[]{:S(2)}) copy-start(bf16[256,8192]{1,0:T(8,128)(2,1)S(1)} %fusion.2) | copy-start | bytes 12582916
  72.8 3.1 %copy-start.3 = (bf16[8192,128]{1,0:T(8,128)(2,1)S(1)}, bf16[8192,128]{1,0:T(8,128)(2,1)}, u32[]{:S(2)}) copy-start(bf16[8192,128]{1,0:T(8,128)(2,1)} %param.20) | copy-start | bytes 6291460
  72.8 3.1 %copy-start.6 = (f32[128]{0:T(128)S(1)}, f32[128]{0:T(128)}, u32[]{:S(2)}) copy-start(f32[128]{0:T(128)} %param.21) | copy-start | bytes 1540
  75.9 2.0 %copy-start.5 = (s32[4096]{0:T(1024)S(1)}, s32[4096]{0:T(1024)}, u32[]{:S(2)}) copy-start(s32[4096]{0:T(1024)} %param.15) | copy-start | bytes 49156
  75.9 7.9 %copy-start.7 = (f32[1024]{0:T(1024)S(1)}, f32[1024]{0:T(1024)}, u32[]{:S(2)}) copy-start(f32[1024]{0:T(1024)} %param.18) | copy-start | bytes 12292
Sparse Core Ops, SparseCore 0:
  78.0 32.1 all-gather.1

commit v7 on v5

--- a/solution.py
+++ b/solution.py
@@ -208,7 +208,7 @@
     return flash_attention(block_range, queries, incoming_keys, own_docs, doc_ids, kv_heads)
 
 
-KEY_BLOCK = 512
+KEY_BLOCK = 256
 
 
 def flash_kernel(

time: 138 us -> 151 us (1.094)
  the two profiles are of different devices: /device:TPU:48 before, /device:TPU:57 now
where the time goes in v7:
time: 151 us; the launch traced here: 150 us
  Pallas kernels  88 us (58%)
  matrix products  20.9 us (14%)
  between operations  16.9 us (11%)
  waiting for transfers between devices  13.3 us (9%)
  other arithmetic  6.83 us (5%)
  local copies, waits for them, and re-layouts  4.16 us (3%)
    pallas_call x1, Pallas kernels, exchange_frames(): pl.pallas_call(exchange_kernel, out_shape=jax.ShapeDtypeStruct((vis_count...  53.3 us
    pallas_call x1, Pallas kernels, flash_attention(): pl.pallas_call(flash_kernel, out_shape=jax.ShapeDtypeStruct((rows, width)...  34.6 us
    all_gather x1, waiting for transfers between devices, on_device(): incoming_keys = lax.all_gather(keyval, 'seq', axis=0, tiled=True)  13.3 us
    dot_general x1, matrix products, on_device(): jnp.dot(normed, w_query, preferred_element_type=jnp.float32) + q_bias  12.6 us
    dot_general x1, matrix products, place_frames(): lax.dot_general(lookup.astype(incoming.dtype), incoming, (((1, 2), (0, 1)...  3.68 us
  transfers between devices with their start and end apart: 1, of which 1 were waited for; matrix products, arithmetic and copies ran while one was open for 11% of the time, Pallas kernels for 0%

profile of v7, /device:TPU:57, one launch (start us, length us, event | category | flops | bytes accessed | tf_op | source)
XLA Modules:
  0.0 150.1 jit_solution(2715891319121766570)
XLA Ops:
  7.3 0.7 multiply_subtract_fusion
  8.0 0.1 fusion.7
  8.2 0.1 fusion.11
  8.3 0.1 select_reduce_fusion
  8.4 1.5 convolution_convert_fusion
  9.8 0.1 broadcast_in_dim.27
  10.0 1.0 reshape.40.payload_ref
  11.0 53.3 %shard_map.109 = bf16[128,2,8320]{2,1,0:T(2,128)(2,1)} custom-call(bf16[16,2,8320]{2,1,0:T(2,128)(2,1)} %reshape.40.payload_ref), custom_call_target="tpu_custom_call" | custom-call | tf_op jit(solution)/shard_map/pallas_call | solution.py:160
  64.3 0.9 slice_convert_fusion.1
  65.2 0.1 copy.26
  65.3 3.7 %convolution_bitcast_fusion = bf16[256,8320]{1,0:T(8,128)(2,1)S(1)} fusion(bf16[128,2,8320]{2,1,0:T(2,128)(2,1)} %shard_map.109, s32[128,2]{0,1:T(2,128)S(1)} %bitcast.17), kind=kOutput, calls=%fused_computation | convolution fusion | flops 1090584576 | bytes 8520704 | tf_op jit(solution)/shard_map/dot_general | solution.py:42
  69.0 0.1 fusion.8
  69.1 0.0 copy-done.1
  69.1 0.0 copy-start.5
  69.1 2.3 %fusion = (f32[256]{0:T(256)S(1)}, bf16[256,8192]{1,0:T(8,128)(2,1)S(1)}) fusion(bf16[256,8192]{1,0:T(8,128)(2,1)S(1)} %copy-done.1, bf16[256,8320]{1,0:T(8,128)(2,1)S(1)} %convolution_bitcast_fusion, pred[256]{0:T(512)(128)(4,1)S(1)} %fusion.8), kind=kLoop, calls=%fused_computation.4 | loop fusion | flops 8388352 | bytes 12584192 | tf_op jit(solution)/shard_map/reduce_sum | solution.py:191
  71.4 0.0 copy-done
  71.5 0.0 copy-start.4
  71.5 0.0 copy-start.7
  71.5 1.5 %convolution_convert_fusion.1 = bf16[256,128]{1,0:T(8,128)(2,1)S(1)} fusion(bf16[8192,128]{1,0:T(8,128)(2,1)S(1)} %copy-done, bf16[256,8192]{1,0:T(8,128)(2,1)S(1)} %get-tuple-element.6, f32[8192]{0:T(1024)S(1)} %copy-done.5, f32[256]{0:T(256)S(1)} %add_rsqrt_fusion), kind=kOutput, calls=%fused_computation.14 | convolution fusion | flops 545292288 | bytes 6390784 | tf_op jit(solution)/shard_map/dot_general | solution.py:196
  73.0 0.5 copy-done.2
  73.5 1.0 copy-done.4
  74.6 1.5 %fusion.6 = bf16[256,128]{1,0:T(8,128)(2,1)S(1)} fusion(bf16[8192,128]{1,0:T(8,128)(2,1)S(1)} %copy-done.4, f32[128]{0:T(128)S(1)} %copy-done.7, bf16[256,8192]{1,0:T(8,128)(2,1)S(1)} %get-tuple-element.6, f32[8192]{0:T(1024)S(1)} %copy-done.5, f32[256]{0:T(256)S(1)} %add_rsqrt_fusion), kind=kOutput, calls=%fused_computation.13 | convolution fusion | flops 545325056 | bytes 6391296 | tf_op jit(solution)/shard_map/dot_general | solution.py:197
  76.1 0.7 pad_maximum_fusion.1
  76.8 0.0 all-gather.2.cloned.1.call-update
  76.8 0.1 dynamic_slice.3
  76.9 0.5 slice.10
  77.4 1.3 convert_reduce_fusion
  81.3 0.8 copy.30.qdoc_ref
  82.1 0.6 pad_add_fusion.range_ref
  82.7 12.6 %fusion.5.q_ref = bf16[256,1024]{1,0:T(8,128)(2,1)} fusion(bf16[8192,1024]{1,0:T(8,128)(2,1)} %param.17, f32[1024]{0:T(1024)S(1)} %copy-done.6, bf16[256,8192]{1,0:T(8,128)(2,1)} %copy-done.2, f32[8192]{0:T(1024)S(1)} %copy-done.5, f32[256]{0:T(256)S(1)} %add_rsqrt_fusion), kind=kOutput, calls=%fused_computation.11 | convolution fusion | flops 4303880192 | bytes 21533696 | tf_op jit(solution)/shard_map/dot_general | solution.py:193
  95.3 13.3 %all-gather.2.cloned.1.call-done.k_ref.v_ref = bf16[4096,256]{1,0:T(8,128)(2,1)} async-done(((bf16[256,256]{1,0:T(8,128)(2,1)}), bf16[4096,256]{1,0:T(8,128)(2,1)}) %all-gather.2.cloned.1.call-update) | async-done | bytes 2097168 | tf_op jit(solution)/shard_map/all_gather | solution.py:204
  108.6 34.6 %shard_map.110 = bf16[256,1024]{1,0:T(8,128)(2,1)} custom-call(s32[3]{0:T(128)} %pad_add_fusion.range_ref, bf16[256,1024]{1,0:T(8,128)(2,1)} %fusion.5.q_ref, bf16[4096,256]{1,0:T(8,128)(2,1)} %all-gather.2.cloned.1.call-done.k_ref.v_ref, bf16[4096,256]{1,0:T(8,128)(2,1)} %all-gather.2.cloned.1.call-done.k_ref.v_ref, s32[256,1]{1,0:T(8,128)} %copy.30.qdoc_ref, ...), custom_call_target="tpu_custom_call" | custom-call | flops 2147483648 | bytes 3145728 | tf_op jit(solution)/shard_map/pallas_call | solution.py:291
  (15 shorter events, 0.1 us)
Async XLA Ops:
  6.5 64.9 %copy-start = (bf16[8192,128]{1,0:T(8,128)(2,1)S(1)}, bf16[8192,128]{1,0:T(8,128)(2,1)}, u32[]{:S(2)}) copy-start(bf16[8192,128]{1,0:T(8,128)(2,1)} %param.19) | copy-start | bytes 6291460
  6.5 102.1 %all-gather.2.cloned.1.call-start = ((), (), s32[]{:S(2)}) async-start(), calls=%async_computation | async-start | bytes 2228224 | tf_op jit(solution)/shard_map/all_gather | solution.py:204
  65.3 3.8 %copy-start.1 = (bf16[256,8192]{1,0:T(8,128)(2,1)S(1)}, bf16[256,8192]{1,0:T(8,128)(2,1)}, u32[]{:S(2)}) copy-start(bf16[256,8192]{1,0:T(8,128)(2,1)} %param.11) | copy-start | bytes 12582916
  69.1 2.3 %copy-start.5 = (f32[8192]{0:T(1024)S(1)}, f32[8192]{0:T(1024)}, u32[]{:S(2)}) copy-start(f32[8192]{0:T(1024)} %param.16) | copy-start | bytes 98308
  71.4 2.1 %copy-start.2 = (bf16[256,8192]{1,0:T(8,128)(2,1)}, bf16[256,8192]{1,0:T(8,128)(2,1)S(1)}, u32[]{:S(2)}) copy-start(bf16[256,8192]{1,0:T(8,128)(2,1)S(1)} %get-tuple-element.6) | copy-start | bytes 12582916
  71.5 3.1 %copy-start.4 = (bf16[8192,128]{1,0:T(8,128)(2,1)S(1)}, bf16[8192,128]{1,0:T(8,128)(2,1)}, u32[]{:S(2)}) copy-start(bf16[8192,128]{1,0:T(8,128)(2,1)} %param.20) | copy-start | bytes 6291460
  71.5 3.1 %copy-start.7 = (f32[128]{0:T(128)S(1)}, f32[128]{0:T(128)}, u32[]{:S(2)}) copy-start(f32[128]{0:T(128)} %param.21) | copy-start | bytes 1540
  74.6 2.2 %copy-start.3 = (s32[4096]{0:T(1024)S(1)}, s32[4096]{0:T(1024)}, u32[]{:S(2)}) copy-start(s32[4096]{0:T(1024)} %param.15) | copy-start | bytes 49156
  74.6 8.1 %copy-start.6 = (f32[1024]{0:T(1024)S(1)}, f32[1024]{0:T(1024)}, u32[]{:S(2)}) copy-start(f32[1024]{0:T(1024)} %param.18) | copy-start | bytes 12292
Sparse Core Ops, SparseCore 0:
  76.9 31.6 all-gather.1

commit v8 on v5

--- a/solution.py
+++ b/solution.py
@@ -211,8 +211,12 @@
 KEY_BLOCK = 512
 
 
+CHUNK = 32
+
+
 def flash_kernel(
-    range_ref, q_ref, k_ref, v_ref, qdoc_ref, kdoc_ref, out_ref, peak_ref, total_ref, acc_ref
+    range_ref, q_ref, k_ref, v_ref, qdoc_ref, kdoc_ref, out_ref,
+    peak_ref, total_ref, acc_ref, score_ref, weight_ref,
 ):
     step = pl.program_id(0)
     block = range_ref[0] + step
@@ -228,31 +232,46 @@
     @pl.when(block <= range_ref[1])
     def _():
         key_place = block * KEY_BLOCK + lax.broadcasted_iota(jnp.int32, (1, KEY_BLOCK), 1)
-        query_place = range_ref[2] + lax.broadcasted_iota(jnp.int32, (rows, 1), 0)
-        allowed = (key_place <= query_place) & (kdoc_ref[...] == qdoc_ref[...])
+        key_docs = kdoc_ref[...]
         keys = k_ref[...]
         vals = v_ref[...]
         for h in range(heads):
             cols = slice(h * HEAD_DIM, (h + 1) * HEAD_DIM)
-            scores = lax.dot_general(
+            score_ref[...] = lax.dot_general(
                 q_ref[:, cols], keys, (((1,), (1,)), ((), ())),
                 preferred_element_type=jnp.float32,
             ) * HEAD_DIM ** (-0.5)
-            scores = jnp.where(allowed, scores, negative)
-            old_peak = peak_ref[h]
-            new_peak = jnp.maximum(old_peak, jnp.max(scores, axis=1, keepdims=True))
-            raised = jnp.where(allowed, jnp.exp(scores - new_peak[:, :1]), 0.0)
-            factor = jnp.exp(old_peak - new_peak)
-            total_ref[h] = total_ref[h] * factor + jnp.sum(raised, axis=1, keepdims=True)
-            peak_ref[h] = new_peak
-            product = jnp.dot(raised.astype(jnp.bfloat16), vals, preferred_element_type=jnp.float32)
-            acc_ref[:, cols] = acc_ref[:, cols] * factor[:, :1] + product
+
+            def chunk(c, carry, h=h, cols=cols):
+                r = pl.ds(pl.multiple_of(c * CHUNK, CHUNK), CHUNK)
+                query_place = (
+                    range_ref[2] + c * CHUNK
+                    + lax.broadcasted_iota(jnp.int32, (CHUNK, 1), 0)
+                )
+                allowed = (key_place <= query_place) & (key_docs == qdoc_ref[r, :])
+                scores = jnp.where(allowed, score_ref[r, :], negative)
+                old_peak = peak_ref[h, r, :]
+                new_peak = jnp.maximum(old_peak, jnp.max(scores, axis=1, keepdims=True))
+                raised = jnp.where(allowed, jnp.exp(scores - new_peak), 0.0)
+                factor = jnp.exp(old_peak - new_peak)
+                total_ref[h, r, :] = total_ref[h, r, :] * factor + jnp.sum(
+                    raised, axis=1, keepdims=True
+                )
+                peak_ref[h, r, :] = new_peak
+                weight_ref[r, :] = raised.astype(jnp.bfloat16)
+                acc_ref[r, cols] = acc_ref[r, cols] * factor
+                return carry
+
+            lax.fori_loop(0, rows // CHUNK, chunk, 0)
+            acc_ref[:, cols] = acc_ref[:, cols] + jnp.dot(
+                weight_ref[...], vals, preferred_element_type=jnp.float32
+            )
 
     @pl.when(step == pl.num_programs(0) - 1)
     def _():
         for h in range(heads):
             cols = slice(h * HEAD_DIM, (h + 1) * HEAD_DIM)
-            out_ref[:, cols] = (acc_ref[:, cols] / total_ref[h][:, :1]).astype(out_ref.dtype)
+            out_ref[:, cols] = (acc_ref[:, cols] / total_ref[h]).astype(out_ref.dtype)
 
 
 def flash_attention(block_range, queries, keyval, own_docs, doc_ids, kv_heads):
@@ -285,6 +304,8 @@
             pltpu.VMEM((heads, rows, 1), jnp.float32),
             pltpu.VMEM((heads, rows, 1), jnp.float32),
             pltpu.VMEM((rows, width), jnp.float32),
+            pltpu.VMEM((rows, KEY_BLOCK), jnp.float32),
+            pltpu.VMEM((rows, KEY_BLOCK), jnp.bfloat16),
         ],
     )
     flops = 4 * rows * width * key_rows // 2

time: 138 us -> 210 us (1.52)
  the two profiles are of different devices: /device:TPU:48 before, /device:TPU:43 now
where the time goes in v8:
time: 210 us
  Pallas kernels  145 us (69%)
  matrix products  20.8 us (10%)
  between operations  16.9 us (8%)
  waiting for transfers between devices  16.2 us (8%)
  other arithmetic  6.83 us (3%)
  local copies, waits for them, and re-layouts  4.16 us (2%)
    pallas_call x1, Pallas kernels, flash_attention(): pl.pallas_call(flash_kernel, out_shape=jax.ShapeDtypeStruct((rows, width)...  93.6 us
    pallas_call x1, Pallas kernels, exchange_frames(): pl.pallas_call(exchange_kernel, out_shape=jax.ShapeDtypeStruct((vis_count...  51.5 us
    all_gather x1, waiting for transfers between devices, on_device(): incoming_keys = lax.all_gather(keyval, 'seq', axis=0, tiled=True)  16.2 us
    dot_general x1, matrix products, on_device(): jnp.dot(normed, w_query, preferred_element_type=jnp.float32) + q_bias  12.5 us
  transfers between devices with their start and end apart: 1, of which 1 were waited for; matrix products, arithmetic and copies ran while one was open for 8% of the time, Pallas kernels for 0%

profile of v8, /device:TPU:43, one launch (start us, length us, event | category | flops | bytes accessed | tf_op | source)
XLA Modules:
  0.0 210.0 jit_solution(17131231982563074816)
XLA Ops:
  6.5 0.0 copy-start
  7.3 0.7 multiply_subtract_fusion
  8.0 0.1 fusion.7
  8.2 0.1 fusion.11
  8.3 0.1 select_reduce_fusion
  8.4 1.4 convolution_convert_fusion
  9.8 0.1 broadcast_in_dim.27
  10.0 1.0 reshape.40.payload_ref
  11.0 51.5 %shard_map.109 = bf16[128,2,8320]{2,1,0:T(2,128)(2,1)} custom-call(bf16[16,2,8320]{2,1,0:T(2,128)(2,1)} %reshape.40.payload_ref), custom_call_target="tpu_custom_call" | custom-call | tf_op jit(solution)/shard_map/pallas_call | solution.py:160
  62.5 0.9 slice_convert_fusion.1
  63.4 0.1 copy.26
  63.5 3.7 %convolution_bitcast_fusion = bf16[256,8320]{1,0:T(8,128)(2,1)S(1)} fusion(bf16[128,2,8320]{2,1,0:T(2,128)(2,1)} %shard_map.109, s32[128,2]{0,1:T(2,128)S(1)} %bitcast.17), kind=kOutput, calls=%fused_computation | convolution fusion | flops 1090584576 | bytes 8520704 | tf_op jit(solution)/shard_map/dot_general | solution.py:42
  67.1 0.1 fusion.8
  67.3 0.0 copy-done.1
  67.3 0.0 copy-start.5
  67.3 2.3 %fusion = (f32[256]{0:T(256)S(1)}, bf16[256,8192]{1,0:T(8,128)(2,1)S(1)}) fusion(bf16[256,8192]{1,0:T(8,128)(2,1)S(1)} %copy-done.1, bf16[256,8320]{1,0:T(8,128)(2,1)S(1)} %convolution_bitcast_fusion, pred[256]{0:T(512)(128)(4,1)S(1)} %fusion.8), kind=kLoop, calls=%fused_computation.4 | loop fusion | flops 8388352 | bytes 12584192 | tf_op jit(solution)/shard_map/reduce_sum | solution.py:191
  69.6 0.0 copy-start.4
  69.6 0.0 copy-start.7
  69.6 1.5 convolution_convert_fusion.1
  71.1 0.5 copy-done.2
  71.7 1.0 copy-done.4
  72.7 1.5 fusion.6
  74.2 0.7 pad_maximum_fusion.1
  74.9 0.0 all-gather.2.cloned.1.call-update
  74.9 0.1 dynamic_slice.3
  75.0 0.5 slice.10
  75.6 1.3 convert_reduce_fusion
  79.4 0.8 copy.30.qdoc_ref
  80.2 0.6 pad_add_fusion.range_ref
  80.8 12.5 %fusion.5.q_ref = bf16[256,1024]{1,0:T(8,128)(2,1)} fusion(bf16[8192,1024]{1,0:T(8,128)(2,1)} %param.17, f32[1024]{0:T(1024)S(1)} %copy-done.6, bf16[256,8192]{1,0:T(8,128)(2,1)} %copy-done.2, f32[8192]{0:T(1024)S(1)} %copy-done.5, f32[256]{0:T(256)S(1)} %add_rsqrt_fusion), kind=kOutput, calls=%fused_computation.11 | convolution fusion | flops 4303880192 | bytes 21533696 | tf_op jit(solution)/shard_map/dot_general | solution.py:193
  93.3 16.2 %all-gather.2.cloned.1.call-done.k_ref.v_ref = bf16[4096,256]{1,0:T(8,128)(2,1)} async-done(((bf16[256,256]{1,0:T(8,128)(2,1)}), bf16[4096,256]{1,0:T(8,128)(2,1)}) %all-gather.2.cloned.1.call-update) | async-done | bytes 2097168 | tf_op jit(solution)/shard_map/all_gather | solution.py:204
  109.5 93.6 %shard_map.110 = bf16[256,1024]{1,0:T(8,128)(2,1)} custom-call(s32[3]{0:T(128)} %pad_add_fusion.range_ref, bf16[256,1024]{1,0:T(8,128)(2,1)} %fusion.5.q_ref, bf16[4096,256]{1,0:T(8,128)(2,1)} %all-gather.2.cloned.1.call-done.k_ref.v_ref, bf16[4096,256]{1,0:T(8,128)(2,1)} %all-gather.2.cloned.1.call-done.k_ref.v_ref, s32[256,1]{1,0:T(8,128)} %copy.30.qdoc_ref, ...), custom_call_target="tpu_custom_call" | custom-call | flops 2147483648 | bytes 3145728 | tf_op jit(solution)/shard_map/pallas_call | solution.py:312
  (15 shorter events, 0.1 us)
Async XLA Ops:
  6.5 63.1 %copy-start = (bf16[8192,128]{1,0:T(8,128)(2,1)S(1)}, bf16[8192,128]{1,0:T(8,128)(2,1)}, u32[]{:S(2)}) copy-start(bf16[8192,128]{1,0:T(8,128)(2,1)} %param.19) | copy-start | bytes 6291460
  6.5 103.0 %all-gather.2.cloned.1.call-start = ((), (), s32[]{:S(2)}) async-start(), calls=%async_computation | async-start | bytes 2228224 | tf_op jit(solution)/shard_map/all_gather | solution.py:204
  63.5 3.8 %copy-start.1 = (bf16[256,8192]{1,0:T(8,128)(2,1)S(1)}, bf16[256,8192]{1,0:T(8,128)(2,1)}, u32[]{:S(2)}) copy-start(bf16[256,8192]{1,0:T(8,128)(2,1)} %param.11) | copy-start | bytes 12582916
  67.3 2.3 %copy-start.5 = (f32[8192]{0:T(1024)S(1)}, f32[8192]{0:T(1024)}, u32[]{:S(2)}) copy-start(f32[8192]{0:T(1024)} %param.16) | copy-start | bytes 98308
  69.6 2.1 %copy-start.2 = (bf16[256,8192]{1,0:T(8,128)(2,1)}, bf16[256,8192]{1,0:T(8,128)(2,1)S(1)}, u32[]{:S(2)}) copy-start(bf16[256,8192]{1,0:T(8,128)(2,1)S(1)} %get-tuple-element.6) | copy-start | bytes 12582916
  69.6 3.1 %copy-start.4 = (bf16[8192,128]{1,0:T(8,128)(2,1)S(1)}, bf16[8192,128]{1,0:T(8,128)(2,1)}, u32[]{:S(2)}) copy-start(bf16[8192,128]{1,0:T(8,128)(2,1)} %param.20) | copy-start | bytes 6291460
  69.6 3.1 %copy-start.7 = (f32[128]{0:T(128)S(1)}, f32[128]{0:T(128)}, u32[]{:S(2)}) copy-start(f32[128]{0:T(128)} %param.21) | copy-start | bytes 1540
  72.7 2.2 %copy-start.3 = (s32[4096]{0:T(1024)S(1)}, s32[4096]{0:T(1024)}, u32[]{:S(2)}) copy-start(s32[4096]{0:T(1024)} %param.15) | copy-start | bytes 49156
  72.7 8.1 %copy-start.6 = (f32[1024]{0:T(1024)S(1)}, f32[1024]{0:T(1024)}, u32[]{:S(2)}) copy-start(f32[1024]{0:T(1024)} %param.18) | copy-start | bytes 12292
Sparse Core Ops, SparseCore 0:
  75.0 34.4 all-gather.1

commit v9 on v7

--- a/solution.py
+++ b/solution.py
@@ -208,7 +208,7 @@
     return flash_attention(block_range, queries, incoming_keys, own_docs, doc_ids, kv_heads)
 
 
-KEY_BLOCK = 256
+KEY_BLOCK = 1024
 
 
 def flash_kernel(

time: 151 us -> 132 us (0.87)
  Pallas kernels: 88 us -> 67.9 us
    pallas_call x1, Pallas kernels: 34.6 us -> 14.5 us  [flash_attention(): pl.pallas_call(flash_kernel, out_shape=jax.ShapeDtypeStruct((rows, width)...]
  transfers between devices with their start and end apart: 1 -> 1, of which waited for: 1 -> 1; matrix products, arithmetic and copies ran while one was open for 11% -> 12% of each run, Pallas kernels for 0% -> 0%
where the time goes in v9:
time: 132 us; the launch traced here: 130 us
  Pallas kernels  67.9 us (51%)
  matrix products  20.9 us (16%)
  between operations  16.9 us (13%)
  waiting for transfers between devices  13.3 us (10%)
  other arithmetic  6.65 us (5%)
  local copies, waits for them, and re-layouts  4.16 us (3%)
    pallas_call x1, Pallas kernels, exchange_frames(): pl.pallas_call(exchange_kernel, out_shape=jax.ShapeDtypeStruct((vis_count...  53.3 us
    pallas_call x1, Pallas kernels, flash_attention(): pl.pallas_call(flash_kernel, out_shape=jax.ShapeDtypeStruct((rows, width)...  14.5 us
    all_gather x1, waiting for transfers between devices, on_device(): incoming_keys = lax.all_gather(keyval, 'seq', axis=0, tiled=True)  13.3 us
    dot_general x1, matrix products, on_device(): jnp.dot(normed, w_query, preferred_element_type=jnp.float32) + q_bias  12.6 us
    dot_general x1, matrix products, place_frames(): lax.dot_general(lookup.astype(incoming.dtype), incoming, (((1, 2), (0, 1)...  3.68 us
  transfers between devices with their start and end apart: 1, of which 1 were waited for; matrix products, arithmetic and copies ran while one was open for 12% of the time, Pallas kernels for 0%

profile of v9, /device:TPU:57, one launch (start us, length us, event | category | flops | bytes accessed | tf_op | source)
XLA Modules:
  0.0 129.8 jit_solution(9599543334620506964)
XLA Ops:
  7.3 0.7 multiply_subtract_fusion
  8.0 0.1 fusion.7
  8.2 0.1 fusion.11
  8.3 0.1 select_reduce_fusion
  8.4 1.5 %convolution_convert_fusion = bf16[32,8192]{1,0:T(8,128)(2,1)S(1)} fusion(bf16[32,8192]{1,0:T(8,128)(2,1)} %param.12, s32[32]{0:T(128)S(1)} %multiply_add_fusion, pred[32]{0:T(512)(128)(4,1)S(1)} %iota_compare_fusion.7), kind=kOutput, calls=%fused_computation.3 | convolution fusion | flops 17041408 | bytes 1048736 | tf_op jit(solution)/shard_map/dot_general | solution.py:31
  9.8 0.1 broadcast_in_dim.27
  10.0 1.0 reshape.40.payload_ref
  11.0 53.3 %shard_map.109 = bf16[128,2,8320]{2,1,0:T(2,128)(2,1)} custom-call(bf16[16,2,8320]{2,1,0:T(2,128)(2,1)} %reshape.40.payload_ref), custom_call_target="tpu_custom_call" | custom-call | tf_op jit(solution)/shard_map/pallas_call | solution.py:160
  64.3 0.9 slice_convert_fusion.1
  65.2 0.1 copy.26
  65.3 3.7 %convolution_bitcast_fusion = bf16[256,8320]{1,0:T(8,128)(2,1)S(1)} fusion(bf16[128,2,8320]{2,1,0:T(2,128)(2,1)} %shard_map.109, s32[128,2]{0,1:T(2,128)S(1)} %bitcast.17), kind=kOutput, calls=%fused_computation | convolution fusion | flops 1090584576 | bytes 8520704 | tf_op jit(solution)/shard_map/dot_general | solution.py:42
  69.0 0.1 fusion.8
  69.1 0.0 copy-done.1
  69.1 0.0 copy-start.5
  69.1 2.1 %fusion = (f32[256]{0:T(256)S(1)}, bf16[256,8192]{1,0:T(8,128)(2,1)S(1)}) fusion(bf16[256,8192]{1,0:T(8,128)(2,1)S(1)} %copy-done.1, bf16[256,8320]{1,0:T(8,128)(2,1)S(1)} %convolution_bitcast_fusion, pred[256]{0:T(512)(128)(4,1)S(1)} %fusion.8), kind=kLoop, calls=%fused_computation.4 | loop fusion | flops 8388352 | bytes 12584192 | tf_op jit(solution)/shard_map/reduce_sum | solution.py:191
  71.2 0.0 copy-start.2
  71.3 0.0 copy-start.4
  71.3 0.0 copy-start.7
  71.3 1.5 %convolution_convert_fusion.1 = bf16[256,128]{1,0:T(8,128)(2,1)S(1)} fusion(bf16[8192,128]{1,0:T(8,128)(2,1)S(1)} %copy-done, bf16[256,8192]{1,0:T(8,128)(2,1)S(1)} %get-tuple-element.6, f32[8192]{0:T(1024)S(1)} %copy-done.5, f32[256]{0:T(256)S(1)} %add_rsqrt_fusion), kind=kOutput, calls=%fused_computation.14 | convolution fusion | flops 545292288 | bytes 6390784 | tf_op jit(solution)/shard_map/dot_general | solution.py:196
  72.8 0.5 copy-done.2
  73.4 1.0 copy-done.4
  74.4 1.5 %fusion.6 = bf16[256,128]{1,0:T(8,128)(2,1)S(1)} fusion(bf16[8192,128]{1,0:T(8,128)(2,1)S(1)} %copy-done.4, f32[128]{0:T(128)S(1)} %copy-done.7, bf16[256,8192]{1,0:T(8,128)(2,1)S(1)} %get-tuple-element.6, f32[8192]{0:T(1024)S(1)} %copy-done.5, f32[256]{0:T(256)S(1)} %add_rsqrt_fusion), kind=kOutput, calls=%fused_computation.13 | convolution fusion | flops 545325056 | bytes 6391296 | tf_op jit(solution)/shard_map/dot_general | solution.py:197
  75.9 0.7 pad_maximum_fusion.1
  76.6 0.0 all-gather.2.cloned.1.call-update
  76.6 0.1 dynamic_slice.3
  76.7 0.5 slice.10
  77.2 1.3 %convert_reduce_fusion = s32[]{:T(128)} fusion(s32[4096]{0:T(1024)S(1)} %copy-done.3, s32[]{:T(128)} %bitcast), kind=kLoop, calls=%fused_computation.26 | loop fusion | flops 12287 | bytes 16392 | tf_op jit(solution)/shard_map/reduce_sum | solution.py:205
  81.1 0.8 copy.30.qdoc_ref
  81.9 0.6 pad_add_fusion.range_ref
  82.5 12.6 %fusion.5.q_ref = bf16[256,1024]{1,0:T(8,128)(2,1)} fusion(bf16[8192,1024]{1,0:T(8,128)(2,1)} %param.17, f32[1024]{0:T(1024)S(1)} %copy-done.6, bf16[256,8192]{1,0:T(8,128)(2,1)} %copy-done.2, f32[8192]{0:T(1024)S(1)} %copy-done.5, f32[256]{0:T(256)S(1)} %add_rsqrt_fusion), kind=kOutput, calls=%fused_computation.11 | convolution fusion | flops 4303880192 | bytes 21533696 | tf_op jit(solution)/shard_map/dot_general | solution.py:193
  95.1 13.3 %all-gather.2.cloned.1.call-done.k_ref.v_ref = bf16[4096,256]{1,0:T(8,128)(2,1)} async-done(((bf16[256,256]{1,0:T(8,128)(2,1)}), bf16[4096,256]{1,0:T(8,128)(2,1)}) %all-gather.2.cloned.1.call-update) | async-done | bytes 2097168 | tf_op jit(solution)/shard_map/all_gather | solution.py:204
  108.4 14.5 %shard_map.110 = bf16[256,1024]{1,0:T(8,128)(2,1)} custom-call(s32[3]{0:T(128)} %pad_add_fusion.range_ref, bf16[256,1024]{1,0:T(8,128)(2,1)} %fusion.5.q_ref, bf16[4096,256]{1,0:T(8,128)(2,1)} %all-gather.2.cloned.1.call-done.k_ref.v_ref, bf16[4096,256]{1,0:T(8,128)(2,1)} %all-gather.2.cloned.1.call-done.k_ref.v_ref, s32[256,1]{1,0:T(8,128)} %copy.30.qdoc_ref, ...), custom_call_target="tpu_custom_call" | custom-call | flops 2147483648 | bytes 3145728 | tf_op jit(solution)/shard_map/pallas_call | solution.py:291
  (15 shorter events, 0.1 us)
Async XLA Ops:
  6.5 64.7 %copy-start = (bf16[8192,128]{1,0:T(8,128)(2,1)S(1)}, bf16[8192,128]{1,0:T(8,128)(2,1)}, u32[]{:S(2)}) copy-start(bf16[8192,128]{1,0:T(8,128)(2,1)} %param.19) | copy-start | bytes 6291460
  6.5 101.9 %all-gather.2.cloned.1.call-start = ((), (), s32[]{:S(2)}) async-start(), calls=%async_computation | async-start | bytes 2228224 | tf_op jit(solution)/shard_map/all_gather | solution.py:204
  65.3 3.8 %copy-start.1 = (bf16[256,8192]{1,0:T(8,128)(2,1)S(1)}, bf16[256,8192]{1,0:T(8,128)(2,1)}, u32[]{:S(2)}) copy-start(bf16[256,8192]{1,0:T(8,128)(2,1)} %param.11) | copy-start | bytes 12582916
  69.1 2.2 %copy-start.5 = (f32[8192]{0:T(1024)S(1)}, f32[8192]{0:T(1024)}, u32[]{:S(2)}) copy-start(f32[8192]{0:T(1024)} %param.16) | copy-start | bytes 98308
  71.2 2.1 %copy-start.2 = (bf16[256,8192]{1,0:T(8,128)(2,1)}, bf16[256,8192]{1,0:T(8,128)(2,1)S(1)}, u32[]{:S(2)}) copy-start(bf16[256,8192]{1,0:T(8,128)(2,1)S(1)} %get-tuple-element.6) | copy-start | bytes 12582916
  71.3 3.1 %copy-start.4 = (bf16[8192,128]{1,0:T(8,128)(2,1)S(1)}, bf16[8192,128]{1,0:T(8,128)(2,1)}, u32[]{:S(2)}) copy-start(bf16[8192,128]{1,0:T(8,128)(2,1)} %param.20) | copy-start | bytes 6291460
  71.3 3.1 %copy-start.7 = (f32[128]{0:T(128)S(1)}, f32[128]{0:T(128)}, u32[]{:S(2)}) copy-start(f32[128]{0:T(128)} %param.21) | copy-start | bytes 1540
  74.4 2.2 %copy-start.3 = (s32[4096]{0:T(1024)S(1)}, s32[4096]{0:T(1024)}, u32[]{:S(2)}) copy-start(s32[4096]{0:T(1024)} %param.15) | copy-start | bytes 49156
  74.4 8.1 %copy-start.6 = (f32[1024]{0:T(1024)S(1)}, f32[1024]{0:T(1024)}, u32[]{:S(2)}) copy-start(f32[1024]{0:T(1024)} %param.18) | copy-start | bytes 12292
Sparse Core Ops, SparseCore 0:
  76.7 31.6 all-gather.1

commit v10 on v5

--- a/solution.py
+++ b/solution.py
@@ -200,8 +200,9 @@
     keyval = jnp.concatenate([key_rows, value_rows], axis=1)
     kv_heads = w_key.shape[1] // HEAD_DIM
     per_group = w_query.shape[1] // HEAD_DIM // kv_heads
+    incoming_keys = lax.all_gather(keyval, "seq", axis=0, tiled=True)
+    queries, doc_ids = lax.optimization_barrier((queries, doc_ids))
     own_docs = lax.dynamic_slice_in_dim(doc_ids, first_row, shard_rows)
-    incoming_keys = lax.all_gather(keyval, "seq", axis=0, tiled=True)
     doc_start = jnp.sum((doc_ids < own_docs[0]).astype(jnp.int32))
     last_row = first_row + shard_rows - 1
     block_range = jnp.stack([doc_start // KEY_BLOCK, last_row // KEY_BLOCK, first_row]).astype(jnp.int32)
@@ -209,6 +210,7 @@
 
 
 KEY_BLOCK = 512
+DOC_SPAN = 2048
 
 
 def flash_kernel(
@@ -258,7 +260,7 @@
 def flash_attention(block_range, queries, keyval, own_docs, doc_ids, kv_heads):
     rows, width = queries.shape
     key_rows = keyval.shape[0]
-    steps = key_rows // KEY_BLOCK
+    steps = min(key_rows // KEY_BLOCK, (DOC_SPAN + rows - 2) // KEY_BLOCK + 2)
     heads = width // HEAD_DIM
 
     def key_block(j, r):

time: 138 us -> 135 us (0.978)
  the two profiles are of different devices: /device:TPU:48 before, /device:TPU:43 now
where the time goes in v10:
time: 135 us; the launch traced here: 134 us
  Pallas kernels  69.6 us (52%)
  matrix products  20.6 us (15%)
  between operations  16.6 us (12%)
  waiting for transfers between devices  16.5 us (12%)
  other arithmetic  6.87 us (5%)
  local copies, waits for them, and re-layouts  4.29 us (3%)
    pallas_call x1, Pallas kernels, exchange_frames(): pl.pallas_call(exchange_kernel, out_shape=jax.ShapeDtypeStruct((vis_count...  51.5 us
    pallas_call x1, Pallas kernels, flash_attention(): pl.pallas_call(flash_kernel, out_shape=jax.ShapeDtypeStruct((rows, width)...  18.1 us
    all_gather x1, waiting for transfers between devices, on_device(): incoming_keys = lax.all_gather(keyval, 'seq', axis=0, tiled=True)  16.5 us
    dot_general x1, matrix products, on_device(): jnp.dot(normed, w_query, preferred_element_type=jnp.float32) + q_bias  12.4 us
    dot_general x1, matrix products, place_frames(): lax.dot_general(lookup.astype(incoming.dtype), incoming, (((1, 2), (0, 1)...  3.67 us
  transfers between devices with their start and end apart: 1, of which 1 were waited for; matrix products, arithmetic and copies ran while one was open for 12% of the time, Pallas kernels for 0%

profile of v10, /device:TPU:43, one launch (start us, length us, event | category | flops | bytes accessed | tf_op | source)
XLA Modules:
  0.0 134.4 jit_solution(16499697915901647219)
XLA Ops:
  6.5 0.0 copy-start
  7.3 0.7 multiply_subtract_fusion
  8.0 0.1 fusion.7
  8.2 0.1 fusion.11
  8.3 0.1 select_reduce_fusion
  8.4 1.4 %convolution_convert_fusion = bf16[32,8192]{1,0:T(8,128)(2,1)S(1)} fusion(bf16[32,8192]{1,0:T(8,128)(2,1)} %param.12, s32[32]{0:T(128)S(1)} %multiply_add_fusion, pred[32]{0:T(512)(128)(4,1)S(1)} %iota_compare_fusion.7), kind=kOutput, calls=%fused_computation.3 | convolution fusion | flops 17041408 | bytes 1048736 | tf_op jit(solution)/shard_map/dot_general | solution.py:31
  9.8 0.1 broadcast_in_dim.27
  10.0 1.0 reshape.40.payload_ref
  11.0 51.5 %shard_map.109 = bf16[128,2,8320]{2,1,0:T(2,128)(2,1)} custom-call(bf16[16,2,8320]{2,1,0:T(2,128)(2,1)} %reshape.40.payload_ref), custom_call_target="tpu_custom_call" | custom-call | tf_op jit(solution)/shard_map/pallas_call | solution.py:160
  62.5 0.9 slice_convert_fusion.1
  63.4 0.1 copy.26
  63.5 3.7 %convolution_bitcast_fusion = bf16[256,8320]{1,0:T(8,128)(2,1)S(1)} fusion(bf16[128,2,8320]{2,1,0:T(2,128)(2,1)} %shard_map.109, s32[128,2]{0,1:T(2,128)S(1)} %bitcast.17), kind=kOutput, calls=%fused_computation | convolution fusion | flops 1090584576 | bytes 8520704 | tf_op jit(solution)/shard_map/dot_general | solution.py:42
  67.1 0.1 fusion.8
  67.3 0.0 copy-start.5
  67.3 2.3 %fusion = (f32[256]{0:T(256)S(1)}, bf16[256,8192]{1,0:T(8,128)(2,1)S(1)}) fusion(bf16[256,8192]{1,0:T(8,128)(2,1)S(1)} %copy-done.1, bf16[256,8320]{1,0:T(8,128)(2,1)S(1)} %convolution_bitcast_fusion, pred[256]{0:T(512)(128)(4,1)S(1)} %fusion.8), kind=kLoop, calls=%fused_computation.4 | loop fusion | flops 8388352 | bytes 12584192 | tf_op jit(solution)/shard_map/reduce_sum | solution.py:191
  69.6 0.0 copy-start.4
  69.6 0.0 copy-start.7
  69.6 1.4 %convolution_convert_fusion.1 = bf16[256,128]{1,0:T(8,128)(2,1)S(1)} fusion(bf16[8192,128]{1,0:T(8,128)(2,1)S(1)} %copy-done, bf16[256,8192]{1,0:T(8,128)(2,1)S(1)} %get-tuple-element.10, f32[8192]{0:T(1024)S(1)} %copy-done.5, f32[256]{0:T(256)S(1)} %add_rsqrt_fusion), kind=kOutput, calls=%fused_computation.14 | convolution fusion | flops 545292288 | bytes 6390784 | tf_op jit(solution)/shard_map/dot_general | solution.py:196
  71.1 0.6 copy-done.2
  71.7 1.0 copy-done.4
  72.7 1.5 %fusion.6 = bf16[256,128]{1,0:T(8,128)(2,1)S(1)} fusion(bf16[8192,128]{1,0:T(8,128)(2,1)S(1)} %copy-done.4, f32[128]{0:T(128)S(1)} %copy-done.7, bf16[256,8192]{1,0:T(8,128)(2,1)S(1)} %get-tuple-element.10, f32[8192]{0:T(1024)S(1)} %copy-done.5, f32[256]{0:T(256)S(1)} %add_rsqrt_fusion), kind=kOutput, calls=%fused_computation.13 | convolution fusion | flops 545325056 | bytes 6391296 | tf_op jit(solution)/shard_map/dot_general | solution.py:197
  74.2 0.7 pad_maximum_fusion.1
  74.8 0.0 all-gather.2.cloned.1.call-update
  74.9 0.0 copy-start.3
  74.9 12.4 %fusion.5.q_ref = bf16[256,1024]{1,0:T(8,128)(2,1)} fusion(bf16[8192,1024]{1,0:T(8,128)(2,1)} %param.17, f32[1024]{0:T(1024)S(1)} %copy-done.6, bf16[256,8192]{1,0:T(8,128)(2,1)} %copy-done.2, f32[8192]{0:T(1024)S(1)} %copy-done.5, f32[256]{0:T(256)S(1)} %add_rsqrt_fusion), kind=kOutput, calls=%fused_computation.11 | convolution fusion | flops 4303880192 | bytes 21533696 | tf_op jit(solution)/shard_map/dot_general | solution.py:193
  87.3 0.1 dynamic_slice.3
  87.4 0.6 slice.12
  88.0 1.3 convert_reduce_fusion
  91.5 0.8 copy.30.qdoc_ref
  92.3 0.7 pad_add_fusion.range_ref
  93.0 16.5 %all-gather.2.cloned.1.call-done.k_ref.v_ref = bf16[4096,256]{1,0:T(8,128)(2,1)} async-done(((bf16[256,256]{1,0:T(8,128)(2,1)}), bf16[4096,256]{1,0:T(8,128)(2,1)}) %all-gather.2.cloned.1.call-update) | async-done | bytes 2097168 | tf_op jit(solution)/shard_map/all_gather | solution.py:203
  109.5 18.1 %shard_map.110 = bf16[256,1024]{1,0:T(8,128)(2,1)} custom-call(s32[3]{0:T(128)} %pad_add_fusion.range_ref, bf16[256,1024]{1,0:T(8,128)(2,1)} %fusion.5.q_ref, bf16[4096,256]{1,0:T(8,128)(2,1)} %all-gather.2.cloned.1.call-done.k_ref.v_ref, bf16[4096,256]{1,0:T(8,128)(2,1)} %all-gather.2.cloned.1.call-done.k_ref.v_ref, s32[256,1]{1,0:T(8,128)} %copy.30.qdoc_ref, ...), custom_call_target="tpu_custom_call" | custom-call | flops 2147483648 | bytes 3145728 | tf_op jit(solution)/shard_map/pallas_call | solution.py:293
  (15 shorter events, 0.1 us)
Async XLA Ops:
  6.5 63.0 %copy-start = (bf16[8192,128]{1,0:T(8,128)(2,1)S(1)}, bf16[8192,128]{1,0:T(8,128)(2,1)}, u32[]{:S(2)}) copy-start(bf16[8192,128]{1,0:T(8,128)(2,1)} %param.19) | copy-start | bytes 6291460
  6.5 102.9 %all-gather.2.cloned.1.call-start = ((), (), s32[]{:S(2)}) async-start(), calls=%async_computation | async-start | bytes 2228224 | tf_op jit(solution)/shard_map/all_gather | solution.py:203
  63.5 3.8 %copy-start.1 = (bf16[256,8192]{1,0:T(8,128)(2,1)S(1)}, bf16[256,8192]{1,0:T(8,128)(2,1)}, u32[]{:S(2)}) copy-start(bf16[256,8192]{1,0:T(8,128)(2,1)} %param.11) | copy-start | bytes 12582916
  67.3 2.3 %copy-start.5 = (f32[8192]{0:T(1024)S(1)}, f32[8192]{0:T(1024)}, u32[]{:S(2)}) copy-start(f32[8192]{0:T(1024)} %param.16) | copy-start | bytes 98308
  69.6 2.1 %copy-start.2 = (bf16[256,8192]{1,0:T(8,128)(2,1)}, bf16[256,8192]{1,0:T(8,128)(2,1)S(1)}, u32[]{:S(2)}) copy-start(bf16[256,8192]{1,0:T(8,128)(2,1)S(1)} %get-tuple-element.10) | copy-start | bytes 12582916
  69.6 3.1 %copy-start.4 = (bf16[8192,128]{1,0:T(8,128)(2,1)S(1)}, bf16[8192,128]{1,0:T(8,128)(2,1)}, u32[]{:S(2)}) copy-start(bf16[8192,128]{1,0:T(8,128)(2,1)} %param.20) | copy-start | bytes 6291460
  69.6 3.1 %copy-start.7 = (f32[128]{0:T(128)S(1)}, f32[128]{0:T(128)}, u32[]{:S(2)}) copy-start(f32[128]{0:T(128)} %param.21) | copy-start | bytes 1540
  72.7 2.2 %copy-start.6 = (f32[1024]{0:T(1024)S(1)}, f32[1024]{0:T(1024)}, u32[]{:S(2)}) copy-start(f32[1024]{0:T(1024)} %param.18) | copy-start | bytes 12292
  74.9 12.4 %copy-start.3 = (s32[4096]{0:T(1024)S(1)}, s32[4096]{0:T(1024)}, u32[]{:S(2)}) copy-start(s32[4096]{0:T(1024)} %param.15) | copy-start | bytes 49156
Sparse Core Ops, SparseCore 0:
  75.0 34.4 all-gather.1

commit v11 on v10

--- a/solution.py
+++ b/solution.py
@@ -171,6 +171,105 @@
         ],
         compiler_params=pltpu.CompilerParams(collective_id=1, has_side_effects=True),
     )(payload)
+
+
+def gather_kernel(block_ref, out_ref, send_sem, recv_sem, local_sem):
+    rows = block_ref.shape[0]
+    me_seq = lax.axis_index("seq")
+    me_vis = lax.axis_index("vis")
+    column = me_seq // 4
+    layer = lax.rem(me_seq // 2, 2)
+    core = lax.rem(me_seq, 2)
+    ring = lax.axis_size("seq") // 4
+
+    def seq_of(y, z, c):
+        return (lax.rem(y + ring, ring) * 2 + z) * 2 + c
+
+    mate = seq_of(column, layer, 1 - core)
+    across = seq_of(column, 1 - layer, core)
+    diagonal = seq_of(column, 1 - layer, 1 - core)
+    up = seq_of(column + 1, layer, core)
+    down = seq_of(column - 1, layer, core)
+    barrier = pltpu.get_barrier_semaphore()
+    for peer in (mate, across, diagonal, up, down):
+        pl.semaphore_signal(
+            barrier, inc=1, device_id=(peer, me_vis), device_id_type=pl.DeviceIdType.MESH
+        )
+    pl.semaphore_wait(barrier, 5)
+
+    def rows_of(start, count):
+        return out_ref.at[pl.ds(pl.multiple_of(start, rows), count)]
+
+    def link(src, dst, peer, index):
+        return pltpu.make_async_remote_copy(
+            src_ref=src, dst_ref=dst, send_sem=send_sem.at[index], recv_sem=recv_sem.at[index],
+            device_id=(peer, me_vis), device_id_type=pl.DeviceIdType.MESH,
+        )
+
+    sent = []
+
+    def send(src, dst, peer, index):
+        copy = link(src, dst, peer, index)
+        copy.start()
+        sent.append(copy)
+
+    own = rows_of(me_seq * rows, rows)
+    local = pltpu.make_async_copy(block_ref, own, local_sem.at[0])
+    local.start()
+    send(block_ref, own, mate, 0)
+    send(block_ref, own, across, 1)
+    send(block_ref, own, diagonal, 2)
+    local.wait()
+    link(block_ref, rows_of(mate * rows, rows), mate, 0).wait_recv()
+    link(block_ref, rows_of(across * rows, rows), across, 1).wait_recv()
+    link(block_ref, rows_of(diagonal * rows, rows), diagonal, 2).wait_recv()
+
+    def half(y, h):
+        return rows_of((lax.rem(y + ring, ring) * 4 + h * 2) * rows, 2 * rows)
+
+    def quarter(y, h, q):
+        return rows_of((lax.rem(y + ring, ring) * 4 + h * 2 + q) * rows, rows)
+
+    mine = half(column, core)
+    send(mine, mine, up, 3)
+    send(mine, mine, down, 4)
+    below = half(column - 1, core)
+    link(below, below, down, 3).wait_recv()
+    send(below, below, mate, 7)
+    piece = quarter(column - 1, core, 0)
+    send(piece, piece, up, 5)
+    above = half(column + 1, core)
+    link(above, above, up, 4).wait_recv()
+    send(above, above, mate, 9)
+    piece = quarter(column + 1, core, 1)
+    send(piece, piece, down, 6)
+    far_low = quarter(column + 2, core, 0)
+    far_high = quarter(column + 2, core, 1)
+    link(far_low, far_low, down, 5).wait_recv()
+    link(far_high, far_high, up, 6).wait_recv()
+    far = half(column + 2, core)
+    send(far, far, mate, 8)
+    for offset, index in ((-1, 7), (2, 8), (1, 9)):
+        theirs = half(column + offset, 1 - core)
+        link(theirs, theirs, mate, index).wait_recv()
+    for copy in sent:
+        copy.wait_send()
+
+
+def gather_keys(block, seq_count):
+    rows, width = block.shape
+    return pl.pallas_call(
+        gather_kernel,
+        out_shape=jax.ShapeDtypeStruct((seq_count * rows, width), block.dtype),
+        in_specs=[pl.BlockSpec(memory_space=pl.ANY)],
+        out_specs=pl.BlockSpec(memory_space=pl.ANY),
+        scratch_shapes=[
+            pltpu.SemaphoreType.DMA((10,)),
+            pltpu.SemaphoreType.DMA((10,)),
+            pltpu.SemaphoreType.DMA((1,)),
+        ],
+        compiler_params=pltpu.CompilerParams(collective_id=2, has_side_effects=True),
+    )(block)
 
 
 def on_device(
@@ -200,7 +299,7 @@
     keyval = jnp.concatenate([key_rows, value_rows], axis=1)
     kv_heads = w_key.shape[1] // HEAD_DIM
     per_group = w_query.shape[1] // HEAD_DIM // kv_heads
-    incoming_keys = lax.all_gather(keyval, "seq", axis=0, tiled=True)
+    incoming_keys = gather_keys(keyval, seq_count)
     queries, doc_ids = lax.optimization_barrier((queries, doc_ids))
     own_docs = lax.dynamic_slice_in_dim(doc_ids, first_row, shard_rows)
     doc_start = jnp.sum((doc_ids < own_docs[0]).astype(jnp.int32))

time: 135 us -> 136 us (level)
  the two profiles are of different devices: /device:TPU:43 before, /device:TPU:17 now
where the time goes in v11:
time: 136 us; the launch traced here: 135 us
  Pallas kernels  100 us (74%)
  matrix products  20.6 us (15%)
  other arithmetic  6.74 us (5%)
  local copies, waits for them, and re-layouts  4.2 us (3%)
  between operations  3.7 us (3%)
    pallas_call x1, Pallas kernels, exchange_frames(): pl.pallas_call(exchange_kernel, out_shape=jax.ShapeDtypeStruct((vis_count...  53.6 us
    pallas_call x1, Pallas kernels, gather_keys(): pl.pallas_call(gather_kernel, out_shape=jax.ShapeDtypeStruct((seq_count *...  24.7 us
    pallas_call x1, Pallas kernels, flash_attention(): pl.pallas_call(flash_kernel, out_shape=jax.ShapeDtypeStruct((rows, width)...  21.8 us
    dot_general x1, matrix products, on_device(): jnp.dot(normed, w_query, preferred_element_type=jnp.float32) + q_bias  12.4 us
    dot_general x1, matrix products, place_frames(): lax.dot_general(lookup.astype(incoming.dtype), incoming, (((1, 2), (0, 1)...  3.68 us

profile of v11, /device:TPU:17, one launch (start us, length us, event | category | flops | bytes accessed | tf_op | source)
XLA Modules:
  0.0 135.3 jit_solution(4813761003334568024)
XLA Ops:
  0.0 0.0 copy-start
  0.8 0.7 multiply_subtract_fusion
  1.5 0.1 fusion.7
  1.6 0.1 select_reduce_fusion
  1.7 0.1 fusion.11
  1.8 0.1 broadcast_in_dim.27
  1.9 1.5 %convolution_convert_fusion = bf16[32,8192]{1,0:T(8,128)(2,1)S(1)} fusion(bf16[32,8192]{1,0:T(8,128)(2,1)} %param.12, s32[32]{0:T(128)S(1)} %multiply_add_fusion, pred[32]{0:T(512)(128)(4,1)S(1)} %iota_compare_fusion.7), kind=kOutput, calls=%fused_computation.3 | convolution fusion | flops 17041408 | bytes 1048736 | tf_op jit(solution)/shard_map/dot_general | solution.py:31
  3.4 1.0 reshape.40.payload_ref
  4.5 53.6 %shard_map.109 = bf16[128,2,8320]{2,1,0:T(2,128)(2,1)} custom-call(bf16[16,2,8320]{2,1,0:T(2,128)(2,1)} %reshape.40.payload_ref), custom_call_target="tpu_custom_call" | custom-call | tf_op jit(solution)/shard_map/pallas_call | solution.py:160
  58.0 0.9 slice_convert_fusion.1
  58.9 0.1 copy.26
  59.0 3.7 %convolution_bitcast_fusion = bf16[256,8320]{1,0:T(8,128)(2,1)S(1)} fusion(bf16[128,2,8320]{2,1,0:T(2,128)(2,1)} %shard_map.109, s32[128,2]{0,1:T(2,128)S(1)} %bitcast.17), kind=kOutput, calls=%fused_computation | convolution fusion | flops 1090584576 | bytes 8520704 | tf_op jit(solution)/shard_map/dot_general | solution.py:42
  62.7 0.1 fusion.8
  62.8 0.0 copy-start.5
  62.8 2.3 %fusion = (f32[256]{0:T(256)S(1)}, bf16[256,8192]{1,0:T(8,128)(2,1)S(1)}) fusion(bf16[256,8192]{1,0:T(8,128)(2,1)S(1)} %copy-done.1, bf16[256,8320]{1,0:T(8,128)(2,1)S(1)} %convolution_bitcast_fusion, pred[256]{0:T(512)(128)(4,1)S(1)} %fusion.8), kind=kLoop, calls=%fused_computation.4 | loop fusion | flops 8388352 | bytes 12584192 | tf_op jit(solution)/shard_map/reduce_sum | solution.py:290
  65.1 0.0 copy-start.2
  65.2 0.0 copy-start.4
  65.2 0.0 copy-start.7
  65.2 1.4 %convolution_convert_fusion.1 = bf16[256,128]{1,0:T(8,128)(2,1)S(1)} fusion(bf16[8192,128]{1,0:T(8,128)(2,1)S(1)} %copy-done, bf16[256,8192]{1,0:T(8,128)(2,1)S(1)} %get-tuple-element.10, f32[8192]{0:T(1024)S(1)} %copy-done.5, f32[256]{0:T(256)S(1)} %add_rsqrt_fusion), kind=kOutput, calls=%fused_computation.14 | convolution fusion | flops 545292288 | bytes 6390784 | tf_op jit(solution)/shard_map/dot_general | solution.py:295
  66.6 0.6 copy-done.2
  67.3 1.0 copy-done.4
  68.3 1.5 %fusion.6 = bf16[256,128]{1,0:T(8,128)(2,1)S(1)} fusion(bf16[8192,128]{1,0:T(8,128)(2,1)S(1)} %copy-done.4, f32[128]{0:T(128)S(1)} %copy-done.7, bf16[256,8192]{1,0:T(8,128)(2,1)S(1)} %get-tuple-element.10, f32[8192]{0:T(1024)S(1)} %copy-done.5, f32[256]{0:T(256)S(1)} %add_rsqrt_fusion), kind=kOutput, calls=%fused_computation.13 | convolution fusion | flops 545325056 | bytes 6391296 | tf_op jit(solution)/shard_map/dot_general | solution.py:296
  69.7 0.7 pad_maximum_fusion.1.block_ref
  70.4 24.7 %shard_map.110.k_ref.v_ref = bf16[4096,256]{1,0:T(8,128)(2,1)} custom-call(bf16[256,256]{1,0:T(8,128)(2,1)} %pad_maximum_fusion.1.block_ref), custom_call_target="tpu_custom_call" | custom-call | tf_op jit(solution)/shard_map/pallas_call | solution.py:261
  95.2 0.0 copy-start.3
  95.2 12.4 %fusion.5.q_ref = bf16[256,1024]{1,0:T(8,128)(2,1)} fusion(bf16[8192,1024]{1,0:T(8,128)(2,1)} %param.17, f32[1024]{0:T(1024)S(1)} %copy-done.6, bf16[256,8192]{1,0:T(8,128)(2,1)} %copy-done.2, f32[8192]{0:T(1024)S(1)} %copy-done.5, f32[256]{0:T(256)S(1)} %add_rsqrt_fusion), kind=kOutput, calls=%fused_computation.11 | convolution fusion | flops 4303880192 | bytes 21533696 | tf_op jit(solution)/shard_map/dot_general | solution.py:292
  107.6 0.1 dynamic_slice.3
  107.7 0.8 copy.30.qdoc_ref
  108.5 0.5 slice.12
  109.0 1.3 convert_reduce_fusion
  113.0 0.6 pad_add_fusion.range_ref
  113.5 21.8 %shard_map.111 = bf16[256,1024]{1,0:T(8,128)(2,1)} custom-call(s32[3]{0:T(128)} %pad_add_fusion.range_ref, bf16[256,1024]{1,0:T(8,128)(2,1)} %fusion.5.q_ref, bf16[4096,256]{1,0:T(8,128)(2,1)} %shard_map.110.k_ref.v_ref, bf16[4096,256]{1,0:T(8,128)(2,1)} %shard_map.110.k_ref.v_ref, s32[256,1]{1,0:T(8,128)} %copy.30.qdoc_ref, s32[1,4096]{1,0:T(1,128)} %bitcast.16), custom_call_target="tpu_custom_call" | custom-call | flops 2147483648 | bytes 3145728 | tf_op jit(solution)/shard_map/pallas_call | solution.py:392
  (13 shorter events, 0.1 us)
Async XLA Ops:
  0.0 65.2 %copy-start = (bf16[8192,128]{1,0:T(8,128)(2,1)S(1)}, bf16[8192,128]{1,0:T(8,128)(2,1)}, u32[]{:S(2)}) copy-start(bf16[8192,128]{1,0:T(8,128)(2,1)} %param.19) | copy-start | bytes 6291460
  59.0 3.8 %copy-start.1 = (bf16[256,8192]{1,0:T(8,128)(2,1)S(1)}, bf16[256,8192]{1,0:T(8,128)(2,1)}, u32[]{:S(2)}) copy-start(bf16[256,8192]{1,0:T(8,128)(2,1)} %param.11) | copy-start | bytes 12582916
  62.8 2.3 %copy-start.5 = (f32[8192]{0:T(1024)S(1)}, f32[8192]{0:T(1024)}, u32[]{:S(2)}) copy-start(f32[8192]{0:T(1024)} %param.16) | copy-start | bytes 98308
  65.1 2.1 %copy-start.2 = (bf16[256,8192]{1,0:T(8,128)(2,1)}, bf16[256,8192]{1,0:T(8,128)(2,1)S(1)}, u32[]{:S(2)}) copy-start(bf16[256,8192]{1,0:T(8,128)(2,1)S(1)} %get-tuple-element.10) | copy-start | bytes 12582916
  65.2 3.1 %copy-start.4 = (bf16[8192,128]{1,0:T(8,128)(2,1)S(1)}, bf16[8192,128]{1,0:T(8,128)(2,1)}, u32[]{:S(2)}) copy-start(bf16[8192,128]{1,0:T(8,128)(2,1)} %param.20) | copy-start | bytes 6291460
  65.2 3.1 %copy-start.7 = (f32[128]{0:T(128)S(1)}, f32[128]{0:T(128)}, u32[]{:S(2)}) copy-start(f32[128]{0:T(128)} %param.21) | copy-start | bytes 1540
  68.3 26.9 %copy-start.6 = (f32[1024]{0:T(1024)S(1)}, f32[1024]{0:T(1024)}, u32[]{:S(2)}) copy-start(f32[1024]{0:T(1024)} %param.18) | copy-start | bytes 12292
  95.2 12.4 %copy-start.3 = (s32[4096]{0:T(1024)S(1)}, s32[4096]{0:T(1024)}, u32[]{:S(2)}) copy-start(s32[4096]{0:T(1024)} %param.15) | copy-start | bytes 49156

commit v12 on v11

--- a/solution.py
+++ b/solution.py
@@ -173,7 +173,9 @@
     )(payload)
 
 
-def gather_kernel(block_ref, out_ref, send_sem, recv_sem, local_sem):
+def gather_kernel(
+    block_ref, normed_ref, w_ref, bias_ref, out_ref, q_ref, send_sem, recv_sem, local_sem, acc_ref
+):
     rows = block_ref.shape[0]
     me_seq = lax.axis_index("seq")
     me_vis = lax.axis_index("vis")
@@ -230,9 +232,26 @@
     def quarter(y, h, q):
         return rows_of((lax.rem(y + ring, ring) * 4 + h * 2 + q) * rows, rows)
 
+    depth = normed_ref.shape[1] // 2
+
+    def project(part):
+        def body(n_blk, w_blk):
+            acc_ref[...] += jnp.dot(n_blk[...], w_blk[...], preferred_element_type=jnp.float32)
+
+        pltpu.emit_pipeline(
+            body,
+            grid=(depth // PROJ_TILE,),
+            in_specs=[
+                pl.BlockSpec((normed_ref.shape[0], PROJ_TILE), lambda k: (0, k)),
+                pl.BlockSpec((PROJ_TILE, w_ref.shape[1]), lambda k: (k, 0)),
+            ],
+        )(normed_ref.at[:, pl.ds(part * depth, depth)], w_ref.at[pl.ds(part * depth, depth)])
+
+    acc_ref[...] = jnp.zeros(acc_ref.shape, jnp.float32)
     mine = half(column, core)
     send(mine, mine, up, 3)
     send(mine, mine, down, 4)
+    project(0)
     below = half(column - 1, core)
     link(below, below, down, 3).wait_recv()
     send(below, below, mate, 7)
@@ -243,6 +262,8 @@
     send(above, above, mate, 9)
     piece = quarter(column + 1, core, 1)
     send(piece, piece, down, 6)
+    project(1)
+    q_ref[...] = (acc_ref[...] + bias_ref[...]).astype(q_ref.dtype)
     far_low = quarter(column + 2, core, 0)
     far_high = quarter(column + 2, core, 1)
     link(far_low, far_low, down, 5).wait_recv()
@@ -256,20 +277,32 @@
         copy.wait_send()
 
 
-def gather_keys(block, seq_count):
+PROJ_TILE = 512
+
+
+def gather_keys(block, normed, w_query, q_bias, seq_count):
     rows, width = block.shape
     return pl.pallas_call(
         gather_kernel,
-        out_shape=jax.ShapeDtypeStruct((seq_count * rows, width), block.dtype),
-        in_specs=[pl.BlockSpec(memory_space=pl.ANY)],
-        out_specs=pl.BlockSpec(memory_space=pl.ANY),
+        out_shape=(
+            jax.ShapeDtypeStruct((seq_count * rows, width), block.dtype),
+            jax.ShapeDtypeStruct((normed.shape[0], w_query.shape[1]), jnp.bfloat16),
+        ),
+        in_specs=[
+            pl.BlockSpec(memory_space=pl.ANY),
+            pl.BlockSpec(memory_space=pl.ANY),
+            pl.BlockSpec(memory_space=pl.ANY),
+            pl.BlockSpec(memory_space=pltpu.VMEM),
+        ],
+        out_specs=(pl.BlockSpec(memory_space=pl.ANY), pl.BlockSpec(memory_space=pltpu.VMEM)),
         scratch_shapes=[
             pltpu.SemaphoreType.DMA((10,)),
             pltpu.SemaphoreType.DMA((10,)),
             pltpu.SemaphoreType.DMA((1,)),
+            pltpu.VMEM((normed.shape[0], w_query.shape[1]), jnp.float32),
         ],
         compiler_params=pltpu.CompilerParams(collective_id=2, has_side_effects=True),
-    )(block)
+    )(block, normed, w_query, q_bias.reshape(1, -1))
 
 
 def on_device(
@@ -289,9 +322,6 @@
     widened = merged.astype(jnp.float32)
     mean_square = jnp.mean(widened * widened, axis=1, keepdims=True)
     normed = (widened * lax.rsqrt(mean_square + epsilon) * norm_gain).astype(jnp.bfloat16)
-    queries = (jnp.dot(normed, w_query, preferred_element_type=jnp.float32) + q_bias).astype(
-        jnp.bfloat16
-    )
     key_rows = jnp.dot(normed, w_key, preferred_element_type=jnp.float32).astype(jnp.bfloat16)
     value_rows = (jnp.dot(normed, w_value, preferred_element_type=jnp.float32) + v_bias).astype(
         jnp.bfloat16
@@ -299,7 +329,7 @@
     keyval = jnp.concatenate([key_rows, value_rows], axis=1)
     kv_heads = w_key.shape[1] // HEAD_DIM
     per_group = w_query.shape[1] // HEAD_DIM // kv_heads
-    incoming_keys = gather_keys(keyval, seq_count)
+    incoming_keys, queries = gather_keys(keyval, normed, w_query, q_bias, seq_count)
     queries, doc_ids = lax.optimization_barrier((queries, doc_ids))
     own_docs = lax.dynamic_slice_in_dim(doc_ids, first_row, shard_rows)
     doc_start = jnp.sum((doc_ids < own_docs[0]).astype(jnp.int32))

time: 136 us -> 129 us (0.949)
  matrix products: 20.6 us -> 7.86 us
  Pallas kernels: 100 us -> 104 us
    dot_general x1 -> x0, matrix products: 12.4 us -> none  [on_device(): jnp.dot(normed, w_query, preferred_element_type=jnp.float32) + q_bias]
    pallas_call x1, Pallas kernels: 24.7 us -> 28.8 us  [gather_keys(): pl.pallas_call(gather_kernel, out_shape=(jax.ShapeDtypeStruct((seq_count...]
where the time goes in v12:
time: 129 us; the launch traced here: 128 us
  Pallas kernels  104 us (81%)
  other arithmetic  7.93 us (6%)
  matrix products  7.86 us (6%)
  local copies, waits for them, and re-layouts  4.36 us (3%)
  between operations  3.71 us (3%)
    pallas_call x1, Pallas kernels, exchange_frames(): pl.pallas_call(exchange_kernel, out_shape=jax.ShapeDtypeStruct((vis_count...  53.6 us
    pallas_call x1, Pallas kernels, gather_keys(): pl.pallas_call(gather_kernel, out_shape=(jax.ShapeDtypeStruct((seq_count...  28.8 us
    pallas_call x1, Pallas kernels, flash_attention(): pl.pallas_call(flash_kernel, out_shape=jax.ShapeDtypeStruct((rows, width)...  21.8 us
    dot_general x1, matrix products, place_frames(): lax.dot_general(lookup.astype(incoming.dtype), incoming, (((1, 2), (0, 1)...  3.68 us

profile of v12, /device:TPU:17, one launch (start us, length us, event | category | flops | bytes accessed | tf_op | source)
XLA Modules:
  0.0 128.0 jit_solution(9863838828786056416)
XLA Ops:
  0.0 0.0 copy-start
  0.8 0.7 multiply_subtract_fusion
  1.5 0.1 fusion.6
  1.6 0.1 select_reduce_fusion
  1.7 0.1 fusion.10
  1.8 0.1 broadcast_in_dim.27
  1.9 1.5 %convolution_convert_fusion = bf16[32,8192]{1,0:T(8,128)(2,1)S(1)} fusion(bf16[32,8192]{1,0:T(8,128)(2,1)} %param.12, s32[32]{0:T(128)S(1)} %multiply_add_fusion, pred[32]{0:T(512)(128)(4,1)S(1)} %iota_compare_fusion.7), kind=kOutput, calls=%fused_computation.3 | convolution fusion | flops 17041408 | bytes 1048736 | tf_op jit(solution)/shard_map/dot_general | solution.py:31
  3.4 1.0 reshape.42.payload_ref
  4.5 53.6 %shard_map.109 = bf16[128,2,8320]{2,1,0:T(2,128)(2,1)} custom-call(bf16[16,2,8320]{2,1,0:T(2,128)(2,1)} %reshape.42.payload_ref), custom_call_target="tpu_custom_call" | custom-call | tf_op jit(solution)/shard_map/pallas_call | solution.py:160
  58.0 0.9 slice_convert_fusion.1
  58.9 0.1 copy.26
  59.0 3.7 %convolution_bitcast_fusion = bf16[256,8320]{1,0:T(8,128)(2,1)S(1)} fusion(bf16[128,2,8320]{2,1,0:T(2,128)(2,1)} %shard_map.109, s32[128,2]{0,1:T(2,128)S(1)} %bitcast.19), kind=kOutput, calls=%fused_computation | convolution fusion | flops 1090584576 | bytes 8520704 | tf_op jit(solution)/shard_map/dot_general | solution.py:42
  62.7 0.1 fusion.7
  62.8 0.0 copy-done.2
  62.8 0.0 copy-start.4
  62.8 2.3 %fusion = (f32[256]{0:T(256)S(1)}, bf16[256,8192]{1,0:T(8,128)(2,1)S(1)}) fusion(bf16[256,8192]{1,0:T(8,128)(2,1)S(1)} %copy-done.2, bf16[256,8320]{1,0:T(8,128)(2,1)S(1)} %convolution_bitcast_fusion, pred[256]{0:T(512)(128)(4,1)S(1)} %fusion.7), kind=kLoop, calls=%fused_computation.4 | loop fusion | flops 8388352 | bytes 12584192 | tf_op jit(solution)/shard_map/reduce_sum | solution.py:323
  65.1 0.0 copy-done.4
  65.2 1.2 fusion.2.normed_ref
  66.4 0.0 copy-start.3
  66.4 0.0 copy-start.6
  66.4 1.3 %convolution_convert_fusion.1 = bf16[256,128]{1,0:T(8,128)(2,1)S(1)} fusion(bf16[256,8192]{1,0:T(8,128)(2,1)S(1)} %fusion.2.normed_ref, bf16[8192,128]{1,0:T(8,128)(2,1)S(1)} %copy-done), kind=kOutput, calls=%fused_computation.12 | convolution fusion | flops 536903680 | bytes 6356992 | tf_op jit(solution)/shard_map/dot_general | solution.py:325
  67.7 1.8 %copy-done.3 = bf16[8192,128]{1,0:T(8,128)(2,1)S(1)} copy-done((bf16[8192,128]{1,0:T(8,128)(2,1)S(1)}, bf16[8192,128]{1,0:T(8,128)(2,1)}, u32[]{:S(2)}) %copy-start.3) | copy-done | bytes 2097176
  69.5 1.3 %fusion.5 = bf16[256,128]{1,0:T(8,128)(2,1)S(1)} fusion(bf16[256,8192]{1,0:T(8,128)(2,1)S(1)} %fusion.2.normed_ref, bf16[8192,128]{1,0:T(8,128)(2,1)S(1)} %copy-done.3, f32[128]{0:T(128)S(1)} %copy-done.6), kind=kOutput, calls=%fused_computation.11 | convolution fusion | flops 536936448 | bytes 6357504 | tf_op jit(solution)/shard_map/dot_general | solution.py:326
  70.8 0.0 copy-done.1
  70.8 0.7 pad_maximum_fusion.1.block_ref
  71.4 28.8 %shard_map.110 = (bf16[4096,256]{1,0:T(8,128)(2,1)}, bf16[256,1024]{1,0:T(8,128)(2,1)}) custom-call(bf16[256,256]{1,0:T(8,128)(2,1)} %pad_maximum_fusion.1.block_ref, bf16[256,8192]{1,0:T(8,128)(2,1)} %copy-done.1, bf16[8192,1024]{1,0:T(8,128)(2,1)} %w_ref.1, f32[1,1024]{1,0:T(1,128)} %bitcast.22), custom_call_target="tpu_custom_call" | custom-call | tf_op jit(solution)/shard_map/pallas_call | solution.py:285
  100.3 0.1 dynamic_slice.3
  100.4 0.8 copy.30.qdoc_ref
  101.2 0.5 slice.12
  101.7 1.3 convert_reduce_fusion
  105.7 0.6 pad_add_fusion.range_ref
  106.3 21.8 %shard_map.111 = bf16[256,1024]{1,0:T(8,128)(2,1)} custom-call(s32[3]{0:T(128)} %pad_add_fusion.range_ref, bf16[256,1024]{1,0:T(8,128)(2,1)} %get-tuple-element.11.q_ref, bf16[4096,256]{1,0:T(8,128)(2,1)} %get-tuple-element.12.k_ref.v_ref, bf16[4096,256]{1,0:T(8,128)(2,1)} %get-tuple-element.12.k_ref.v_ref, s32[256,1]{1,0:T(8,128)} %copy.30.qdoc_ref, ...), custom_call_target="tpu_custom_call" | custom-call | flops 2147483648 | bytes 3145728 | tf_op jit(solution)/shard_map/pallas_call | solution.py:422
  (11 shorter events, 0.1 us)
Async XLA Ops:
  0.0 66.3 %copy-start = (bf16[8192,128]{1,0:T(8,128)(2,1)S(1)}, bf16[8192,128]{1,0:T(8,128)(2,1)}, u32[]{:S(2)}) copy-start(bf16[8192,128]{1,0:T(8,128)(2,1)} %param.19) | copy-start | bytes 6291460
  59.0 3.8 %copy-start.2 = (bf16[256,8192]{1,0:T(8,128)(2,1)S(1)}, bf16[256,8192]{1,0:T(8,128)(2,1)}, u32[]{:S(2)}) copy-start(bf16[256,8192]{1,0:T(8,128)(2,1)} %param.11) | copy-start | bytes 12582916
  62.8 2.3 %copy-start.4 = (f32[8192]{0:T(1024)S(1)}, f32[8192]{0:T(1024)}, u32[]{:S(2)}) copy-start(f32[8192]{0:T(1024)} %param.16) | copy-start | bytes 98308
  66.4 4.4 %copy-start.1 = (bf16[256,8192]{1,0:T(8,128)(2,1)}, bf16[256,8192]{1,0:T(8,128)(2,1)S(1)}, u32[]{:S(2)}) copy-start(bf16[256,8192]{1,0:T(8,128)(2,1)S(1)} %fusion.2.normed_ref) | copy-start | bytes 12582916
  66.4 3.1 %copy-start.3 = (bf16[8192,128]{1,0:T(8,128)(2,1)S(1)}, bf16[8192,128]{1,0:T(8,128)(2,1)}, u32[]{:S(2)}) copy-start(bf16[8192,128]{1,0:T(8,128)(2,1)} %param.20) | copy-start | bytes 6291460
  66.4 3.1 %copy-start.6 = (f32[128]{0:T(128)S(1)}, f32[128]{0:T(128)}, u32[]{:S(2)}) copy-start(f32[128]{0:T(128)} %param.21) | copy-start | bytes 1540
  71.4 28.8 %copy-start.5 = (s32[4096]{0:T(1024)S(1)}, s32[4096]{0:T(1024)}, u32[]{:S(2)}) copy-start(s32[4096]{0:T(1024)} %param.15) | copy-start | bytes 49156

commit v13 on v12

--- a/solution.py
+++ b/solution.py
@@ -330,37 +330,45 @@
     kv_heads = w_key.shape[1] // HEAD_DIM
     per_group = w_query.shape[1] // HEAD_DIM // kv_heads
     incoming_keys, queries = gather_keys(keyval, normed, w_query, q_bias, seq_count)
-    queries, doc_ids = lax.optimization_barrier((queries, doc_ids))
-    own_docs = lax.dynamic_slice_in_dim(doc_ids, first_row, shard_rows)
-    doc_start = jnp.sum((doc_ids < own_docs[0]).astype(jnp.int32))
-    last_row = first_row + shard_rows - 1
-    block_range = jnp.stack([doc_start // KEY_BLOCK, last_row // KEY_BLOCK, first_row]).astype(jnp.int32)
-    return flash_attention(block_range, queries, incoming_keys, own_docs, doc_ids, kv_heads)
+    return flash_attention(doc_ids, queries, incoming_keys)
 
 
 KEY_BLOCK = 512
 DOC_SPAN = 2048
 
 
-def flash_kernel(
-    range_ref, q_ref, k_ref, v_ref, qdoc_ref, kdoc_ref, out_ref, peak_ref, total_ref, acc_ref
-):
+def block_bounds(doc_ref, rows, key_rows):
+    first = lax.axis_index("seq") * rows
+    first_doc = doc_ref[first]
+    low = 0
+    for b in range(key_rows // KEY_BLOCK):
+        low = low + (doc_ref[(b + 1) * KEY_BLOCK - 1] < first_doc).astype(jnp.int32)
+    return low, (first + rows - 1) // KEY_BLOCK, first
+
+
+def flash_kernel(doc_ref, q_ref, k_ref, v_ref, qdoc_ref, kdoc_ref, out_ref, peak_ref, total_ref, acc_ref, qcol_ref):
     step = pl.program_id(0)
-    block = range_ref[0] + step
     rows = q_ref.shape[0]
     heads = q_ref.shape[1] // HEAD_DIM
+    low, high, first = block_bounds(doc_ref, rows, doc_ref.shape[0])
+    block = low + step
 
     @pl.when(step == 0)
     def _():
         peak_ref[...] = jnp.full(peak_ref.shape, negative, jnp.float32)
         total_ref[...] = jnp.zeros(total_ref.shape, jnp.float32)
         acc_ref[...] = jnp.zeros(acc_ref.shape, jnp.float32)
-
-    @pl.when(block <= range_ref[1])
+        spread = jnp.broadcast_to(qdoc_ref[...], (rows, rows))
+        diagonal = lax.broadcasted_iota(jnp.int32, (rows, rows), 0) == lax.broadcasted_iota(
+            jnp.int32, (rows, rows), 1
+        )
+        qcol_ref[...] = jnp.sum(jnp.where(diagonal, spread, 0), axis=1, keepdims=True)
+
+    @pl.when(block <= high)
     def _():
         key_place = block * KEY_BLOCK + lax.broadcasted_iota(jnp.int32, (1, KEY_BLOCK), 1)
-        query_place = range_ref[2] + lax.broadcasted_iota(jnp.int32, (rows, 1), 0)
-        allowed = (key_place <= query_place) & (kdoc_ref[...] == qdoc_ref[...])
+        query_place = first + lax.broadcasted_iota(jnp.int32, (rows, 1), 0)
+        allowed = (key_place <= query_place) & (kdoc_ref[...] == qcol_ref[...])
         keys = k_ref[...]
         vals = v_ref[...]
         for h in range(heads):
@@ -386,39 +394,36 @@
             out_ref[:, cols] = (acc_ref[:, cols] / total_ref[h][:, :1]).astype(out_ref.dtype)
 
 
-def flash_attention(block_range, queries, keyval, own_docs, doc_ids, kv_heads):
+def flash_attention(doc_ids, queries, keyval):
     rows, width = queries.shape
     key_rows = keyval.shape[0]
     steps = min(key_rows // KEY_BLOCK, (DOC_SPAN + rows - 2) // KEY_BLOCK + 2)
     heads = width // HEAD_DIM
 
-    def key_block(j, r):
-        return (jnp.minimum(r[0] + j, r[1]), 0)
-
-    def value_block(j, r):
-        return (jnp.minimum(r[0] + j, r[1]), 1)
-
-    def doc_block(j, r):
-        return (0, jnp.minimum(r[0] + j, r[1]))
+    def clamp(j, d):
+        low, high, _ = block_bounds(d, rows, key_rows)
+        return jnp.minimum(low + j, high)
 
     grid_spec = pltpu.PrefetchScalarGridSpec(
         num_scalar_prefetch=1,
         grid=(steps,),
         in_specs=[
-            pl.BlockSpec((rows, width), lambda j, r: (0, 0)),
-            pl.BlockSpec((KEY_BLOCK, HEAD_DIM), key_block),
-            pl.BlockSpec((KEY_BLOCK, HEAD_DIM), value_block),
-            pl.BlockSpec((rows, 1), lambda j, r: (0, 0)),
-            pl.BlockSpec((1, KEY_BLOCK), doc_block),
+            pl.BlockSpec((rows, width), lambda j, d: (0, 0)),
+            pl.BlockSpec((KEY_BLOCK, HEAD_DIM), lambda j, d: (clamp(j, d), 0)),
+            pl.BlockSpec((KEY_BLOCK, HEAD_DIM), lambda j, d: (clamp(j, d), 1)),
+            pl.BlockSpec((1, rows), lambda j, d: (0, lax.axis_index("seq"))),
+            pl.BlockSpec((1, KEY_BLOCK), lambda j, d: (0, clamp(j, d))),
         ],
-        out_specs=pl.BlockSpec((rows, width), lambda j, r: (0, 0)),
+        out_specs=pl.BlockSpec((rows, width), lambda j, d: (0, 0)),
         scratch_shapes=[
             pltpu.VMEM((heads, rows, 1), jnp.float32),
             pltpu.VMEM((heads, rows, 1), jnp.float32),
             pltpu.VMEM((rows, width), jnp.float32),
+            pltpu.VMEM((rows, 1), jnp.int32),
         ],
     )
     flops = 4 * rows * width * key_rows // 2
+    doc_row = doc_ids.reshape(1, -1)
     return pl.pallas_call(
         flash_kernel,
         out_shape=jax.ShapeDtypeStruct((rows, width), jnp.bfloat16),
@@ -428,7 +433,7 @@
             flops=flops, transcendentals=rows * heads * key_rows // 2,
             bytes_accessed=2 * (2 * rows * width + key_rows * 2 * HEAD_DIM),
         ),
-    )(block_range, queries, keyval, keyval, own_docs.reshape(rows, 1), doc_ids.reshape(1, -1))
+    )(doc_ids, queries, keyval, keyval, doc_row, doc_row)
 
 
 def solution(mesh):

time: 129 us -> 121 us (0.938)
  the two profiles are of different devices: /device:TPU:17 before, /device:TPU:57 now
where the time goes in v13:
time: 121 us; the launch traced here: 120 us
  Pallas kernels  102 us (84%)
  matrix products  7.84 us (6%)
  other arithmetic  6.1 us (5%)
  local copies, waits for them, and re-layouts  3 us (2%)
    pallas_call x1, Pallas kernels, exchange_frames(): pl.pallas_call(exchange_kernel, out_shape=jax.ShapeDtypeStruct((vis_count...  53.3 us
    pallas_call x1, Pallas kernels, gather_keys(): pl.pallas_call(gather_kernel, out_shape=(jax.ShapeDtypeStruct((seq_count...  29.6 us
    pallas_call x1, Pallas kernels, flash_attention(): pl.pallas_call(flash_kernel, out_shape=jax.ShapeDtypeStruct((rows, width)...  19.5 us
    dot_general x1, matrix products, place_frames(): lax.dot_general(lookup.astype(incoming.dtype), incoming, (((1, 2), (0, 1)...  3.67 us

profile of v13, /device:TPU:57, one launch (start us, length us, event | category | flops | bytes accessed | tf_op | source)
XLA Modules:
  0.0 120.3 jit_solution(11992822215609366422)
XLA Ops:
  0.0 0.0 copy-start
  0.8 0.7 multiply_subtract_fusion
  1.5 0.1 fusion.6
  1.6 0.1 select_reduce_fusion
  1.7 0.1 fusion.10
  1.8 0.1 broadcast_in_dim.27
  1.9 1.5 %convolution_convert_fusion = bf16[32,8192]{1,0:T(8,128)(2,1)S(1)} fusion(bf16[32,8192]{1,0:T(8,128)(2,1)} %param.12, s32[32]{0:T(128)S(1)} %multiply_add_fusion, pred[32]{0:T(512)(128)(4,1)S(1)} %iota_compare_fusion.7), kind=kOutput, calls=%fused_computation.3 | convolution fusion | flops 17041408 | bytes 1048736 | tf_op jit(solution)/shard_map/dot_general | solution.py:31
  3.4 1.0 reshape.39.payload_ref
  4.4 53.3 %shard_map.109 = bf16[128,2,8320]{2,1,0:T(2,128)(2,1)} custom-call(bf16[16,2,8320]{2,1,0:T(2,128)(2,1)} %reshape.39.payload_ref), custom_call_target="tpu_custom_call" | custom-call | tf_op jit(solution)/shard_map/pallas_call | solution.py:160
  57.8 0.9 slice_convert_fusion.1
  58.7 0.1 copy.24
  58.8 0.0 copy-start.2
  58.8 3.7 %convolution_bitcast_fusion = bf16[256,8320]{1,0:T(8,128)(2,1)S(1)} fusion(bf16[128,2,8320]{2,1,0:T(2,128)(2,1)} %shard_map.109, s32[128,2]{0,1:T(2,128)S(1)} %bitcast.13), kind=kOutput, calls=%fused_computation | convolution fusion | flops 1090584576 | bytes 8520704 | tf_op jit(solution)/shard_map/dot_general | solution.py:42
  62.5 0.1 fusion.7
  62.6 0.0 copy-done.2
  62.6 0.0 copy-start.4
  62.6 2.3 %fusion = (f32[256]{0:T(256)S(1)}, bf16[256,8192]{1,0:T(8,128)(2,1)S(1)}) fusion(bf16[256,8192]{1,0:T(8,128)(2,1)S(1)} %copy-done.2, bf16[256,8320]{1,0:T(8,128)(2,1)S(1)} %convolution_bitcast_fusion, pred[256]{0:T(512)(128)(4,1)S(1)} %fusion.7), kind=kLoop, calls=%fused_computation.4 | loop fusion | flops 8388352 | bytes 12584192 | tf_op jit(solution)/shard_map/reduce_sum | solution.py:323
  64.9 0.0 copy-done.4
  64.9 0.0 copy-start.5
  64.9 1.2 fusion.2.normed_ref
  66.1 0.0 copy-done
  66.1 0.0 copy-done.5
  66.1 0.0 copy-start.1
  66.1 0.0 copy-start.3
  66.2 1.3 %fusion.5 = bf16[256,128]{1,0:T(8,128)(2,1)S(1)} fusion(bf16[256,8192]{1,0:T(8,128)(2,1)S(1)} %fusion.2.normed_ref, bf16[8192,128]{1,0:T(8,128)(2,1)S(1)} %copy-done, f32[128]{0:T(128)S(1)} %copy-done.5), kind=kOutput, calls=%fused_computation.11 | convolution fusion | flops 536936448 | bytes 6357504 | tf_op jit(solution)/shard_map/dot_general | solution.py:326
  67.5 1.8 %copy-done.3 = bf16[8192,128]{1,0:T(8,128)(2,1)S(1)} copy-done((bf16[8192,128]{1,0:T(8,128)(2,1)S(1)}, bf16[8192,128]{1,0:T(8,128)(2,1)}, u32[]{:S(2)}) %copy-start.3) | copy-done | bytes 2097176
  69.2 1.3 %convolution_convert_fusion.1 = bf16[256,128]{1,0:T(8,128)(2,1)S(1)} fusion(bf16[256,8192]{1,0:T(8,128)(2,1)S(1)} %fusion.2.normed_ref, bf16[8192,128]{1,0:T(8,128)(2,1)S(1)} %copy-done.3), kind=kOutput, calls=%fused_computation.12 | convolution fusion | flops 536903680 | bytes 6356992 | tf_op jit(solution)/shard_map/dot_general | solution.py:325
  70.5 0.0 copy-done.1
  70.5 0.7 pad_maximum_fusion.1.block_ref
  71.2 29.6 %shard_map.110 = (bf16[4096,256]{1,0:T(8,128)(2,1)}, bf16[256,1024]{1,0:T(8,128)(2,1)}) custom-call(bf16[256,256]{1,0:T(8,128)(2,1)} %pad_maximum_fusion.1.block_ref, bf16[256,8192]{1,0:T(8,128)(2,1)} %copy-done.1, bf16[8192,1024]{1,0:T(8,128)(2,1)} %w_ref.1, f32[1,1024]{1,0:T(1,128)} %bitcast.15), custom_call_target="tpu_custom_call" | custom-call | tf_op jit(solution)/shard_map/pallas_call | solution.py:285
  100.8 19.5 %shard_map.111 = bf16[256,1024]{1,0:T(8,128)(2,1)} custom-call(s32[4096]{0:T(1024)} %doc_ref.1, bf16[256,1024]{1,0:T(8,128)(2,1)} %get-tuple-element.7.q_ref, bf16[4096,256]{1,0:T(8,128)(2,1)} %get-tuple-element.8.k_ref.v_ref, bf16[4096,256]{1,0:T(8,128)(2,1)} %get-tuple-element.8.k_ref.v_ref, s32[1,4096]{1,0:T(1,128)} %bitcast.16, s32[1,4096]{1,0:T(1,128)} %bitcast.17), custom_call_target="tpu_custom_call" | custom-call | flops 2147483648 | bytes 3145728 | tf_op jit(solution)/shard_map/pallas_call | solution.py:427
  (5 shorter events, 0.1 us)
Async XLA Ops:
  0.0 66.1 %copy-start = (bf16[8192,128]{1,0:T(8,128)(2,1)S(1)}, bf16[8192,128]{1,0:T(8,128)(2,1)}, u32[]{:S(2)}) copy-start(bf16[8192,128]{1,0:T(8,128)(2,1)} %param.20) | copy-start | bytes 6291460
  58.8 3.8 %copy-start.2 = (bf16[256,8192]{1,0:T(8,128)(2,1)S(1)}, bf16[256,8192]{1,0:T(8,128)(2,1)}, u32[]{:S(2)}) copy-start(bf16[256,8192]{1,0:T(8,128)(2,1)} %param.11) | copy-start | bytes 12582916
  62.6 2.3 %copy-start.4 = (f32[8192]{0:T(1024)S(1)}, f32[8192]{0:T(1024)}, u32[]{:S(2)}) copy-start(f32[8192]{0:T(1024)} %param.16) | copy-start | bytes 98308
  64.9 1.2 %copy-start.5 = (f32[128]{0:T(128)S(1)}, f32[128]{0:T(128)}, u32[]{:S(2)}) copy-start(f32[128]{0:T(128)} %param.21) | copy-start | bytes 1540
  66.1 4.4 %copy-start.1 = (bf16[256,8192]{1,0:T(8,128)(2,1)}, bf16[256,8192]{1,0:T(8,128)(2,1)S(1)}, u32[]{:S(2)}) copy-start(bf16[256,8192]{1,0:T(8,128)(2,1)S(1)} %fusion.2.normed_ref) | copy-start | bytes 12582916
  66.1 3.1 %copy-start.3 = (bf16[8192,128]{1,0:T(8,128)(2,1)S(1)}, bf16[8192,128]{1,0:T(8,128)(2,1)}, u32[]{:S(2)}) copy-start(bf16[8192,128]{1,0:T(8,128)(2,1)} %param.19) | copy-start | bytes 6291460

commit v14 on v13

--- a/solution.py
+++ b/solution.py
@@ -221,17 +221,6 @@
     send(block_ref, own, mate, 0)
     send(block_ref, own, across, 1)
     send(block_ref, own, diagonal, 2)
-    local.wait()
-    link(block_ref, rows_of(mate * rows, rows), mate, 0).wait_recv()
-    link(block_ref, rows_of(across * rows, rows), across, 1).wait_recv()
-    link(block_ref, rows_of(diagonal * rows, rows), diagonal, 2).wait_recv()
-
-    def half(y, h):
-        return rows_of((lax.rem(y + ring, ring) * 4 + h * 2) * rows, 2 * rows)
-
-    def quarter(y, h, q):
-        return rows_of((lax.rem(y + ring, ring) * 4 + h * 2 + q) * rows, rows)
-
     depth = normed_ref.shape[1] // 2
 
     def project(part):
@@ -248,10 +237,22 @@
         )(normed_ref.at[:, pl.ds(part * depth, depth)], w_ref.at[pl.ds(part * depth, depth)])
 
     acc_ref[...] = jnp.zeros(acc_ref.shape, jnp.float32)
+    project(0)
+    local.wait()
+    link(block_ref, rows_of(mate * rows, rows), mate, 0).wait_recv()
+    link(block_ref, rows_of(across * rows, rows), across, 1).wait_recv()
+    link(block_ref, rows_of(diagonal * rows, rows), diagonal, 2).wait_recv()
+
+    def half(y, h):
+        return rows_of((lax.rem(y + ring, ring) * 4 + h * 2) * rows, 2 * rows)
+
+    def quarter(y, h, q):
+        return rows_of((lax.rem(y + ring, ring) * 4 + h * 2 + q) * rows, rows)
+
     mine = half(column, core)
     send(mine, mine, up, 3)
     send(mine, mine, down, 4)
-    project(0)
+    project(1)
     below = half(column - 1, core)
     link(below, below, down, 3).wait_recv()
     send(below, below, mate, 7)
@@ -262,7 +263,6 @@
     send(above, above, mate, 9)
     piece = quarter(column + 1, core, 1)
     send(piece, piece, down, 6)
-    project(1)
     q_ref[...] = (acc_ref[...] + bias_ref[...]).astype(q_ref.dtype)
     far_low = quarter(column + 2, core, 0)
     far_high = quarter(column + 2, core, 1)

time: 121 us -> 123 us (1.017)
  the two profiles are of different devices: /device:TPU:57 before, /device:TPU:25 now
where the time goes in v14:
time: 123 us; the launch traced here: 122 us
  Pallas kernels  104 us (85%)
  matrix products  7.85 us (6%)
  other arithmetic  6.1 us (5%)
  local copies, waits for them, and re-layouts  3 us (2%)
    pallas_call x1, Pallas kernels, exchange_frames(): pl.pallas_call(exchange_kernel, out_shape=jax.ShapeDtypeStruct((vis_count...  53.4 us
    pallas_call x1, Pallas kernels, gather_keys(): pl.pallas_call(gather_kernel, out_shape=(jax.ShapeDtypeStruct((seq_count...  27.7 us
    pallas_call x1, Pallas kernels, flash_attention(): pl.pallas_call(flash_kernel, out_shape=jax.ShapeDtypeStruct((rows, width)...  23.2 us
    dot_general x1, matrix products, place_frames(): lax.dot_general(lookup.astype(incoming.dtype), incoming, (((1, 2), (0, 1)...  3.67 us

profile of v14, /device:TPU:25, one launch (start us, length us, event | category | flops | bytes accessed | tf_op | source)
XLA Modules:
  0.0 122.3 jit_solution(7425635547598290219)
XLA Ops:
  0.0 0.0 copy-start
  0.8 0.7 multiply_subtract_fusion
  1.5 0.1 fusion.6
  1.6 0.1 select_reduce_fusion
  1.7 0.1 fusion.10
  1.8 0.1 broadcast_in_dim.27
  1.9 1.5 %convolution_convert_fusion = bf16[32,8192]{1,0:T(8,128)(2,1)S(1)} fusion(bf16[32,8192]{1,0:T(8,128)(2,1)} %param.12, s32[32]{0:T(128)S(1)} %multiply_add_fusion, pred[32]{0:T(512)(128)(4,1)S(1)} %iota_compare_fusion.7), kind=kOutput, calls=%fused_computation.3 | convolution fusion | flops 17041408 | bytes 1048736 | tf_op jit(solution)/shard_map/dot_general | solution.py:31
  3.4 1.0 reshape.39.payload_ref
  4.5 53.4 %shard_map.109 = bf16[128,2,8320]{2,1,0:T(2,128)(2,1)} custom-call(bf16[16,2,8320]{2,1,0:T(2,128)(2,1)} %reshape.39.payload_ref), custom_call_target="tpu_custom_call" | custom-call | tf_op jit(solution)/shard_map/pallas_call | solution.py:160
  57.9 0.9 slice_convert_fusion.1
  58.8 0.1 copy.24
  58.9 0.0 copy-start.2
  58.9 3.7 %convolution_bitcast_fusion = bf16[256,8320]{1,0:T(8,128)(2,1)S(1)} fusion(bf16[128,2,8320]{2,1,0:T(2,128)(2,1)} %shard_map.109, s32[128,2]{0,1:T(2,128)S(1)} %bitcast.13), kind=kOutput, calls=%fused_computation | convolution fusion | flops 1090584576 | bytes 8520704 | tf_op jit(solution)/shard_map/dot_general | solution.py:42
  62.5 0.1 fusion.7
  62.7 0.0 copy-done.2
  62.7 0.0 copy-start.4
  62.7 2.3 %fusion = (f32[256]{0:T(256)S(1)}, bf16[256,8192]{1,0:T(8,128)(2,1)S(1)}) fusion(bf16[256,8192]{1,0:T(8,128)(2,1)S(1)} %copy-done.2, bf16[256,8320]{1,0:T(8,128)(2,1)S(1)} %convolution_bitcast_fusion, pred[256]{0:T(512)(128)(4,1)S(1)} %fusion.7), kind=kLoop, calls=%fused_computation.4 | loop fusion | flops 8388352 | bytes 12584192 | tf_op jit(solution)/shard_map/reduce_sum | solution.py:323
  65.0 0.0 copy-done.4
  65.0 0.0 copy-start.5
  65.0 1.2 fusion.2.normed_ref
  66.2 0.0 copy-done
  66.2 0.0 copy-done.5
  66.2 0.0 copy-start.1
  66.2 0.0 copy-start.3
  66.2 1.3 %fusion.5 = bf16[256,128]{1,0:T(8,128)(2,1)S(1)} fusion(bf16[256,8192]{1,0:T(8,128)(2,1)S(1)} %fusion.2.normed_ref, bf16[8192,128]{1,0:T(8,128)(2,1)S(1)} %copy-done, f32[128]{0:T(128)S(1)} %copy-done.5), kind=kOutput, calls=%fused_computation.11 | convolution fusion | flops 536936448 | bytes 6357504 | tf_op jit(solution)/shard_map/dot_general | solution.py:326
  67.5 1.8 %copy-done.3 = bf16[8192,128]{1,0:T(8,128)(2,1)S(1)} copy-done((bf16[8192,128]{1,0:T(8,128)(2,1)S(1)}, bf16[8192,128]{1,0:T(8,128)(2,1)}, u32[]{:S(2)}) %copy-start.3) | copy-done | bytes 2097176
  69.3 1.3 %convolution_convert_fusion.1 = bf16[256,128]{1,0:T(8,128)(2,1)S(1)} fusion(bf16[256,8192]{1,0:T(8,128)(2,1)S(1)} %fusion.2.normed_ref, bf16[8192,128]{1,0:T(8,128)(2,1)S(1)} %copy-done.3), kind=kOutput, calls=%fused_computation.12 | convolution fusion | flops 536903680 | bytes 6356992 | tf_op jit(solution)/shard_map/dot_general | solution.py:325
  70.6 0.0 copy-done.1
  70.6 0.7 pad_maximum_fusion.1.block_ref
  71.3 27.7 %shard_map.110 = (bf16[4096,256]{1,0:T(8,128)(2,1)}, bf16[256,1024]{1,0:T(8,128)(2,1)}) custom-call(bf16[256,256]{1,0:T(8,128)(2,1)} %pad_maximum_fusion.1.block_ref, bf16[256,8192]{1,0:T(8,128)(2,1)} %copy-done.1, bf16[8192,1024]{1,0:T(8,128)(2,1)} %w_ref.1, f32[1,1024]{1,0:T(1,128)} %bitcast.15), custom_call_target="tpu_custom_call" | custom-call | tf_op jit(solution)/shard_map/pallas_call | solution.py:285
  99.1 23.2 %shard_map.111 = bf16[256,1024]{1,0:T(8,128)(2,1)} custom-call(s32[4096]{0:T(1024)} %doc_ref.1, bf16[256,1024]{1,0:T(8,128)(2,1)} %get-tuple-element.7.q_ref, bf16[4096,256]{1,0:T(8,128)(2,1)} %get-tuple-element.8.k_ref.v_ref, bf16[4096,256]{1,0:T(8,128)(2,1)} %get-tuple-element.8.k_ref.v_ref, s32[1,4096]{1,0:T(1,128)} %bitcast.16, s32[1,4096]{1,0:T(1,128)} %bitcast.17), custom_call_target="tpu_custom_call" | custom-call | flops 2147483648 | bytes 3145728 | tf_op jit(solution)/shard_map/pallas_call | solution.py:427
  (5 shorter events, 0.1 us)
Async XLA Ops:
  0.0 66.2 %copy-start = (bf16[8192,128]{1,0:T(8,128)(2,1)S(1)}, bf16[8192,128]{1,0:T(8,128)(2,1)}, u32[]{:S(2)}) copy-start(bf16[8192,128]{1,0:T(8,128)(2,1)} %param.20) | copy-start | bytes 6291460
  58.9 3.8 %copy-start.2 = (bf16[256,8192]{1,0:T(8,128)(2,1)S(1)}, bf16[256,8192]{1,0:T(8,128)(2,1)}, u32[]{:S(2)}) copy-start(bf16[256,8192]{1,0:T(8,128)(2,1)} %param.11) | copy-start | bytes 12582916
  62.7 2.3 %copy-start.4 = (f32[8192]{0:T(1024)S(1)}, f32[8192]{0:T(1024)}, u32[]{:S(2)}) copy-start(f32[8192]{0:T(1024)} %param.16) | copy-start | bytes 98308
  65.0 1.2 copy-start.5
  66.2 4.4 %copy-start.1 = (bf16[256,8192]{1,0:T(8,128)(2,1)}, bf16[256,8192]{1,0:T(8,128)(2,1)S(1)}, u32[]{:S(2)}) copy-start(bf16[256,8192]{1,0:T(8,128)(2,1)S(1)} %fusion.2.normed_ref) | copy-start | bytes 12582916
  66.2 3.1 %copy-start.3 = (bf16[8192,128]{1,0:T(8,128)(2,1)S(1)}, bf16[8192,128]{1,0:T(8,128)(2,1)}, u32[]{:S(2)}) copy-start(bf16[8192,128]{1,0:T(8,128)(2,1)} %param.19) | copy-start | bytes 6291460

commit v15 on v14

--- a/solution.py
+++ b/solution.py
@@ -136,13 +136,13 @@
     send(me_vis, 0, right, 1)
     send(me_vis, 0, left, 2)
     send(me_vis, 0, partner, 3)
-    link(partner, 0, partner, 3).wait_recv()
-    send(partner, 0, right, 4)
-    send(partner, 0, left, 5)
     link(left, 0, left, 1).wait_recv()
     send(left, 1, right, 6)
     link(right, 0, right, 2).wait_recv()
     send(right, 2, left, 7)
+    link(partner, 0, partner, 3).wait_recv()
+    send(partner, 0, right, 4)
+    send(partner, 0, left, 5)
     link(left_partner, 0, left, 4).wait_recv()
     send(left_partner, 1, right, 8)
     link(right_partner, 0, right, 5).wait_recv()

time: 123 us -> 118 us (0.959)
  the two profiles are of different devices: /device:TPU:25 before, /device:TPU:57 now
where the time goes in v15:
time: 118 us; the launch traced here: 117 us
  Pallas kernels  98.9 us (84%)
  matrix products  7.84 us (7%)
  other arithmetic  6.1 us (5%)
  local copies, waits for them, and re-layouts  3 us (3%)
    pallas_call x1, Pallas kernels, exchange_frames(): pl.pallas_call(exchange_kernel, out_shape=jax.ShapeDtypeStruct((vis_count...  52.1 us
    pallas_call x1, Pallas kernels, gather_keys(): pl.pallas_call(gather_kernel, out_shape=(jax.ShapeDtypeStruct((seq_count...  27.2 us
    pallas_call x1, Pallas kernels, flash_attention(): pl.pallas_call(flash_kernel, out_shape=jax.ShapeDtypeStruct((rows, width)...  19.6 us
    dot_general x1, matrix products, place_frames(): lax.dot_general(lookup.astype(incoming.dtype), incoming, (((1, 2), (0, 1)...  3.67 us

profile of v15, /device:TPU:57, one launch (start us, length us, event | category | flops | bytes accessed | tf_op | source)
XLA Modules:
  0.0 116.8 jit_solution(18247128406509883351)
XLA Ops:
  0.0 0.0 copy-start
  0.8 0.7 multiply_subtract_fusion
  1.5 0.1 fusion.6
  1.6 0.1 select_reduce_fusion
  1.7 0.1 fusion.10
  1.8 0.1 broadcast_in_dim.27
  1.9 1.5 %convolution_convert_fusion = bf16[32,8192]{1,0:T(8,128)(2,1)S(1)} fusion(bf16[32,8192]{1,0:T(8,128)(2,1)} %param.12, s32[32]{0:T(128)S(1)} %multiply_add_fusion, pred[32]{0:T(512)(128)(4,1)S(1)} %iota_compare_fusion.7), kind=kOutput, calls=%fused_computation.3 | convolution fusion | flops 17041408 | bytes 1048736 | tf_op jit(solution)/shard_map/dot_general | solution.py:31
  3.4 1.0 reshape.39.payload_ref
  4.4 52.1 %shard_map.109 = bf16[128,2,8320]{2,1,0:T(2,128)(2,1)} custom-call(bf16[16,2,8320]{2,1,0:T(2,128)(2,1)} %reshape.39.payload_ref), custom_call_target="tpu_custom_call" | custom-call | tf_op jit(solution)/shard_map/pallas_call | solution.py:160
  56.6 0.9 slice_convert_fusion.1
  57.5 0.1 copy.24
  57.6 0.0 copy-start.2
  57.6 3.7 %convolution_bitcast_fusion = bf16[256,8320]{1,0:T(8,128)(2,1)S(1)} fusion(bf16[128,2,8320]{2,1,0:T(2,128)(2,1)} %shard_map.109, s32[128,2]{0,1:T(2,128)S(1)} %bitcast.13), kind=kOutput, calls=%fused_computation | convolution fusion | flops 1090584576 | bytes 8520704 | tf_op jit(solution)/shard_map/dot_general | solution.py:42
  61.2 0.1 fusion.7
  61.4 0.0 copy-done.2
  61.4 0.0 copy-start.4
  61.4 2.3 %fusion = (f32[256]{0:T(256)S(1)}, bf16[256,8192]{1,0:T(8,128)(2,1)S(1)}) fusion(bf16[256,8192]{1,0:T(8,128)(2,1)S(1)} %copy-done.2, bf16[256,8320]{1,0:T(8,128)(2,1)S(1)} %convolution_bitcast_fusion, pred[256]{0:T(512)(128)(4,1)S(1)} %fusion.7), kind=kLoop, calls=%fused_computation.4 | loop fusion | flops 8388352 | bytes 12584192 | tf_op jit(solution)/shard_map/reduce_sum | solution.py:323
  63.7 0.0 copy-done.4
  63.7 0.0 copy-start.5
  63.7 1.2 %fusion.2.normed_ref = bf16[256,8192]{1,0:T(8,128)(2,1)S(1)} fusion(bf16[256,8192]{1,0:T(8,128)(2,1)S(1)} %get-tuple-element.10, f32[8192]{0:T(1024)S(1)} %copy-done.4, f32[256]{0:T(256)S(1)} %add_rsqrt_fusion), kind=kLoop, calls=%fused_computation.6 | loop fusion | flops 8388608 | bytes 8422400 | tf_op jit(solution)/shard_map/convert_element_type | solution.py:324
  64.9 0.0 copy-done
  64.9 0.0 copy-done.5
  64.9 0.0 copy-start.1
  64.9 0.0 copy-start.3
  64.9 1.3 %fusion.5 = bf16[256,128]{1,0:T(8,128)(2,1)S(1)} fusion(bf16[256,8192]{1,0:T(8,128)(2,1)S(1)} %fusion.2.normed_ref, bf16[8192,128]{1,0:T(8,128)(2,1)S(1)} %copy-done, f32[128]{0:T(128)S(1)} %copy-done.5), kind=kOutput, calls=%fused_computation.11 | convolution fusion | flops 536936448 | bytes 6357504 | tf_op jit(solution)/shard_map/dot_general | solution.py:326
  66.2 1.8 %copy-done.3 = bf16[8192,128]{1,0:T(8,128)(2,1)S(1)} copy-done((bf16[8192,128]{1,0:T(8,128)(2,1)S(1)}, bf16[8192,128]{1,0:T(8,128)(2,1)}, u32[]{:S(2)}) %copy-start.3) | copy-done | bytes 2097176
  68.0 1.3 %convolution_convert_fusion.1 = bf16[256,128]{1,0:T(8,128)(2,1)S(1)} fusion(bf16[256,8192]{1,0:T(8,128)(2,1)S(1)} %fusion.2.normed_ref, bf16[8192,128]{1,0:T(8,128)(2,1)S(1)} %copy-done.3), kind=kOutput, calls=%fused_computation.12 | convolution fusion | flops 536903680 | bytes 6356992 | tf_op jit(solution)/shard_map/dot_general | solution.py:325
  69.3 0.0 copy-done.1
  69.3 0.7 pad_maximum_fusion.1.block_ref
  70.0 27.2 %shard_map.110 = (bf16[4096,256]{1,0:T(8,128)(2,1)}, bf16[256,1024]{1,0:T(8,128)(2,1)}) custom-call(bf16[256,256]{1,0:T(8,128)(2,1)} %pad_maximum_fusion.1.block_ref, bf16[256,8192]{1,0:T(8,128)(2,1)} %copy-done.1, bf16[8192,1024]{1,0:T(8,128)(2,1)} %w_ref.1, f32[1,1024]{1,0:T(1,128)} %bitcast.15), custom_call_target="tpu_custom_call" | custom-call | tf_op jit(solution)/shard_map/pallas_call | solution.py:285
  97.2 19.6 %shard_map.111 = bf16[256,1024]{1,0:T(8,128)(2,1)} custom-call(s32[4096]{0:T(1024)} %doc_ref.1, bf16[256,1024]{1,0:T(8,128)(2,1)} %get-tuple-element.7.q_ref, bf16[4096,256]{1,0:T(8,128)(2,1)} %get-tuple-element.8.k_ref.v_ref, bf16[4096,256]{1,0:T(8,128)(2,1)} %get-tuple-element.8.k_ref.v_ref, s32[1,4096]{1,0:T(1,128)} %bitcast.16, s32[1,4096]{1,0:T(1,128)} %bitcast.17), custom_call_target="tpu_custom_call" | custom-call | flops 2147483648 | bytes 3145728 | tf_op jit(solution)/shard_map/pallas_call | solution.py:427
  (5 shorter events, 0.1 us)
Async XLA Ops:
  0.0 64.9 %copy-start = (bf16[8192,128]{1,0:T(8,128)(2,1)S(1)}, bf16[8192,128]{1,0:T(8,128)(2,1)}, u32[]{:S(2)}) copy-start(bf16[8192,128]{1,0:T(8,128)(2,1)} %param.20) | copy-start | bytes 6291460
  57.6 3.8 %copy-start.2 = (bf16[256,8192]{1,0:T(8,128)(2,1)S(1)}, bf16[256,8192]{1,0:T(8,128)(2,1)}, u32[]{:S(2)}) copy-start(bf16[256,8192]{1,0:T(8,128)(2,1)} %param.11) | copy-start | bytes 12582916
  61.4 2.3 %copy-start.4 = (f32[8192]{0:T(1024)S(1)}, f32[8192]{0:T(1024)}, u32[]{:S(2)}) copy-start(f32[8192]{0:T(1024)} %param.16) | copy-start | bytes 98308
  63.7 1.2 %copy-start.5 = (f32[128]{0:T(128)S(1)}, f32[128]{0:T(128)}, u32[]{:S(2)}) copy-start(f32[128]{0:T(128)} %param.21) | copy-start | bytes 1540
  64.9 4.4 %copy-start.1 = (bf16[256,8192]{1,0:T(8,128)(2,1)}, bf16[256,8192]{1,0:T(8,128)(2,1)S(1)}, u32[]{:S(2)}) copy-start(bf16[256,8192]{1,0:T(8,128)(2,1)S(1)} %fusion.2.normed_ref) | copy-start | bytes 12582916
  64.9 3.1 %copy-start.3 = (bf16[8192,128]{1,0:T(8,128)(2,1)S(1)}, bf16[8192,128]{1,0:T(8,128)(2,1)}, u32[]{:S(2)}) copy-start(bf16[8192,128]{1,0:T(8,128)(2,1)} %param.19) | copy-start | bytes 6291460

commit v16 on v14

--- a/solution.py
+++ b/solution.py
@@ -46,7 +46,7 @@
     return jnp.where(covered[:, None], placed, text)
 
 
-def exchange_kernel(payload_ref, out_ref, send_a, recv_a, send_b, recv_b, local_sem):
+def exchange_kernel(payload_ref, out_ref, send_a, recv_a, send_b, recv_b, local_sem, relay):
     seq_count = lax.axis_size("seq")
     vis_count = lax.axis_size("vis")
     ring = vis_count // 2
@@ -61,6 +61,10 @@
     right = vis_of(ring_id, ring_pos + 1)
     left = vis_of(ring_id, ring_pos - 1)
     partner = vis_of(1 - ring_id, ring_pos)
+    level = lax.rem(me_seq // 2, 2)
+    flip = me_seq + 2 - 4 * level
+    lower = (flip, jnp.where(level == 1, me_vis, partner))
+    upper = (flip, jnp.where(level == 0, me_vis, partner))
     barrier = pltpu.get_barrier_semaphore()
     for k in range(1, seq_count):
         pl.semaphore_signal(
@@ -71,7 +75,9 @@
         pl.semaphore_signal(
             barrier, inc=1, device_id=(me_seq, peer), device_id_type=pl.DeviceIdType.MESH
         )
-    pl.semaphore_wait(barrier, seq_count + 2)
+    for device in (lower, upper):
+        pl.semaphore_signal(barrier, inc=1, device_id=device, device_id_type=pl.DeviceIdType.MESH)
+    pl.semaphore_wait(barrier, seq_count + 4)
     base = me_vis * seq_count
     local = pltpu.make_async_copy(payload_ref.at[me_seq], out_ref.at[base + me_seq], local_sem.at[0])
     local.start()
@@ -133,10 +139,29 @@
         copy.start()
         sent.append(copy)
 
+    def hop(src, dst, device, index):
+        return pltpu.make_async_remote_copy(
+            src_ref=src, dst_ref=dst, send_sem=send_b.at[index], recv_sem=recv_b.at[index],
+            device_id=device, device_id_type=pl.DeviceIdType.MESH,
+        )
+
+    def push(src, dst, device, index):
+        copy = hop(src, dst, device, index)
+        copy.start()
+        sent.append(copy)
+
     send(me_vis, 0, right, 1)
     send(me_vis, 0, left, 2)
-    send(me_vis, 0, partner, 3)
-    link(partner, 0, partner, 3).wait_recv()
+    push(region(me_vis, 1), relay.at[0], upper, 10)
+    push(region(me_vis, 2), relay.at[1], lower, 11)
+    hop(region(me_vis, 1), relay.at[0], lower, 10).wait_recv()
+    lower_vis = lower[1]
+    upper_vis = upper[1]
+    push(relay.at[0], region(lower_vis, 1), upper, 12)
+    hop(region(me_vis, 2), relay.at[1], upper, 11).wait_recv()
+    push(relay.at[1], region(upper_vis, 2), lower, 13)
+    hop(relay.at[0], region(partner, 1), lower, 12).wait_recv()
+    hop(relay.at[1], region(partner, 2), upper, 13).wait_recv()
     send(partner, 0, right, 4)
     send(partner, 0, left, 5)
     link(left, 0, left, 1).wait_recv()
@@ -165,9 +190,10 @@
         scratch_shapes=[
             pltpu.SemaphoreType.DMA((owners,)),
             pltpu.SemaphoreType.DMA((owners,)),
-            pltpu.SemaphoreType.DMA((10,)),
-            pltpu.SemaphoreType.DMA((10,)),
+            pltpu.SemaphoreType.DMA((14,)),
+            pltpu.SemaphoreType.DMA((14,)),
             pltpu.SemaphoreType.DMA((1,)),
+            pltpu.VMEM((2, owners // 2, capacity, width), payload.dtype),
         ],
         compiler_params=pltpu.CompilerParams(collective_id=1, has_side_effects=True),
     )(payload)

time: 123 us -> 124 us (level)
  the two profiles are of different devices: /device:TPU:25 before, /device:TPU:17 now
where the time goes in v16:
time: 124 us
  Pallas kernels  106 us (85%)
  matrix products  7.86 us (6%)
  other arithmetic  6.1 us (5%)
  local copies, waits for them, and re-layouts  3 us (2%)
    pallas_call x1, Pallas kernels, exchange_frames(): pl.pallas_call(exchange_kernel, out_shape=jax.ShapeDtypeStruct((vis_count...  54 us
    pallas_call x1, Pallas kernels, gather_keys(): pl.pallas_call(gather_kernel, out_shape=(jax.ShapeDtypeStruct((seq_count...  28.4 us
    pallas_call x1, Pallas kernels, flash_attention(): pl.pallas_call(flash_kernel, out_shape=jax.ShapeDtypeStruct((rows, width)...  23.2 us
    dot_general x1, matrix products, place_frames(): lax.dot_general(lookup.astype(incoming.dtype), incoming, (((1, 2), (0, 1)...  3.68 us

profile of v16, /device:TPU:17, one launch (start us, length us, event | category | flops | bytes accessed | tf_op | source)
XLA Modules:
  0.0 123.5 jit_solution(5706089297313427470)
XLA Ops:
  0.0 0.0 copy-start
  0.8 0.7 multiply_subtract_fusion
  1.5 0.1 fusion.6
  1.6 0.1 select_reduce_fusion
  1.7 0.1 fusion.10
  1.8 0.1 broadcast_in_dim.27
  1.9 1.5 %convolution_convert_fusion = bf16[32,8192]{1,0:T(8,128)(2,1)S(1)} fusion(bf16[32,8192]{1,0:T(8,128)(2,1)} %param.12, s32[32]{0:T(128)S(1)} %multiply_add_fusion, pred[32]{0:T(512)(128)(4,1)S(1)} %iota_compare_fusion.7), kind=kOutput, calls=%fused_computation.3 | convolution fusion | flops 17041408 | bytes 1048736 | tf_op jit(solution)/shard_map/dot_general | solution.py:31
  3.4 1.0 reshape.39.payload_ref
  4.5 54.0 %shard_map.109 = bf16[128,2,8320]{2,1,0:T(2,128)(2,1)} custom-call(bf16[16,2,8320]{2,1,0:T(2,128)(2,1)} %reshape.39.payload_ref), custom_call_target="tpu_custom_call" | custom-call | tf_op jit(solution)/shard_map/pallas_call | solution.py:185
  58.5 0.9 slice_convert_fusion.1
  59.4 0.1 copy.24
  59.5 0.0 copy-start.2
  59.5 3.7 %convolution_bitcast_fusion = bf16[256,8320]{1,0:T(8,128)(2,1)S(1)} fusion(bf16[128,2,8320]{2,1,0:T(2,128)(2,1)} %shard_map.109, s32[128,2]{0,1:T(2,128)S(1)} %bitcast.13), kind=kOutput, calls=%fused_computation | convolution fusion | flops 1090584576 | bytes 8520704 | tf_op jit(solution)/shard_map/dot_general | solution.py:42
  63.2 0.1 fusion.7
  63.3 0.0 copy-done.2
  63.3 0.0 copy-start.4
  63.3 2.3 %fusion = (f32[256]{0:T(256)S(1)}, bf16[256,8192]{1,0:T(8,128)(2,1)S(1)}) fusion(bf16[256,8192]{1,0:T(8,128)(2,1)S(1)} %copy-done.2, bf16[256,8320]{1,0:T(8,128)(2,1)S(1)} %convolution_bitcast_fusion, pred[256]{0:T(512)(128)(4,1)S(1)} %fusion.7), kind=kLoop, calls=%fused_computation.4 | loop fusion | flops 8388352 | bytes 12584192 | tf_op jit(solution)/shard_map/reduce_sum | solution.py:349
  65.6 0.0 copy-done.4
  65.6 0.0 copy-start.5
  65.6 1.2 fusion.2.normed_ref
  66.8 0.0 copy-done
  66.8 0.0 copy-done.5
  66.8 0.0 copy-start.1
  66.8 0.0 copy-start.3
  66.9 1.3 %fusion.5 = bf16[256,128]{1,0:T(8,128)(2,1)S(1)} fusion(bf16[256,8192]{1,0:T(8,128)(2,1)S(1)} %fusion.2.normed_ref, bf16[8192,128]{1,0:T(8,128)(2,1)S(1)} %copy-done, f32[128]{0:T(128)S(1)} %copy-done.5), kind=kOutput, calls=%fused_computation.11 | convolution fusion | flops 536936448 | bytes 6357504 | tf_op jit(solution)/shard_map/dot_general | solution.py:352
  68.2 1.8 %copy-done.3 = bf16[8192,128]{1,0:T(8,128)(2,1)S(1)} copy-done((bf16[8192,128]{1,0:T(8,128)(2,1)S(1)}, bf16[8192,128]{1,0:T(8,128)(2,1)}, u32[]{:S(2)}) %copy-start.3) | copy-done | bytes 2097176
  70.0 1.3 %convolution_convert_fusion.1 = bf16[256,128]{1,0:T(8,128)(2,1)S(1)} fusion(bf16[256,8192]{1,0:T(8,128)(2,1)S(1)} %fusion.2.normed_ref, bf16[8192,128]{1,0:T(8,128)(2,1)S(1)} %copy-done.3), kind=kOutput, calls=%fused_computation.12 | convolution fusion | flops 536903680 | bytes 6356992 | tf_op jit(solution)/shard_map/dot_general | solution.py:351
  71.2 0.0 copy-done.1
  71.2 0.7 pad_maximum_fusion.1.block_ref
  71.9 28.4 %shard_map.110 = (bf16[4096,256]{1,0:T(8,128)(2,1)}, bf16[256,1024]{1,0:T(8,128)(2,1)}) custom-call(bf16[256,256]{1,0:T(8,128)(2,1)} %pad_maximum_fusion.1.block_ref, bf16[256,8192]{1,0:T(8,128)(2,1)} %copy-done.1, bf16[8192,1024]{1,0:T(8,128)(2,1)} %w_ref.1, f32[1,1024]{1,0:T(1,128)} %bitcast.15), custom_call_target="tpu_custom_call" | custom-call | tf_op jit(solution)/shard_map/pallas_call | solution.py:311
  100.3 23.2 %shard_map.111 = bf16[256,1024]{1,0:T(8,128)(2,1)} custom-call(s32[4096]{0:T(1024)} %doc_ref.1, bf16[256,1024]{1,0:T(8,128)(2,1)} %get-tuple-element.7.q_ref, bf16[4096,256]{1,0:T(8,128)(2,1)} %get-tuple-element.8.k_ref.v_ref, bf16[4096,256]{1,0:T(8,128)(2,1)} %get-tuple-element.8.k_ref.v_ref, s32[1,4096]{1,0:T(1,128)} %bitcast.16, s32[1,4096]{1,0:T(1,128)} %bitcast.17), custom_call_target="tpu_custom_call" | custom-call | flops 2147483648 | bytes 3145728 | tf_op jit(solution)/shard_map/pallas_call | solution.py:453
  (5 shorter events, 0.1 us)
Async XLA Ops:
  0.0 66.8 %copy-start = (bf16[8192,128]{1,0:T(8,128)(2,1)S(1)}, bf16[8192,128]{1,0:T(8,128)(2,1)}, u32[]{:S(2)}) copy-start(bf16[8192,128]{1,0:T(8,128)(2,1)} %param.20) | copy-start | bytes 6291460
  59.5 3.8 %copy-start.2 = (bf16[256,8192]{1,0:T(8,128)(2,1)S(1)}, bf16[256,8192]{1,0:T(8,128)(2,1)}, u32[]{:S(2)}) copy-start(bf16[256,8192]{1,0:T(8,128)(2,1)} %param.11) | copy-start | bytes 12582916
  63.3 2.3 %copy-start.4 = (f32[8192]{0:T(1024)S(1)}, f32[8192]{0:T(1024)}, u32[]{:S(2)}) copy-start(f32[8192]{0:T(1024)} %param.16) | copy-start | bytes 98308
  65.6 1.2 copy-start.5
  66.8 4.4 %copy-start.1 = (bf16[256,8192]{1,0:T(8,128)(2,1)}, bf16[256,8192]{1,0:T(8,128)(2,1)S(1)}, u32[]{:S(2)}) copy-start(bf16[256,8192]{1,0:T(8,128)(2,1)S(1)} %fusion.2.normed_ref) | copy-start | bytes 12582916
  66.8 3.1 %copy-start.3 = (bf16[8192,128]{1,0:T(8,128)(2,1)S(1)}, bf16[8192,128]{1,0:T(8,128)(2,1)}, u32[]{:S(2)}) copy-start(bf16[8192,128]{1,0:T(8,128)(2,1)} %param.19) | copy-start | bytes 6291460

commit v17 on v14

--- a/solution.py
+++ b/solution.py
@@ -73,14 +73,14 @@
         )
     pl.semaphore_wait(barrier, seq_count + 2)
     base = me_vis * seq_count
-    local = pltpu.make_async_copy(payload_ref.at[me_seq], out_ref.at[base + me_seq], local_sem.at[0])
+    local = pltpu.make_async_copy(payload_ref.at[me_seq], out_ref.at[base], local_sem.at[0])
     local.start()
     first = []
     for k in range(1, seq_count):
         target = lax.rem(me_seq + k, seq_count)
         copy = pltpu.make_async_remote_copy(
             src_ref=payload_ref.at[target],
-            dst_ref=out_ref.at[base + me_seq],
+            dst_ref=out_ref.at[base + k],
             send_sem=send_a.at[k],
             recv_sem=recv_a.at[k],
             device_id=(target, me_vis),
@@ -89,19 +89,21 @@
         copy.start()
         first.append(copy)
     local.wait()
-    for k in range(1, seq_count):
-        source = lax.rem(me_seq + seq_count - k, seq_count)
-        incoming = pltpu.make_async_remote_copy(
-            src_ref=payload_ref.at[source],
-            dst_ref=out_ref.at[base + source],
-            send_sem=send_a.at[k],
-            recv_sem=recv_a.at[k],
-            device_id=(source, me_vis),
-            device_id_type=pl.DeviceIdType.MESH,
-        )
-        incoming.wait_recv()
-    for copy in first:
-        copy.wait_send()
+
+    def arrivals(ks):
+        for k in ks:
+            source = lax.rem(me_seq + seq_count - k, seq_count)
+            incoming = pltpu.make_async_remote_copy(
+                src_ref=payload_ref.at[source],
+                dst_ref=out_ref.at[base + k],
+                send_sem=send_a.at[k],
+                recv_sem=recv_a.at[k],
+                device_id=(source, me_vis),
+                device_id_type=pl.DeviceIdType.MESH,
+            )
+            incoming.wait_recv()
+
+    arrivals(range(1, seq_count // 2))
 
     half = seq_count // 2
 
@@ -133,15 +135,24 @@
         copy.start()
         sent.append(copy)
 
-    send(me_vis, 0, right, 1)
-    send(me_vis, 0, left, 2)
-    send(me_vis, 0, partner, 3)
-    link(partner, 0, partner, 3).wait_recv()
+    send(me_vis, 1, right, 1)
+    send(me_vis, 1, left, 2)
+    send(me_vis, 1, partner, 3)
+    arrivals(range(seq_count // 2, seq_count))
+    for copy in first:
+        copy.wait_send()
+    send(me_vis, 2, right, 10)
+    send(me_vis, 2, left, 11)
+    send(me_vis, 2, partner, 12)
+    link(partner, 1, partner, 3).wait_recv()
+    link(partner, 2, partner, 12).wait_recv()
     send(partner, 0, right, 4)
     send(partner, 0, left, 5)
-    link(left, 0, left, 1).wait_recv()
+    link(left, 1, left, 1).wait_recv()
+    link(left, 2, left, 10).wait_recv()
     send(left, 1, right, 6)
-    link(right, 0, right, 2).wait_recv()
+    link(right, 1, right, 2).wait_recv()
+    link(right, 2, right, 11).wait_recv()
     send(right, 2, left, 7)
     link(left_partner, 0, left, 4).wait_recv()
     send(left_partner, 1, right, 8)
@@ -165,8 +176,8 @@
         scratch_shapes=[
             pltpu.SemaphoreType.DMA((owners,)),
             pltpu.SemaphoreType.DMA((owners,)),
-            pltpu.SemaphoreType.DMA((10,)),
-            pltpu.SemaphoreType.DMA((10,)),
+            pltpu.SemaphoreType.DMA((13,)),
+            pltpu.SemaphoreType.DMA((13,)),
             pltpu.SemaphoreType.DMA((1,)),
         ],
         compiler_params=pltpu.CompilerParams(collective_id=1, has_side_effects=True),

time: 123 us -> 121 us (0.984)
  the two profiles are of different devices: /device:TPU:25 before, /device:TPU:24 now
where the time goes in v17:
time: 121 us; the launch traced here: 120 us
  Pallas kernels  102 us (84%)
  matrix products  7.84 us (6%)
  other arithmetic  6.1 us (5%)
  local copies, waits for them, and re-layouts  3 us (2%)
    pallas_call x1, Pallas kernels, exchange_frames(): pl.pallas_call(exchange_kernel, out_shape=jax.ShapeDtypeStruct((vis_count...  52.8 us
    pallas_call x1, Pallas kernels, gather_keys(): pl.pallas_call(gather_kernel, out_shape=(jax.ShapeDtypeStruct((seq_count...  26.4 us
    pallas_call x1, Pallas kernels, flash_attention(): pl.pallas_call(flash_kernel, out_shape=jax.ShapeDtypeStruct((rows, width)...  23.2 us
    dot_general x1, matrix products, place_frames(): lax.dot_general(lookup.astype(incoming.dtype), incoming, (((1, 2), (0, 1)...  3.67 us

profile of v17, /device:TPU:24, one launch (start us, length us, event | category | flops | bytes accessed | tf_op | source)
XLA Modules:
  0.0 120.3 jit_solution(3196929992951250482)
XLA Ops:
  0.0 0.0 copy-start
  0.8 0.7 multiply_subtract_fusion
  1.5 0.1 fusion.6
  1.6 0.1 select_reduce_fusion
  1.7 0.1 fusion.10
  1.8 0.1 broadcast_in_dim.27
  1.9 1.5 %convolution_convert_fusion = bf16[32,8192]{1,0:T(8,128)(2,1)S(1)} fusion(bf16[32,8192]{1,0:T(8,128)(2,1)} %param.12, s32[32]{0:T(128)S(1)} %multiply_add_fusion, pred[32]{0:T(512)(128)(4,1)S(1)} %iota_compare_fusion.7), kind=kOutput, calls=%fused_computation.3 | convolution fusion | flops 17041408 | bytes 1048736 | tf_op jit(solution)/shard_map/dot_general | solution.py:31
  3.4 1.0 reshape.39.payload_ref
  4.5 52.8 %shard_map.109 = bf16[128,2,8320]{2,1,0:T(2,128)(2,1)} custom-call(bf16[16,2,8320]{2,1,0:T(2,128)(2,1)} %reshape.39.payload_ref), custom_call_target="tpu_custom_call" | custom-call | tf_op jit(solution)/shard_map/pallas_call | solution.py:171
  57.2 0.9 slice_convert_fusion.1
  58.1 0.1 copy.24
  58.2 0.0 copy-start.2
  58.2 3.7 %convolution_bitcast_fusion = bf16[256,8320]{1,0:T(8,128)(2,1)S(1)} fusion(bf16[128,2,8320]{2,1,0:T(2,128)(2,1)} %shard_map.109, s32[128,2]{0,1:T(2,128)S(1)} %bitcast.13), kind=kOutput, calls=%fused_computation | convolution fusion | flops 1090584576 | bytes 8520704 | tf_op jit(solution)/shard_map/dot_general | solution.py:42
  61.9 0.1 fusion.7
  62.0 0.0 copy-done.2
  62.0 0.0 copy-start.4
  62.0 2.3 %fusion = (f32[256]{0:T(256)S(1)}, bf16[256,8192]{1,0:T(8,128)(2,1)S(1)}) fusion(bf16[256,8192]{1,0:T(8,128)(2,1)S(1)} %copy-done.2, bf16[256,8320]{1,0:T(8,128)(2,1)S(1)} %convolution_bitcast_fusion, pred[256]{0:T(512)(128)(4,1)S(1)} %fusion.7), kind=kLoop, calls=%fused_computation.4 | loop fusion | flops 8388352 | bytes 12584192 | tf_op jit(solution)/shard_map/reduce_sum | solution.py:334
  64.3 0.0 copy-done.4
  64.3 0.0 copy-start.5
  64.4 1.2 fusion.2.normed_ref
  65.5 0.0 copy-done
  65.6 0.0 copy-done.5
  65.6 0.0 copy-start.1
  65.6 0.0 copy-start.3
  65.6 1.3 %fusion.5 = bf16[256,128]{1,0:T(8,128)(2,1)S(1)} fusion(bf16[256,8192]{1,0:T(8,128)(2,1)S(1)} %fusion.2.normed_ref, bf16[8192,128]{1,0:T(8,128)(2,1)S(1)} %copy-done, f32[128]{0:T(128)S(1)} %copy-done.5), kind=kOutput, calls=%fused_computation.11 | convolution fusion | flops 536936448 | bytes 6357504 | tf_op jit(solution)/shard_map/dot_general | solution.py:337
  66.9 1.8 %copy-done.3 = bf16[8192,128]{1,0:T(8,128)(2,1)S(1)} copy-done((bf16[8192,128]{1,0:T(8,128)(2,1)S(1)}, bf16[8192,128]{1,0:T(8,128)(2,1)}, u32[]{:S(2)}) %copy-start.3) | copy-done | bytes 2097176
  68.7 1.3 %convolution_convert_fusion.1 = bf16[256,128]{1,0:T(8,128)(2,1)S(1)} fusion(bf16[256,8192]{1,0:T(8,128)(2,1)S(1)} %fusion.2.normed_ref, bf16[8192,128]{1,0:T(8,128)(2,1)S(1)} %copy-done.3), kind=kOutput, calls=%fused_computation.12 | convolution fusion | flops 536903680 | bytes 6356992 | tf_op jit(solution)/shard_map/dot_general | solution.py:336
  70.0 0.0 copy-done.1
  70.0 0.7 pad_maximum_fusion.1.block_ref
  70.7 26.4 %shard_map.110 = (bf16[4096,256]{1,0:T(8,128)(2,1)}, bf16[256,1024]{1,0:T(8,128)(2,1)}) custom-call(bf16[256,256]{1,0:T(8,128)(2,1)} %pad_maximum_fusion.1.block_ref, bf16[256,8192]{1,0:T(8,128)(2,1)} %copy-done.1, bf16[8192,1024]{1,0:T(8,128)(2,1)} %w_ref.1, f32[1,1024]{1,0:T(1,128)} %bitcast.15), custom_call_target="tpu_custom_call" | custom-call | tf_op jit(solution)/shard_map/pallas_call | solution.py:296
  97.1 23.2 %shard_map.111 = bf16[256,1024]{1,0:T(8,128)(2,1)} custom-call(s32[4096]{0:T(1024)} %doc_ref.1, bf16[256,1024]{1,0:T(8,128)(2,1)} %get-tuple-element.7.q_ref, bf16[4096,256]{1,0:T(8,128)(2,1)} %get-tuple-element.8.k_ref.v_ref, bf16[4096,256]{1,0:T(8,128)(2,1)} %get-tuple-element.8.k_ref.v_ref, s32[1,4096]{1,0:T(1,128)} %bitcast.16, s32[1,4096]{1,0:T(1,128)} %bitcast.17), custom_call_target="tpu_custom_call" | custom-call | flops 2147483648 | bytes 3145728 | tf_op jit(solution)/shard_map/pallas_call | solution.py:438
  (5 shorter events, 0.1 us)
Async XLA Ops:
  0.0 65.5 %copy-start = (bf16[8192,128]{1,0:T(8,128)(2,1)S(1)}, bf16[8192,128]{1,0:T(8,128)(2,1)}, u32[]{:S(2)}) copy-start(bf16[8192,128]{1,0:T(8,128)(2,1)} %param.20) | copy-start | bytes 6291460
  58.2 3.8 %copy-start.2 = (bf16[256,8192]{1,0:T(8,128)(2,1)S(1)}, bf16[256,8192]{1,0:T(8,128)(2,1)}, u32[]{:S(2)}) copy-start(bf16[256,8192]{1,0:T(8,128)(2,1)} %param.11) | copy-start | bytes 12582916
  62.0 2.3 %copy-start.4 = (f32[8192]{0:T(1024)S(1)}, f32[8192]{0:T(1024)}, u32[]{:S(2)}) copy-start(f32[8192]{0:T(1024)} %param.16) | copy-start | bytes 98308
  64.3 1.2 %copy-start.5 = (f32[128]{0:T(128)S(1)}, f32[128]{0:T(128)}, u32[]{:S(2)}) copy-start(f32[128]{0:T(128)} %param.21) | copy-start | bytes 1540
  65.6 4.4 %copy-start.1 = (bf16[256,8192]{1,0:T(8,128)(2,1)}, bf16[256,8192]{1,0:T(8,128)(2,1)S(1)}, u32[]{:S(2)}) copy-start(bf16[256,8192]{1,0:T(8,128)(2,1)S(1)} %fusion.2.normed_ref) | copy-start | bytes 12582916
  65.6 3.1 %copy-start.3 = (bf16[8192,128]{1,0:T(8,128)(2,1)S(1)}, bf16[8192,128]{1,0:T(8,128)(2,1)}, u32[]{:S(2)}) copy-start(bf16[8192,128]{1,0:T(8,128)(2,1)} %param.19) | copy-start | bytes 6291460

commit v18 on v17

--- a/solution.py
+++ b/solution.py
@@ -145,19 +145,23 @@
     send(me_vis, 2, left, 11)
     send(me_vis, 2, partner, 12)
     link(partner, 1, partner, 3).wait_recv()
+    send(partner, 1, right, 4)
+    send(partner, 1, left, 5)
+    link(left, 1, left, 1).wait_recv()
+    send(left, 1, right, 6)
     link(partner, 2, partner, 12).wait_recv()
-    send(partner, 0, right, 4)
-    send(partner, 0, left, 5)
-    link(left, 1, left, 1).wait_recv()
-    link(left, 2, left, 10).wait_recv()
-    send(left, 1, right, 6)
-    link(right, 1, right, 2).wait_recv()
+    send(partner, 2, right, 13)
+    send(partner, 2, left, 14)
     link(right, 2, right, 11).wait_recv()
     send(right, 2, left, 7)
-    link(left_partner, 0, left, 4).wait_recv()
+    link(left_partner, 1, left, 4).wait_recv()
     send(left_partner, 1, right, 8)
-    link(right_partner, 0, right, 5).wait_recv()
+    link(right_partner, 2, right, 14).wait_recv()
     send(right_partner, 2, left, 9)
+    link(left, 2, left, 10).wait_recv()
+    link(right, 1, right, 2).wait_recv()
+    link(left_partner, 2, left, 13).wait_recv()
+    link(right_partner, 1, right, 5).wait_recv()
     link(far, 1, left, 6).wait_recv()
     link(far, 2, right, 7).wait_recv()
     link(far_partner, 1, left, 8).wait_recv()
@@ -176,8 +180,8 @@
         scratch_shapes=[
             pltpu.SemaphoreType.DMA((owners,)),
             pltpu.SemaphoreType.DMA((owners,)),
-            pltpu.SemaphoreType.DMA((13,)),
-            pltpu.SemaphoreType.DMA((13,)),
+            pltpu.SemaphoreType.DMA((15,)),
+            pltpu.SemaphoreType.DMA((15,)),
             pltpu.SemaphoreType.DMA((1,)),
         ],
         compiler_params=pltpu.CompilerParams(collective_id=1, has_side_effects=True),

time: 121 us -> 114 us (0.942)
  the two profiles are of different devices: /device:TPU:24 before, /device:TPU:57 now
where the time goes in v18:
time: 114 us; the launch traced here: 113 us
  Pallas kernels  95.3 us (84%)
  matrix products  7.83 us (7%)
  other arithmetic  6.1 us (5%)
  local copies, waits for them, and re-layouts  3 us (3%)
    pallas_call x1, Pallas kernels, exchange_frames(): pl.pallas_call(exchange_kernel, out_shape=jax.ShapeDtypeStruct((vis_count...  47.8 us
    pallas_call x1, Pallas kernels, gather_keys(): pl.pallas_call(gather_kernel, out_shape=(jax.ShapeDtypeStruct((seq_count...  27.9 us
    pallas_call x1, Pallas kernels, flash_attention(): pl.pallas_call(flash_kernel, out_shape=jax.ShapeDtypeStruct((rows, width)...  19.6 us
    dot_general x1, matrix products, place_frames(): lax.dot_general(lookup.astype(incoming.dtype), incoming, (((1, 2), (0, 1)...  3.67 us
    reduce_sum x1, other arithmetic, on_device(): mean_square = jnp.mean(widened * widened, axis=1, keepdims=True)  2.28 us

profile of v18, /device:TPU:57, one launch (start us, length us, event | category | flops | bytes accessed | tf_op | source)
XLA Modules:
  0.0 113.2 jit_solution(1895488403804136993)
XLA Ops:
  0.0 0.0 copy-start
  0.8 0.7 multiply_subtract_fusion
  1.5 0.1 fusion.6
  1.6 0.1 select_reduce_fusion
  1.7 0.1 fusion.10
  1.8 0.1 broadcast_in_dim.27
  1.9 1.5 %convolution_convert_fusion = bf16[32,8192]{1,0:T(8,128)(2,1)S(1)} fusion(bf16[32,8192]{1,0:T(8,128)(2,1)} %param.12, s32[32]{0:T(128)S(1)} %multiply_add_fusion, pred[32]{0:T(512)(128)(4,1)S(1)} %iota_compare_fusion.7), kind=kOutput, calls=%fused_computation.3 | convolution fusion | flops 17041408 | bytes 1048736 | tf_op jit(solution)/shard_map/dot_general | solution.py:31
  3.4 1.0 reshape.39.payload_ref
  4.4 47.8 %shard_map.109 = bf16[128,2,8320]{2,1,0:T(2,128)(2,1)} custom-call(bf16[16,2,8320]{2,1,0:T(2,128)(2,1)} %reshape.39.payload_ref), custom_call_target="tpu_custom_call" | custom-call | tf_op jit(solution)/shard_map/pallas_call | solution.py:175
  52.3 0.9 slice_convert_fusion.1
  53.2 0.1 copy.24
  53.3 0.0 copy-start.2
  53.3 3.7 %convolution_bitcast_fusion = bf16[256,8320]{1,0:T(8,128)(2,1)S(1)} fusion(bf16[128,2,8320]{2,1,0:T(2,128)(2,1)} %shard_map.109, s32[128,2]{0,1:T(2,128)S(1)} %bitcast.13), kind=kOutput, calls=%fused_computation | convolution fusion | flops 1090584576 | bytes 8520704 | tf_op jit(solution)/shard_map/dot_general | solution.py:42
  56.9 0.1 fusion.7
  57.1 0.0 copy-done.2
  57.1 0.0 copy-start.4
  57.1 2.3 %fusion = (f32[256]{0:T(256)S(1)}, bf16[256,8192]{1,0:T(8,128)(2,1)S(1)}) fusion(bf16[256,8192]{1,0:T(8,128)(2,1)S(1)} %copy-done.2, bf16[256,8320]{1,0:T(8,128)(2,1)S(1)} %convolution_bitcast_fusion, pred[256]{0:T(512)(128)(4,1)S(1)} %fusion.7), kind=kLoop, calls=%fused_computation.4 | loop fusion | flops 8388352 | bytes 12584192 | tf_op jit(solution)/shard_map/reduce_sum | solution.py:338
  59.4 0.0 copy-done.4
  59.4 0.0 copy-start.5
  59.4 1.2 %fusion.2.normed_ref = bf16[256,8192]{1,0:T(8,128)(2,1)S(1)} fusion(bf16[256,8192]{1,0:T(8,128)(2,1)S(1)} %get-tuple-element.10, f32[8192]{0:T(1024)S(1)} %copy-done.4, f32[256]{0:T(256)S(1)} %add_rsqrt_fusion), kind=kLoop, calls=%fused_computation.6 | loop fusion | flops 8388608 | bytes 8422400 | tf_op jit(solution)/shard_map/convert_element_type | solution.py:339
  60.6 0.0 copy-done
  60.6 0.0 copy-done.5
  60.6 0.0 copy-start.1
  60.6 0.0 copy-start.3
  60.6 1.3 %fusion.5 = bf16[256,128]{1,0:T(8,128)(2,1)S(1)} fusion(bf16[256,8192]{1,0:T(8,128)(2,1)S(1)} %fusion.2.normed_ref, bf16[8192,128]{1,0:T(8,128)(2,1)S(1)} %copy-done, f32[128]{0:T(128)S(1)} %copy-done.5), kind=kOutput, calls=%fused_computation.11 | convolution fusion | flops 536936448 | bytes 6357504 | tf_op jit(solution)/shard_map/dot_general | solution.py:341
  61.9 1.8 %copy-done.3 = bf16[8192,128]{1,0:T(8,128)(2,1)S(1)} copy-done((bf16[8192,128]{1,0:T(8,128)(2,1)S(1)}, bf16[8192,128]{1,0:T(8,128)(2,1)}, u32[]{:S(2)}) %copy-start.3) | copy-done | bytes 2097176
  63.7 1.3 %convolution_convert_fusion.1 = bf16[256,128]{1,0:T(8,128)(2,1)S(1)} fusion(bf16[256,8192]{1,0:T(8,128)(2,1)S(1)} %fusion.2.normed_ref, bf16[8192,128]{1,0:T(8,128)(2,1)S(1)} %copy-done.3), kind=kOutput, calls=%fused_computation.12 | convolution fusion | flops 536903680 | bytes 6356992 | tf_op jit(solution)/shard_map/dot_general | solution.py:340
  65.0 0.0 copy-done.1
  65.0 0.7 pad_maximum_fusion.1.block_ref
  65.7 27.9 %shard_map.110 = (bf16[4096,256]{1,0:T(8,128)(2,1)}, bf16[256,1024]{1,0:T(8,128)(2,1)}) custom-call(bf16[256,256]{1,0:T(8,128)(2,1)} %pad_maximum_fusion.1.block_ref, bf16[256,8192]{1,0:T(8,128)(2,1)} %copy-done.1, bf16[8192,1024]{1,0:T(8,128)(2,1)} %w_ref.1, f32[1,1024]{1,0:T(1,128)} %bitcast.15), custom_call_target="tpu_custom_call" | custom-call | tf_op jit(solution)/shard_map/pallas_call | solution.py:300
  93.6 19.6 %shard_map.111 = bf16[256,1024]{1,0:T(8,128)(2,1)} custom-call(s32[4096]{0:T(1024)} %doc_ref.1, bf16[256,1024]{1,0:T(8,128)(2,1)} %get-tuple-element.7.q_ref, bf16[4096,256]{1,0:T(8,128)(2,1)} %get-tuple-element.8.k_ref.v_ref, bf16[4096,256]{1,0:T(8,128)(2,1)} %get-tuple-element.8.k_ref.v_ref, s32[1,4096]{1,0:T(1,128)} %bitcast.16, s32[1,4096]{1,0:T(1,128)} %bitcast.17), custom_call_target="tpu_custom_call" | custom-call | flops 2147483648 | bytes 3145728 | tf_op jit(solution)/shard_map/pallas_call | solution.py:442
  (5 shorter events, 0.1 us)
Async XLA Ops:
  0.0 60.6 %copy-start = (bf16[8192,128]{1,0:T(8,128)(2,1)S(1)}, bf16[8192,128]{1,0:T(8,128)(2,1)}, u32[]{:S(2)}) copy-start(bf16[8192,128]{1,0:T(8,128)(2,1)} %param.20) | copy-start | bytes 6291460
  53.3 3.8 %copy-start.2 = (bf16[256,8192]{1,0:T(8,128)(2,1)S(1)}, bf16[256,8192]{1,0:T(8,128)(2,1)}, u32[]{:S(2)}) copy-start(bf16[256,8192]{1,0:T(8,128)(2,1)} %param.11) | copy-start | bytes 12582916
  57.1 2.3 %copy-start.4 = (f32[8192]{0:T(1024)S(1)}, f32[8192]{0:T(1024)}, u32[]{:S(2)}) copy-start(f32[8192]{0:T(1024)} %param.16) | copy-start | bytes 98308
  59.4 1.2 %copy-start.5 = (f32[128]{0:T(128)S(1)}, f32[128]{0:T(128)}, u32[]{:S(2)}) copy-start(f32[128]{0:T(128)} %param.21) | copy-start | bytes 1540
  60.6 4.4 %copy-start.1 = (bf16[256,8192]{1,0:T(8,128)(2,1)}, bf16[256,8192]{1,0:T(8,128)(2,1)S(1)}, u32[]{:S(2)}) copy-start(bf16[256,8192]{1,0:T(8,128)(2,1)S(1)} %fusion.2.normed_ref) | copy-start | bytes 12582916
  60.6 3.1 %copy-start.3 = (bf16[8192,128]{1,0:T(8,128)(2,1)S(1)}, bf16[8192,128]{1,0:T(8,128)(2,1)}, u32[]{:S(2)}) copy-start(bf16[8192,128]{1,0:T(8,128)(2,1)} %param.19) | copy-start | bytes 6291460

commit v19 on v17

--- a/solution.py
+++ b/solution.py
@@ -103,65 +103,66 @@
             )
             incoming.wait_recv()
 
-    arrivals(range(1, seq_count // 2))
-
-    half = seq_count // 2
-
-    def region(owner, part):
-        if part == 0:
-            return out_ref.at[pl.ds(owner * seq_count, seq_count)]
-        start = owner * seq_count + (part - 1) * half
-        return out_ref.at[pl.ds(start, half)]
-
-    def link(owner, part, peer, index):
-        piece = region(owner, part)
-        return pltpu.make_async_remote_copy(
-            src_ref=piece,
-            dst_ref=piece,
-            send_sem=send_b.at[index],
-            recv_sem=recv_b.at[index],
-            device_id=(me_seq, peer),
-            device_id_type=pl.DeviceIdType.MESH,
-        )
-
+    waves = WAVES
+    size = seq_count // waves
+    split = waves // 2
     far = vis_of(ring_id, ring_pos + 2)
     left_partner = vis_of(1 - ring_id, ring_pos - 1)
     right_partner = vis_of(1 - ring_id, ring_pos + 1)
     far_partner = vis_of(1 - ring_id, ring_pos + 2)
     sent = []
 
-    def send(owner, part, peer, index):
-        copy = link(owner, part, peer, index)
+    def part(owner, w):
+        return out_ref.at[pl.ds(owner * seq_count + w * size, size)]
+
+    def link(owner, w, peer, kind):
+        piece = part(owner, w)
+        return pltpu.make_async_remote_copy(
+            src_ref=piece, dst_ref=piece,
+            send_sem=send_b.at[kind * waves + w], recv_sem=recv_b.at[kind * waves + w],
+            device_id=(me_seq, peer), device_id_type=pl.DeviceIdType.MESH,
+        )
+
+    def send(owner, w, peer, kind):
+        copy = link(owner, w, peer, kind)
         copy.start()
         sent.append(copy)
 
-    send(me_vis, 1, right, 1)
-    send(me_vis, 1, left, 2)
-    send(me_vis, 1, partner, 3)
-    arrivals(range(seq_count // 2, seq_count))
+    for w in range(waves):
+        arrivals(range(max(1, w * size), (w + 1) * size))
+        send(me_vis, w, right, 0)
+        send(me_vis, w, left, 1)
+        send(me_vis, w, partner, 2)
     for copy in first:
         copy.wait_send()
-    send(me_vis, 2, right, 10)
-    send(me_vis, 2, left, 11)
-    send(me_vis, 2, partner, 12)
-    link(partner, 1, partner, 3).wait_recv()
-    link(partner, 2, partner, 12).wait_recv()
-    send(partner, 0, right, 4)
-    send(partner, 0, left, 5)
-    link(left, 1, left, 1).wait_recv()
-    link(left, 2, left, 10).wait_recv()
-    send(left, 1, right, 6)
-    link(right, 1, right, 2).wait_recv()
-    link(right, 2, right, 11).wait_recv()
-    send(right, 2, left, 7)
-    link(left_partner, 0, left, 4).wait_recv()
-    send(left_partner, 1, right, 8)
-    link(right_partner, 0, right, 5).wait_recv()
-    send(right_partner, 2, left, 9)
-    link(far, 1, left, 6).wait_recv()
-    link(far, 2, right, 7).wait_recv()
-    link(far_partner, 1, left, 8).wait_recv()
-    link(far_partner, 2, right, 9).wait_recv()
+    for w in range(waves):
+        link(partner, w, partner, 2).wait_recv()
+        send(partner, w, right, 3)
+        send(partner, w, left, 4)
+        if w < split:
+            link(left, w, left, 0).wait_recv()
+            send(left, w, right, 5)
+        else:
+            link(right, w, right, 1).wait_recv()
+            send(right, w, left, 6)
+    for w in range(waves):
+        if w < split:
+            link(left_partner, w, left, 3).wait_recv()
+            send(left_partner, w, right, 7)
+        else:
+            link(right_partner, w, right, 4).wait_recv()
+            send(right_partner, w, left, 8)
+    for w in range(waves):
+        if w < split:
+            link(right, w, right, 1).wait_recv()
+            link(right_partner, w, right, 4).wait_recv()
+            link(far, w, left, 5).wait_recv()
+            link(far_partner, w, left, 7).wait_recv()
+        else:
+            link(left, w, left, 0).wait_recv()
+            link(left_partner, w, left, 3).wait_recv()
+            link(far, w, right, 6).wait_recv()
+            link(far_partner, w, right, 8).wait_recv()
     for copy in sent:
         copy.wait_send()
 
@@ -176,8 +177,8 @@
         scratch_shapes=[
             pltpu.SemaphoreType.DMA((owners,)),
             pltpu.SemaphoreType.DMA((owners,)),
-            pltpu.SemaphoreType.DMA((13,)),
-            pltpu.SemaphoreType.DMA((13,)),
+            pltpu.SemaphoreType.DMA((9 * WAVES,)),
+            pltpu.SemaphoreType.DMA((9 * WAVES,)),
             pltpu.SemaphoreType.DMA((1,)),
         ],
         compiler_params=pltpu.CompilerParams(collective_id=1, has_side_effects=True),
@@ -345,6 +346,7 @@
 
 
 KEY_BLOCK = 512
+WAVES = 4
 DOC_SPAN = 2048
 
 

time: 121 us -> 112 us (0.926)
  the two profiles are of different devices: /device:TPU:24 before, /device:TPU:57 now
where the time goes in v19:
time: 112 us; the launch traced here: 111 us
  Pallas kernels  93.4 us (83%)
  matrix products  7.84 us (7%)
  other arithmetic  6.1 us (5%)
  local copies, waits for them, and re-layouts  3 us (3%)
    pallas_call x1, Pallas kernels, exchange_frames(): pl.pallas_call(exchange_kernel, out_shape=jax.ShapeDtypeStruct((vis_count...  46.7 us
    pallas_call x1, Pallas kernels, gather_keys(): pl.pallas_call(gather_kernel, out_shape=(jax.ShapeDtypeStruct((seq_count...  27.2 us
    pallas_call x1, Pallas kernels, flash_attention(): pl.pallas_call(flash_kernel, out_shape=jax.ShapeDtypeStruct((rows, width)...  19.6 us
    dot_general x1, matrix products, place_frames(): lax.dot_general(lookup.astype(incoming.dtype), incoming, (((1, 2), (0, 1)...  3.67 us
    reduce_sum x1, other arithmetic, on_device(): mean_square = jnp.mean(widened * widened, axis=1, keepdims=True)  2.28 us

profile of v19, /device:TPU:57, one launch (start us, length us, event | category | flops | bytes accessed | tf_op | source)
XLA Modules:
  0.0 111.3 jit_solution(10651662589206621393)
XLA Ops:
  0.0 0.0 copy-start
  0.8 0.7 multiply_subtract_fusion
  1.5 0.1 fusion.6
  1.6 0.1 select_reduce_fusion
  1.7 0.1 fusion.10
  1.8 0.1 broadcast_in_dim.27
  1.9 1.5 %convolution_convert_fusion = bf16[32,8192]{1,0:T(8,128)(2,1)S(1)} fusion(bf16[32,8192]{1,0:T(8,128)(2,1)} %param.12, s32[32]{0:T(128)S(1)} %multiply_add_fusion, pred[32]{0:T(512)(128)(4,1)S(1)} %iota_compare_fusion.7), kind=kOutput, calls=%fused_computation.3 | convolution fusion | flops 17041408 | bytes 1048736 | tf_op jit(solution)/shard_map/dot_general | solution.py:31
  3.4 1.0 reshape.39.payload_ref
  4.4 46.7 %shard_map.109 = bf16[128,2,8320]{2,1,0:T(2,128)(2,1)} custom-call(bf16[16,2,8320]{2,1,0:T(2,128)(2,1)} %reshape.39.payload_ref), custom_call_target="tpu_custom_call" | custom-call | tf_op jit(solution)/shard_map/pallas_call | solution.py:172
  51.2 0.9 slice_convert_fusion.1
  52.1 0.1 copy.24
  52.2 0.0 copy-start.2
  52.2 3.7 %convolution_bitcast_fusion = bf16[256,8320]{1,0:T(8,128)(2,1)S(1)} fusion(bf16[128,2,8320]{2,1,0:T(2,128)(2,1)} %shard_map.109, s32[128,2]{0,1:T(2,128)S(1)} %bitcast.13), kind=kOutput, calls=%fused_computation | convolution fusion | flops 1090584576 | bytes 8520704 | tf_op jit(solution)/shard_map/dot_general | solution.py:42
  55.9 0.1 fusion.7
  56.0 0.0 copy-done.2
  56.0 0.0 copy-start.4
  56.0 2.3 %fusion = (f32[256]{0:T(256)S(1)}, bf16[256,8192]{1,0:T(8,128)(2,1)S(1)}) fusion(bf16[256,8192]{1,0:T(8,128)(2,1)S(1)} %copy-done.2, bf16[256,8320]{1,0:T(8,128)(2,1)S(1)} %convolution_bitcast_fusion, pred[256]{0:T(512)(128)(4,1)S(1)} %fusion.7), kind=kLoop, calls=%fused_computation.4 | loop fusion | flops 8388352 | bytes 12584192 | tf_op jit(solution)/shard_map/reduce_sum | solution.py:335
  58.3 0.0 copy-done.4
  58.3 0.0 copy-start.5
  58.3 1.2 %fusion.2.normed_ref = bf16[256,8192]{1,0:T(8,128)(2,1)S(1)} fusion(bf16[256,8192]{1,0:T(8,128)(2,1)S(1)} %get-tuple-element.10, f32[8192]{0:T(1024)S(1)} %copy-done.4, f32[256]{0:T(256)S(1)} %add_rsqrt_fusion), kind=kLoop, calls=%fused_computation.6 | loop fusion | flops 8388608 | bytes 8422400 | tf_op jit(solution)/shard_map/convert_element_type | solution.py:336
  59.5 0.0 copy-done
  59.5 0.0 copy-done.5
  59.5 0.0 copy-start.1
  59.5 0.0 copy-start.3
  59.5 1.3 %fusion.5 = bf16[256,128]{1,0:T(8,128)(2,1)S(1)} fusion(bf16[256,8192]{1,0:T(8,128)(2,1)S(1)} %fusion.2.normed_ref, bf16[8192,128]{1,0:T(8,128)(2,1)S(1)} %copy-done, f32[128]{0:T(128)S(1)} %copy-done.5), kind=kOutput, calls=%fused_computation.11 | convolution fusion | flops 536936448 | bytes 6357504 | tf_op jit(solution)/shard_map/dot_general | solution.py:338
  60.8 1.8 %copy-done.3 = bf16[8192,128]{1,0:T(8,128)(2,1)S(1)} copy-done((bf16[8192,128]{1,0:T(8,128)(2,1)S(1)}, bf16[8192,128]{1,0:T(8,128)(2,1)}, u32[]{:S(2)}) %copy-start.3) | copy-done | bytes 2097176
  62.6 1.3 %convolution_convert_fusion.1 = bf16[256,128]{1,0:T(8,128)(2,1)S(1)} fusion(bf16[256,8192]{1,0:T(8,128)(2,1)S(1)} %fusion.2.normed_ref, bf16[8192,128]{1,0:T(8,128)(2,1)S(1)} %copy-done.3), kind=kOutput, calls=%fused_computation.12 | convolution fusion | flops 536903680 | bytes 6356992 | tf_op jit(solution)/shard_map/dot_general | solution.py:337
  63.9 0.0 copy-done.1
  63.9 0.7 pad_maximum_fusion.1.block_ref
  64.6 27.2 %shard_map.110 = (bf16[4096,256]{1,0:T(8,128)(2,1)}, bf16[256,1024]{1,0:T(8,128)(2,1)}) custom-call(bf16[256,256]{1,0:T(8,128)(2,1)} %pad_maximum_fusion.1.block_ref, bf16[256,8192]{1,0:T(8,128)(2,1)} %copy-done.1, bf16[8192,1024]{1,0:T(8,128)(2,1)} %w_ref.1, f32[1,1024]{1,0:T(1,128)} %bitcast.15), custom_call_target="tpu_custom_call" | custom-call | tf_op jit(solution)/shard_map/pallas_call | solution.py:297
  91.8 19.6 %shard_map.111 = bf16[256,1024]{1,0:T(8,128)(2,1)} custom-call(s32[4096]{0:T(1024)} %doc_ref.1, bf16[256,1024]{1,0:T(8,128)(2,1)} %get-tuple-element.7.q_ref, bf16[4096,256]{1,0:T(8,128)(2,1)} %get-tuple-element.8.k_ref.v_ref, bf16[4096,256]{1,0:T(8,128)(2,1)} %get-tuple-element.8.k_ref.v_ref, s32[1,4096]{1,0:T(1,128)} %bitcast.16, s32[1,4096]{1,0:T(1,128)} %bitcast.17), custom_call_target="tpu_custom_call" | custom-call | flops 2147483648 | bytes 3145728 | tf_op jit(solution)/shard_map/pallas_call | solution.py:440
  (5 shorter events, 0.1 us)
Async XLA Ops:
  0.0 59.5 %copy-start = (bf16[8192,128]{1,0:T(8,128)(2,1)S(1)}, bf16[8192,128]{1,0:T(8,128)(2,1)}, u32[]{:S(2)}) copy-start(bf16[8192,128]{1,0:T(8,128)(2,1)} %param.20) | copy-start | bytes 6291460
  52.2 3.8 %copy-start.2 = (bf16[256,8192]{1,0:T(8,128)(2,1)S(1)}, bf16[256,8192]{1,0:T(8,128)(2,1)}, u32[]{:S(2)}) copy-start(bf16[256,8192]{1,0:T(8,128)(2,1)} %param.11) | copy-start | bytes 12582916
  56.0 2.3 %copy-start.4 = (f32[8192]{0:T(1024)S(1)}, f32[8192]{0:T(1024)}, u32[]{:S(2)}) copy-start(f32[8192]{0:T(1024)} %param.16) | copy-start | bytes 98308
  58.3 1.2 %copy-start.5 = (f32[128]{0:T(128)S(1)}, f32[128]{0:T(128)}, u32[]{:S(2)}) copy-start(f32[128]{0:T(128)} %param.21) | copy-start | bytes 1540
  59.5 4.4 %copy-start.1 = (bf16[256,8192]{1,0:T(8,128)(2,1)}, bf16[256,8192]{1,0:T(8,128)(2,1)S(1)}, u32[]{:S(2)}) copy-start(bf16[256,8192]{1,0:T(8,128)(2,1)S(1)} %fusion.2.normed_ref) | copy-start | bytes 12582916
  59.5 3.1 %copy-start.3 = (bf16[8192,128]{1,0:T(8,128)(2,1)S(1)}, bf16[8192,128]{1,0:T(8,128)(2,1)}, u32[]{:S(2)}) copy-start(bf16[8192,128]{1,0:T(8,128)(2,1)} %param.19) | copy-start | bytes 6291460

commit v20 on v18

--- a/solution.py
+++ b/solution.py
@@ -208,11 +208,11 @@
     up = seq_of(column + 1, layer, core)
     down = seq_of(column - 1, layer, core)
     barrier = pltpu.get_barrier_semaphore()
-    for peer in (mate, across, diagonal, up, down):
+    for peer in (mate, across, up, down):
         pl.semaphore_signal(
             barrier, inc=1, device_id=(peer, me_vis), device_id_type=pl.DeviceIdType.MESH
         )
-    pl.semaphore_wait(barrier, 5)
+    pl.semaphore_wait(barrier, 4)
 
     def rows_of(start, count):
         return out_ref.at[pl.ds(pl.multiple_of(start, rows), count)]
@@ -235,7 +235,6 @@
     local.start()
     send(block_ref, own, mate, 0)
     send(block_ref, own, across, 1)
-    send(block_ref, own, diagonal, 2)
     depth = normed_ref.shape[1] // 2
 
     def project(part):
@@ -255,8 +254,11 @@
     project(0)
     local.wait()
     link(block_ref, rows_of(mate * rows, rows), mate, 0).wait_recv()
-    link(block_ref, rows_of(across * rows, rows), across, 1).wait_recv()
-    link(block_ref, rows_of(diagonal * rows, rows), diagonal, 2).wait_recv()
+    crossed = rows_of(across * rows, rows)
+    link(block_ref, crossed, across, 1).wait_recv()
+    send(crossed, crossed, mate, 2)
+    landed = rows_of(diagonal * rows, rows)
+    link(landed, landed, mate, 2).wait_recv()
 
     def half(y, h):
         return rows_of((lax.rem(y + ring, ring) * 4 + h * 2) * rows, 2 * rows)

time: 114 us -> 120 us (1.053)
  the two profiles are of different devices: /device:TPU:57 before, /device:TPU:25 now
where the time goes in v20:
time: 120 us
  Pallas kernels  102 us (85%)
  matrix products  7.86 us (7%)
  other arithmetic  6.1 us (5%)
  local copies, waits for them, and re-layouts  3 us (2%)
    pallas_call x1, Pallas kernels, exchange_frames(): pl.pallas_call(exchange_kernel, out_shape=jax.ShapeDtypeStruct((vis_count...  47.9 us
    pallas_call x1, Pallas kernels, gather_keys(): pl.pallas_call(gather_kernel, out_shape=(jax.ShapeDtypeStruct((seq_count...  30.8 us
    pallas_call x1, Pallas kernels, flash_attention(): pl.pallas_call(flash_kernel, out_shape=jax.ShapeDtypeStruct((rows, width)...  23.2 us
    dot_general x1, matrix products, place_frames(): lax.dot_general(lookup.astype(incoming.dtype), incoming, (((1, 2), (0, 1)...  3.68 us

profile of v20, /device:TPU:25, one launch (start us, length us, event | category | flops | bytes accessed | tf_op | source)
XLA Modules:
  0.0 119.8 jit_solution(5276263673211805848)
XLA Ops:
  0.0 0.0 copy-start
  0.8 0.7 multiply_subtract_fusion
  1.5 0.1 fusion.6
  1.6 0.1 select_reduce_fusion
  1.7 0.1 fusion.10
  1.8 0.1 broadcast_in_dim.27
  1.9 1.5 %convolution_convert_fusion = bf16[32,8192]{1,0:T(8,128)(2,1)S(1)} fusion(bf16[32,8192]{1,0:T(8,128)(2,1)} %param.12, s32[32]{0:T(128)S(1)} %multiply_add_fusion, pred[32]{0:T(512)(128)(4,1)S(1)} %iota_compare_fusion.7), kind=kOutput, calls=%fused_computation.3 | convolution fusion | flops 17041408 | bytes 1048736 | tf_op jit(solution)/shard_map/dot_general | solution.py:31
  3.4 1.0 reshape.39.payload_ref
  4.5 47.9 %shard_map.109 = bf16[128,2,8320]{2,1,0:T(2,128)(2,1)} custom-call(bf16[16,2,8320]{2,1,0:T(2,128)(2,1)} %reshape.39.payload_ref), custom_call_target="tpu_custom_call" | custom-call | tf_op jit(solution)/shard_map/pallas_call | solution.py:175
  52.3 0.9 slice_convert_fusion.1
  53.3 0.1 copy.24
  53.3 0.0 copy-start.2
  53.3 3.7 %convolution_bitcast_fusion = bf16[256,8320]{1,0:T(8,128)(2,1)S(1)} fusion(bf16[128,2,8320]{2,1,0:T(2,128)(2,1)} %shard_map.109, s32[128,2]{0,1:T(2,128)S(1)} %bitcast.13), kind=kOutput, calls=%fused_computation | convolution fusion | flops 1090584576 | bytes 8520704 | tf_op jit(solution)/shard_map/dot_general | solution.py:42
  57.0 0.1 fusion.7
  57.1 0.0 copy-done.2
  57.1 0.0 copy-start.4
  57.2 2.3 %fusion = (f32[256]{0:T(256)S(1)}, bf16[256,8192]{1,0:T(8,128)(2,1)S(1)}) fusion(bf16[256,8192]{1,0:T(8,128)(2,1)S(1)} %copy-done.2, bf16[256,8320]{1,0:T(8,128)(2,1)S(1)} %convolution_bitcast_fusion, pred[256]{0:T(512)(128)(4,1)S(1)} %fusion.7), kind=kLoop, calls=%fused_computation.4 | loop fusion | flops 8388352 | bytes 12584192 | tf_op jit(solution)/shard_map/reduce_sum | solution.py:340
  59.5 0.0 copy-done.4
  59.5 0.0 copy-start.5
  59.5 1.2 fusion.2.normed_ref
  60.7 0.0 copy-done
  60.7 0.0 copy-done.5
  60.7 0.0 copy-start.1
  60.7 0.0 copy-start.3
  60.7 1.3 %fusion.5 = bf16[256,128]{1,0:T(8,128)(2,1)S(1)} fusion(bf16[256,8192]{1,0:T(8,128)(2,1)S(1)} %fusion.2.normed_ref, bf16[8192,128]{1,0:T(8,128)(2,1)S(1)} %copy-done, f32[128]{0:T(128)S(1)} %copy-done.5), kind=kOutput, calls=%fused_computation.11 | convolution fusion | flops 536936448 | bytes 6357504 | tf_op jit(solution)/shard_map/dot_general | solution.py:343
  62.0 1.8 %copy-done.3 = bf16[8192,128]{1,0:T(8,128)(2,1)S(1)} copy-done((bf16[8192,128]{1,0:T(8,128)(2,1)S(1)}, bf16[8192,128]{1,0:T(8,128)(2,1)}, u32[]{:S(2)}) %copy-start.3) | copy-done | bytes 2097176
  63.8 1.3 %convolution_convert_fusion.1 = bf16[256,128]{1,0:T(8,128)(2,1)S(1)} fusion(bf16[256,8192]{1,0:T(8,128)(2,1)S(1)} %fusion.2.normed_ref, bf16[8192,128]{1,0:T(8,128)(2,1)S(1)} %copy-done.3), kind=kOutput, calls=%fused_computation.12 | convolution fusion | flops 536903680 | bytes 6356992 | tf_op jit(solution)/shard_map/dot_general | solution.py:342
  65.1 0.0 copy-done.1
  65.1 0.7 pad_maximum_fusion.1.block_ref
  65.8 30.8 %shard_map.110 = (bf16[4096,256]{1,0:T(8,128)(2,1)}, bf16[256,1024]{1,0:T(8,128)(2,1)}) custom-call(bf16[256,256]{1,0:T(8,128)(2,1)} %pad_maximum_fusion.1.block_ref, bf16[256,8192]{1,0:T(8,128)(2,1)} %copy-done.1, bf16[8192,1024]{1,0:T(8,128)(2,1)} %w_ref.1, f32[1,1024]{1,0:T(1,128)} %bitcast.15), custom_call_target="tpu_custom_call" | custom-call | tf_op jit(solution)/shard_map/pallas_call | solution.py:302
  96.6 23.2 %shard_map.111 = bf16[256,1024]{1,0:T(8,128)(2,1)} custom-call(s32[4096]{0:T(1024)} %doc_ref.1, bf16[256,1024]{1,0:T(8,128)(2,1)} %get-tuple-element.7.q_ref, bf16[4096,256]{1,0:T(8,128)(2,1)} %get-tuple-element.8.k_ref.v_ref, bf16[4096,256]{1,0:T(8,128)(2,1)} %get-tuple-element.8.k_ref.v_ref, s32[1,4096]{1,0:T(1,128)} %bitcast.16, s32[1,4096]{1,0:T(1,128)} %bitcast.17), custom_call_target="tpu_custom_call" | custom-call | flops 2147483648 | bytes 3145728 | tf_op jit(solution)/shard_map/pallas_call | solution.py:444
  (5 shorter events, 0.1 us)
Async XLA Ops:
  0.0 60.7 %copy-start = (bf16[8192,128]{1,0:T(8,128)(2,1)S(1)}, bf16[8192,128]{1,0:T(8,128)(2,1)}, u32[]{:S(2)}) copy-start(bf16[8192,128]{1,0:T(8,128)(2,1)} %param.20) | copy-start | bytes 6291460
  53.3 3.8 %copy-start.2 = (bf16[256,8192]{1,0:T(8,128)(2,1)S(1)}, bf16[256,8192]{1,0:T(8,128)(2,1)}, u32[]{:S(2)}) copy-start(bf16[256,8192]{1,0:T(8,128)(2,1)} %param.11) | copy-start | bytes 12582916
  57.1 2.3 %copy-start.4 = (f32[8192]{0:T(1024)S(1)}, f32[8192]{0:T(1024)}, u32[]{:S(2)}) copy-start(f32[8192]{0:T(1024)} %param.16) | copy-start | bytes 98308
  59.5 1.2 %copy-start.5 = (f32[128]{0:T(128)S(1)}, f32[128]{0:T(128)}, u32[]{:S(2)}) copy-start(f32[128]{0:T(128)} %param.21) | copy-start | bytes 1540
  60.7 4.4 %copy-start.1 = (bf16[256,8192]{1,0:T(8,128)(2,1)}, bf16[256,8192]{1,0:T(8,128)(2,1)S(1)}, u32[]{:S(2)}) copy-start(bf16[256,8192]{1,0:T(8,128)(2,1)S(1)} %fusion.2.normed_ref) | copy-start | bytes 12582916
  60.7 3.1 %copy-start.3 = (bf16[8192,128]{1,0:T(8,128)(2,1)S(1)}, bf16[8192,128]{1,0:T(8,128)(2,1)}, u32[]{:S(2)}) copy-start(bf16[8192,128]{1,0:T(8,128)(2,1)} %param.19) | copy-start | bytes 6291460

commit v21 on v18

--- a/solution.py
+++ b/solution.py
@@ -264,20 +264,27 @@
     def quarter(y, h, q):
         return rows_of((lax.rem(y + ring, ring) * 4 + h * 2 + q) * rows, rows)
 
-    mine = half(column, core)
-    send(mine, mine, up, 3)
-    send(mine, mine, down, 4)
+    first_mine = quarter(column, core, 0)
+    second_mine = quarter(column, core, 1)
+    send(first_mine, first_mine, up, 3)
+    send(second_mine, second_mine, down, 4)
+    send(second_mine, second_mine, up, 10)
+    send(first_mine, first_mine, down, 11)
     project(1)
+    piece = quarter(column - 1, core, 0)
+    link(piece, piece, down, 3).wait_recv()
+    send(piece, piece, up, 5)
+    piece = quarter(column + 1, core, 1)
+    link(piece, piece, up, 4).wait_recv()
+    send(piece, piece, down, 6)
     below = half(column - 1, core)
-    link(below, below, down, 3).wait_recv()
+    rest = quarter(column - 1, core, 1)
+    link(rest, rest, down, 10).wait_recv()
     send(below, below, mate, 7)
-    piece = quarter(column - 1, core, 0)
-    send(piece, piece, up, 5)
     above = half(column + 1, core)
-    link(above, above, up, 4).wait_recv()
+    rest = quarter(column + 1, core, 0)
+    link(rest, rest, up, 11).wait_recv()
     send(above, above, mate, 9)
-    piece = quarter(column + 1, core, 1)
-    send(piece, piece, down, 6)
     q_ref[...] = (acc_ref[...] + bias_ref[...]).astype(q_ref.dtype)
     far_low = quarter(column + 2, core, 0)
     far_high = quarter(column + 2, core, 1)
@@ -311,8 +318,8 @@
         ],
         out_specs=(pl.BlockSpec(memory_space=pl.ANY), pl.BlockSpec(memory_space=pltpu.VMEM)),
         scratch_shapes=[
-            pltpu.SemaphoreType.DMA((10,)),
-            pltpu.SemaphoreType.DMA((10,)),
+            pltpu.SemaphoreType.DMA((12,)),
+            pltpu.SemaphoreType.DMA((12,)),
             pltpu.SemaphoreType.DMA((1,)),
             pltpu.VMEM((normed.shape[0], w_query.shape[1]), jnp.float32),
         ],

time: 114 us -> 118 us (1.035)
  the two profiles are of different devices: /device:TPU:57 before, /device:TPU:17 now
where the time goes in v21:
time: 118 us; the launch traced here: 117 us
  Pallas kernels  99.4 us (84%)
  matrix products  7.85 us (7%)
  other arithmetic  6.1 us (5%)
  local copies, waits for them, and re-layouts  3 us (3%)
    pallas_call x1, Pallas kernels, exchange_frames(): pl.pallas_call(exchange_kernel, out_shape=jax.ShapeDtypeStruct((vis_count...  49.5 us
    pallas_call x1, Pallas kernels, gather_keys(): pl.pallas_call(gather_kernel, out_shape=(jax.ShapeDtypeStruct((seq_count...  26.6 us
    pallas_call x1, Pallas kernels, flash_attention(): pl.pallas_call(flash_kernel, out_shape=jax.ShapeDtypeStruct((rows, width)...  23.2 us
    dot_general x1, matrix products, place_frames(): lax.dot_general(lookup.astype(incoming.dtype), incoming, (((1, 2), (0, 1)...  3.67 us

profile of v21, /device:TPU:17, one launch (start us, length us, event | category | flops | bytes accessed | tf_op | source)
XLA Modules:
  0.0 117.3 jit_solution(9347229994491820156)
XLA Ops:
  0.0 0.0 copy-start
  0.8 0.7 multiply_subtract_fusion
  1.5 0.1 fusion.6
  1.6 0.1 select_reduce_fusion
  1.7 0.1 fusion.10
  1.8 0.1 broadcast_in_dim.27
  1.9 1.5 %convolution_convert_fusion = bf16[32,8192]{1,0:T(8,128)(2,1)S(1)} fusion(bf16[32,8192]{1,0:T(8,128)(2,1)} %param.12, s32[32]{0:T(128)S(1)} %multiply_add_fusion, pred[32]{0:T(512)(128)(4,1)S(1)} %iota_compare_fusion.7), kind=kOutput, calls=%fused_computation.3 | convolution fusion | flops 17041408 | bytes 1048736 | tf_op jit(solution)/shard_map/dot_general | solution.py:31
  3.4 1.0 reshape.39.payload_ref
  4.5 49.5 %shard_map.109 = bf16[128,2,8320]{2,1,0:T(2,128)(2,1)} custom-call(bf16[16,2,8320]{2,1,0:T(2,128)(2,1)} %reshape.39.payload_ref), custom_call_target="tpu_custom_call" | custom-call | tf_op jit(solution)/shard_map/pallas_call | solution.py:175
  54.0 0.9 slice_convert_fusion.1
  54.9 0.1 copy.24
  55.0 0.0 copy-start.2
  55.0 3.7 %convolution_bitcast_fusion = bf16[256,8320]{1,0:T(8,128)(2,1)S(1)} fusion(bf16[128,2,8320]{2,1,0:T(2,128)(2,1)} %shard_map.109, s32[128,2]{0,1:T(2,128)S(1)} %bitcast.13), kind=kOutput, calls=%fused_computation | convolution fusion | flops 1090584576 | bytes 8520704 | tf_op jit(solution)/shard_map/dot_general | solution.py:42
  58.6 0.1 fusion.7
  58.8 0.0 copy-done.2
  58.8 0.0 copy-start.4
  58.8 2.3 %fusion = (f32[256]{0:T(256)S(1)}, bf16[256,8192]{1,0:T(8,128)(2,1)S(1)}) fusion(bf16[256,8192]{1,0:T(8,128)(2,1)S(1)} %copy-done.2, bf16[256,8320]{1,0:T(8,128)(2,1)S(1)} %convolution_bitcast_fusion, pred[256]{0:T(512)(128)(4,1)S(1)} %fusion.7), kind=kLoop, calls=%fused_computation.4 | loop fusion | flops 8388352 | bytes 12584192 | tf_op jit(solution)/shard_map/reduce_sum | solution.py:345
  61.1 0.0 copy-done.4
  61.1 0.0 copy-start.5
  61.1 1.2 %fusion.2.normed_ref = bf16[256,8192]{1,0:T(8,128)(2,1)S(1)} fusion(bf16[256,8192]{1,0:T(8,128)(2,1)S(1)} %get-tuple-element.10, f32[8192]{0:T(1024)S(1)} %copy-done.4, f32[256]{0:T(256)S(1)} %add_rsqrt_fusion), kind=kLoop, calls=%fused_computation.6 | loop fusion | flops 8388608 | bytes 8422400 | tf_op jit(solution)/shard_map/convert_element_type | solution.py:346
  62.3 0.0 copy-done
  62.3 0.0 copy-done.5
  62.3 0.0 copy-start.1
  62.3 0.0 copy-start.3
  62.3 1.3 %fusion.5 = bf16[256,128]{1,0:T(8,128)(2,1)S(1)} fusion(bf16[256,8192]{1,0:T(8,128)(2,1)S(1)} %fusion.2.normed_ref, bf16[8192,128]{1,0:T(8,128)(2,1)S(1)} %copy-done, f32[128]{0:T(128)S(1)} %copy-done.5), kind=kOutput, calls=%fused_computation.11 | convolution fusion | flops 536936448 | bytes 6357504 | tf_op jit(solution)/shard_map/dot_general | solution.py:348
  63.6 1.8 %copy-done.3 = bf16[8192,128]{1,0:T(8,128)(2,1)S(1)} copy-done((bf16[8192,128]{1,0:T(8,128)(2,1)S(1)}, bf16[8192,128]{1,0:T(8,128)(2,1)}, u32[]{:S(2)}) %copy-start.3) | copy-done | bytes 2097176
  65.4 1.3 %convolution_convert_fusion.1 = bf16[256,128]{1,0:T(8,128)(2,1)S(1)} fusion(bf16[256,8192]{1,0:T(8,128)(2,1)S(1)} %fusion.2.normed_ref, bf16[8192,128]{1,0:T(8,128)(2,1)S(1)} %copy-done.3), kind=kOutput, calls=%fused_computation.12 | convolution fusion | flops 536903680 | bytes 6356992 | tf_op jit(solution)/shard_map/dot_general | solution.py:347
  66.7 0.0 copy-done.1
  66.7 0.7 pad_maximum_fusion.1.block_ref
  67.4 26.6 %shard_map.110 = (bf16[4096,256]{1,0:T(8,128)(2,1)}, bf16[256,1024]{1,0:T(8,128)(2,1)}) custom-call(bf16[256,256]{1,0:T(8,128)(2,1)} %pad_maximum_fusion.1.block_ref, bf16[256,8192]{1,0:T(8,128)(2,1)} %copy-done.1, bf16[8192,1024]{1,0:T(8,128)(2,1)} %w_ref.1, f32[1,1024]{1,0:T(1,128)} %bitcast.15), custom_call_target="tpu_custom_call" | custom-call | tf_op jit(solution)/shard_map/pallas_call | solution.py:307
  94.1 23.2 %shard_map.111 = bf16[256,1024]{1,0:T(8,128)(2,1)} custom-call(s32[4096]{0:T(1024)} %doc_ref.1, bf16[256,1024]{1,0:T(8,128)(2,1)} %get-tuple-element.7.q_ref, bf16[4096,256]{1,0:T(8,128)(2,1)} %get-tuple-element.8.k_ref.v_ref, bf16[4096,256]{1,0:T(8,128)(2,1)} %get-tuple-element.8.k_ref.v_ref, s32[1,4096]{1,0:T(1,128)} %bitcast.16, s32[1,4096]{1,0:T(1,128)} %bitcast.17), custom_call_target="tpu_custom_call" | custom-call | flops 2147483648 | bytes 3145728 | tf_op jit(solution)/shard_map/pallas_call | solution.py:449
  (5 shorter events, 0.1 us)
Async XLA Ops:
  0.0 62.3 %copy-start = (bf16[8192,128]{1,0:T(8,128)(2,1)S(1)}, bf16[8192,128]{1,0:T(8,128)(2,1)}, u32[]{:S(2)}) copy-start(bf16[8192,128]{1,0:T(8,128)(2,1)} %param.20) | copy-start | bytes 6291460
  55.0 3.8 %copy-start.2 = (bf16[256,8192]{1,0:T(8,128)(2,1)S(1)}, bf16[256,8192]{1,0:T(8,128)(2,1)}, u32[]{:S(2)}) copy-start(bf16[256,8192]{1,0:T(8,128)(2,1)} %param.11) | copy-start | bytes 12582916
  58.8 2.3 %copy-start.4 = (f32[8192]{0:T(1024)S(1)}, f32[8192]{0:T(1024)}, u32[]{:S(2)}) copy-start(f32[8192]{0:T(1024)} %param.16) | copy-start | bytes 98308
  61.1 1.2 %copy-start.5 = (f32[128]{0:T(128)S(1)}, f32[128]{0:T(128)}, u32[]{:S(2)}) copy-start(f32[128]{0:T(128)} %param.21) | copy-start | bytes 1540
  62.3 4.4 %copy-start.1 = (bf16[256,8192]{1,0:T(8,128)(2,1)}, bf16[256,8192]{1,0:T(8,128)(2,1)S(1)}, u32[]{:S(2)}) copy-start(bf16[256,8192]{1,0:T(8,128)(2,1)S(1)} %fusion.2.normed_ref) | copy-start | bytes 12582916
  62.3 3.1 %copy-start.3 = (bf16[8192,128]{1,0:T(8,128)(2,1)S(1)}, bf16[8192,128]{1,0:T(8,128)(2,1)}, u32[]{:S(2)}) copy-start(bf16[8192,128]{1,0:T(8,128)(2,1)} %param.19) | copy-start | bytes 6291460

commit v22 on v18

--- a/solution.py
+++ b/solution.py
@@ -412,7 +412,10 @@
 def flash_attention(doc_ids, queries, keyval):
     rows, width = queries.shape
     key_rows = keyval.shape[0]
-    steps = min(key_rows // KEY_BLOCK, (DOC_SPAN + rows - 2) // KEY_BLOCK + 2)
+    steps = max(
+        (first + rows - 1) // KEY_BLOCK - max(0, first - DOC_SPAN + 1) // KEY_BLOCK + 1
+        for first in range(0, key_rows, rows)
+    )
     heads = width // HEAD_DIM
 
     def clamp(j, d):

time: 114 us -> 117 us (1.026)
  the two profiles are of different devices: /device:TPU:57 before, /device:TPU:48 now
where the time goes in v22:
time: 117 us; the launch traced here: 116 us
  Pallas kernels  98 us (84%)
  matrix products  7.83 us (7%)
  other arithmetic  6.1 us (5%)
  local copies, waits for them, and re-layouts  3 us (3%)
    pallas_call x1, Pallas kernels, exchange_frames(): pl.pallas_call(exchange_kernel, out_shape=jax.ShapeDtypeStruct((vis_count...  46.4 us
    pallas_call x1, Pallas kernels, gather_keys(): pl.pallas_call(gather_kernel, out_shape=(jax.ShapeDtypeStruct((seq_count...  28.6 us
    pallas_call x1, Pallas kernels, flash_attention(): pl.pallas_call(flash_kernel, out_shape=jax.ShapeDtypeStruct((rows, width)...  22.9 us
    dot_general x1, matrix products, place_frames(): lax.dot_general(lookup.astype(incoming.dtype), incoming, (((1, 2), (0, 1)...  3.67 us

profile of v22, /device:TPU:48, one launch (start us, length us, event | category | flops | bytes accessed | tf_op | source)
XLA Modules:
  0.0 115.9 jit_solution(4876024414479356631)
XLA Ops:
  0.0 0.0 copy-start
  0.8 0.7 multiply_subtract_fusion
  1.5 0.1 fusion.6
  1.6 0.1 select_reduce_fusion
  1.7 0.1 fusion.10
  1.8 0.1 broadcast_in_dim.27
  1.9 1.5 %convolution_convert_fusion = bf16[32,8192]{1,0:T(8,128)(2,1)S(1)} fusion(bf16[32,8192]{1,0:T(8,128)(2,1)} %param.12, s32[32]{0:T(128)S(1)} %multiply_add_fusion, pred[32]{0:T(512)(128)(4,1)S(1)} %iota_compare_fusion.7), kind=kOutput, calls=%fused_computation.3 | convolution fusion | flops 17041408 | bytes 1048736 | tf_op jit(solution)/shard_map/dot_general | solution.py:31
  3.4 1.0 reshape.39.payload_ref
  4.4 46.4 %shard_map.109 = bf16[128,2,8320]{2,1,0:T(2,128)(2,1)} custom-call(bf16[16,2,8320]{2,1,0:T(2,128)(2,1)} %reshape.39.payload_ref), custom_call_target="tpu_custom_call" | custom-call | tf_op jit(solution)/shard_map/pallas_call | solution.py:175
  50.9 0.9 slice_convert_fusion.1
  51.8 0.1 copy.24
  51.9 0.0 copy-start.2
  51.9 3.7 %convolution_bitcast_fusion = bf16[256,8320]{1,0:T(8,128)(2,1)S(1)} fusion(bf16[128,2,8320]{2,1,0:T(2,128)(2,1)} %shard_map.109, s32[128,2]{0,1:T(2,128)S(1)} %bitcast.13), kind=kOutput, calls=%fused_computation | convolution fusion | flops 1090584576 | bytes 8520704 | tf_op jit(solution)/shard_map/dot_general | solution.py:42
  55.6 0.1 fusion.7
  55.7 0.0 copy-done.2
  55.7 0.0 copy-start.4
  55.7 2.3 %fusion = (f32[256]{0:T(256)S(1)}, bf16[256,8192]{1,0:T(8,128)(2,1)S(1)}) fusion(bf16[256,8192]{1,0:T(8,128)(2,1)S(1)} %copy-done.2, bf16[256,8320]{1,0:T(8,128)(2,1)S(1)} %convolution_bitcast_fusion, pred[256]{0:T(512)(128)(4,1)S(1)} %fusion.7), kind=kLoop, calls=%fused_computation.4 | loop fusion | flops 8388352 | bytes 12584192 | tf_op jit(solution)/shard_map/reduce_sum | solution.py:338
  58.0 0.0 copy-done.4
  58.0 0.0 copy-start.5
  58.0 1.2 %fusion.2.normed_ref = bf16[256,8192]{1,0:T(8,128)(2,1)S(1)} fusion(bf16[256,8192]{1,0:T(8,128)(2,1)S(1)} %get-tuple-element.10, f32[8192]{0:T(1024)S(1)} %copy-done.4, f32[256]{0:T(256)S(1)} %add_rsqrt_fusion), kind=kLoop, calls=%fused_computation.6 | loop fusion | flops 8388608 | bytes 8422400 | tf_op jit(solution)/shard_map/convert_element_type | solution.py:339
  59.2 0.0 copy-done
  59.2 0.0 copy-done.5
  59.2 0.0 copy-start.1
  59.2 0.0 copy-start.3
  59.3 1.3 %fusion.5 = bf16[256,128]{1,0:T(8,128)(2,1)S(1)} fusion(bf16[256,8192]{1,0:T(8,128)(2,1)S(1)} %fusion.2.normed_ref, bf16[8192,128]{1,0:T(8,128)(2,1)S(1)} %copy-done, f32[128]{0:T(128)S(1)} %copy-done.5), kind=kOutput, calls=%fused_computation.11 | convolution fusion | flops 536936448 | bytes 6357504 | tf_op jit(solution)/shard_map/dot_general | solution.py:341
  60.6 1.8 %copy-done.3 = bf16[8192,128]{1,0:T(8,128)(2,1)S(1)} copy-done((bf16[8192,128]{1,0:T(8,128)(2,1)S(1)}, bf16[8192,128]{1,0:T(8,128)(2,1)}, u32[]{:S(2)}) %copy-start.3) | copy-done | bytes 2097176
  62.4 1.3 %convolution_convert_fusion.1 = bf16[256,128]{1,0:T(8,128)(2,1)S(1)} fusion(bf16[256,8192]{1,0:T(8,128)(2,1)S(1)} %fusion.2.normed_ref, bf16[8192,128]{1,0:T(8,128)(2,1)S(1)} %copy-done.3), kind=kOutput, calls=%fused_computation.12 | convolution fusion | flops 536903680 | bytes 6356992 | tf_op jit(solution)/shard_map/dot_general | solution.py:340
  63.6 0.0 copy-done.1
  63.7 0.7 pad_maximum_fusion.1.block_ref
  64.3 28.6 %shard_map.110 = (bf16[4096,256]{1,0:T(8,128)(2,1)}, bf16[256,1024]{1,0:T(8,128)(2,1)}) custom-call(bf16[256,256]{1,0:T(8,128)(2,1)} %pad_maximum_fusion.1.block_ref, bf16[256,8192]{1,0:T(8,128)(2,1)} %copy-done.1, bf16[8192,1024]{1,0:T(8,128)(2,1)} %w_ref.1, f32[1,1024]{1,0:T(1,128)} %bitcast.15), custom_call_target="tpu_custom_call" | custom-call | tf_op jit(solution)/shard_map/pallas_call | solution.py:300
  93.0 22.9 %shard_map.111 = bf16[256,1024]{1,0:T(8,128)(2,1)} custom-call(s32[4096]{0:T(1024)} %doc_ref.1, bf16[256,1024]{1,0:T(8,128)(2,1)} %get-tuple-element.7.q_ref, bf16[4096,256]{1,0:T(8,128)(2,1)} %get-tuple-element.8.k_ref.v_ref, bf16[4096,256]{1,0:T(8,128)(2,1)} %get-tuple-element.8.k_ref.v_ref, s32[1,4096]{1,0:T(1,128)} %bitcast.16, s32[1,4096]{1,0:T(1,128)} %bitcast.17), custom_call_target="tpu_custom_call" | custom-call | flops 2147483648 | bytes 3145728 | tf_op jit(solution)/shard_map/pallas_call | solution.py:445
  (5 shorter events, 0.1 us)
Async XLA Ops:
  0.0 59.2 %copy-start = (bf16[8192,128]{1,0:T(8,128)(2,1)S(1)}, bf16[8192,128]{1,0:T(8,128)(2,1)}, u32[]{:S(2)}) copy-start(bf16[8192,128]{1,0:T(8,128)(2,1)} %param.20) | copy-start | bytes 6291460
  51.9 3.8 %copy-start.2 = (bf16[256,8192]{1,0:T(8,128)(2,1)S(1)}, bf16[256,8192]{1,0:T(8,128)(2,1)}, u32[]{:S(2)}) copy-start(bf16[256,8192]{1,0:T(8,128)(2,1)} %param.11) | copy-start | bytes 12582916
  55.7 2.3 %copy-start.4 = (f32[8192]{0:T(1024)S(1)}, f32[8192]{0:T(1024)}, u32[]{:S(2)}) copy-start(f32[8192]{0:T(1024)} %param.16) | copy-start | bytes 98308
  58.0 1.2 %copy-start.5 = (f32[128]{0:T(128)S(1)}, f32[128]{0:T(128)}, u32[]{:S(2)}) copy-start(f32[128]{0:T(128)} %param.21) | copy-start | bytes 1540
  59.2 4.4 %copy-start.1 = (bf16[256,8192]{1,0:T(8,128)(2,1)}, bf16[256,8192]{1,0:T(8,128)(2,1)S(1)}, u32[]{:S(2)}) copy-start(bf16[256,8192]{1,0:T(8,128)(2,1)S(1)} %fusion.2.normed_ref) | copy-start | bytes 12582916
  59.2 3.1 %copy-start.3 = (bf16[8192,128]{1,0:T(8,128)(2,1)S(1)}, bf16[8192,128]{1,0:T(8,128)(2,1)}, u32[]{:S(2)}) copy-start(bf16[8192,128]{1,0:T(8,128)(2,1)} %param.19) | copy-start | bytes 6291460

commit v23 on v22

--- a/solution.py
+++ b/solution.py
@@ -189,9 +189,11 @@
 
 
 def gather_kernel(
-    block_ref, normed_ref, w_ref, bias_ref, out_ref, q_ref, send_sem, recv_sem, local_sem, acc_ref
+    key_ref, value_ref, normed_ref, w_ref, bias_ref, out_ref, q_ref, send_sem, recv_sem, local_sem,
+    acc_ref,
 ):
-    rows = block_ref.shape[0]
+    rows = key_ref.shape[0]
+    lane = key_ref.shape[1]
     me_seq = lax.axis_index("seq")
     me_vis = lax.axis_index("vis")
     column = me_seq // 4
@@ -230,12 +232,20 @@
         copy.start()
         sent.append(copy)
 
-    own = rows_of(me_seq * rows, rows)
-    local = pltpu.make_async_copy(block_ref, own, local_sem.at[0])
-    local.start()
-    send(block_ref, own, mate, 0)
-    send(block_ref, own, across, 1)
-    send(block_ref, own, diagonal, 2)
+    parts = ((key_ref, 0, 0), (value_ref, lane, 10))
+
+    def slab(start, offset):
+        return rows_of(start, rows).at[:, pl.ds(offset, lane)]
+
+    locals_ = []
+    for src_ref, offset, extra in parts:
+        own = slab(me_seq * rows, offset)
+        local = pltpu.make_async_copy(src_ref, own, local_sem.at[extra // 10])
+        local.start()
+        locals_.append(local)
+        send(src_ref, own, mate, 0 + extra)
+        send(src_ref, own, across, 1 + extra)
+        send(src_ref, own, diagonal, 2 + extra)
     depth = normed_ref.shape[1] // 2
 
     def project(part):
@@ -253,10 +263,12 @@
 
     acc_ref[...] = jnp.zeros(acc_ref.shape, jnp.float32)
     project(0)
-    local.wait()
-    link(block_ref, rows_of(mate * rows, rows), mate, 0).wait_recv()
-    link(block_ref, rows_of(across * rows, rows), across, 1).wait_recv()
-    link(block_ref, rows_of(diagonal * rows, rows), diagonal, 2).wait_recv()
+    for local in locals_:
+        local.wait()
+    for src_ref, offset, extra in parts:
+        link(src_ref, slab(mate * rows, offset), mate, 0 + extra).wait_recv()
+        link(src_ref, slab(across * rows, offset), across, 1 + extra).wait_recv()
+        link(src_ref, slab(diagonal * rows, offset), diagonal, 2 + extra).wait_recv()
 
     def half(y, h):
         return rows_of((lax.rem(y + ring, ring) * 4 + h * 2) * rows, 2 * rows)
@@ -295,8 +307,10 @@
 PROJ_TILE = 512
 
 
-def gather_keys(block, normed, w_query, q_bias, seq_count):
-    rows, width = block.shape
+def gather_keys(keys, values, normed, w_query, q_bias, seq_count):
+    rows, lane = keys.shape
+    width = 2 * lane
+    block = keys
     return pl.pallas_call(
         gather_kernel,
         out_shape=(
@@ -307,17 +321,18 @@
             pl.BlockSpec(memory_space=pl.ANY),
             pl.BlockSpec(memory_space=pl.ANY),
             pl.BlockSpec(memory_space=pl.ANY),
+            pl.BlockSpec(memory_space=pl.ANY),
             pl.BlockSpec(memory_space=pltpu.VMEM),
         ],
         out_specs=(pl.BlockSpec(memory_space=pl.ANY), pl.BlockSpec(memory_space=pltpu.VMEM)),
         scratch_shapes=[
-            pltpu.SemaphoreType.DMA((10,)),
-            pltpu.SemaphoreType.DMA((10,)),
-            pltpu.SemaphoreType.DMA((1,)),
+            pltpu.SemaphoreType.DMA((13,)),
+            pltpu.SemaphoreType.DMA((13,)),
+            pltpu.SemaphoreType.DMA((2,)),
             pltpu.VMEM((normed.shape[0], w_query.shape[1]), jnp.float32),
         ],
         compiler_params=pltpu.CompilerParams(collective_id=2, has_side_effects=True),
-    )(block, normed, w_query, q_bias.reshape(1, -1))
+    )(keys, values, normed, w_query, q_bias.reshape(1, -1))
 
 
 def on_device(
@@ -341,10 +356,9 @@
     value_rows = (jnp.dot(normed, w_value, preferred_element_type=jnp.float32) + v_bias).astype(
         jnp.bfloat16
     )
-    keyval = jnp.concatenate([key_rows, value_rows], axis=1)
     kv_heads = w_key.shape[1] // HEAD_DIM
     per_group = w_query.shape[1] // HEAD_DIM // kv_heads
-    incoming_keys, queries = gather_keys(keyval, normed, w_query, q_bias, seq_count)
+    incoming_keys, queries = gather_keys(key_rows, value_rows, normed, w_query, q_bias, seq_count)
     return flash_attention(doc_ids, queries, incoming_keys)
 
 

time: 117 us -> 114 us (0.974)
  the two profiles are of different devices: /device:TPU:48 before, /device:TPU:57 now
where the time goes in v23:
time: 114 us; the launch traced here: 113 us
  Pallas kernels  95 us (83%)
  matrix products  9.09 us (8%)
  other arithmetic  5.42 us (5%)
  local copies, waits for them, and re-layouts  2.4 us (2%)
    pallas_call x1, Pallas kernels, exchange_frames(): pl.pallas_call(exchange_kernel, out_shape=jax.ShapeDtypeStruct((vis_count...  47.8 us
    pallas_call x1, Pallas kernels, gather_keys(): pl.pallas_call(gather_kernel, out_shape=(jax.ShapeDtypeStruct((seq_count...  28 us
    pallas_call x1, Pallas kernels, flash_attention(): pl.pallas_call(flash_kernel, out_shape=jax.ShapeDtypeStruct((rows, width)...  19.2 us
    dot_general x1, matrix products, place_frames(): lax.dot_general(lookup.astype(incoming.dtype), incoming, (((1, 2), (0, 1)...  3.67 us
    reduce_sum x1, other arithmetic, on_device(): mean_square = jnp.mean(widened * widened, axis=1, keepdims=True)  2.28 us

profile of v23, /device:TPU:57, one launch (start us, length us, event | category | flops | bytes accessed | tf_op | source)
XLA Modules:
  0.0 112.9 jit_solution(11072896275854209856)
XLA Ops:
  0.0 0.0 copy-start
  0.8 0.7 multiply_subtract_fusion
  1.5 0.1 fusion.6
  1.6 0.1 select_reduce_fusion
  1.7 0.1 fusion.10
  1.8 0.1 broadcast_in_dim.27
  1.9 1.5 %convolution_convert_fusion = bf16[32,8192]{1,0:T(8,128)(2,1)S(1)} fusion(bf16[32,8192]{1,0:T(8,128)(2,1)} %param.12, s32[32]{0:T(128)S(1)} %multiply_add_fusion, pred[32]{0:T(512)(128)(4,1)S(1)} %iota_compare_fusion.7), kind=kOutput, calls=%fused_computation.3 | convolution fusion | flops 17041408 | bytes 1048736 | tf_op jit(solution)/shard_map/dot_general | solution.py:31
  3.4 1.0 reshape.39.payload_ref
  4.4 47.8 %shard_map.109 = bf16[128,2,8320]{2,1,0:T(2,128)(2,1)} custom-call(bf16[16,2,8320]{2,1,0:T(2,128)(2,1)} %reshape.39.payload_ref), custom_call_target="tpu_custom_call" | custom-call | tf_op jit(solution)/shard_map/pallas_call | solution.py:175
  52.3 0.9 slice_convert_fusion.1
  53.2 0.1 copy.18
  53.3 0.0 copy-start.2
  53.3 3.7 %convolution_bitcast_fusion = bf16[256,8320]{1,0:T(8,128)(2,1)S(1)} fusion(bf16[128,2,8320]{2,1,0:T(2,128)(2,1)} %shard_map.109, s32[128,2]{0,1:T(2,128)S(1)} %bitcast.13), kind=kOutput, calls=%fused_computation | convolution fusion | flops 1090584576 | bytes 8520704 | tf_op jit(solution)/shard_map/dot_general | solution.py:42
  56.9 0.1 fusion.7
  57.1 0.0 copy-done.2
  57.1 0.0 copy-start.4
  57.1 2.3 %fusion = (f32[256]{0:T(256)S(1)}, bf16[256,8192]{1,0:T(8,128)(2,1)S(1)}) fusion(bf16[256,8192]{1,0:T(8,128)(2,1)S(1)} %copy-done.2, bf16[256,8320]{1,0:T(8,128)(2,1)S(1)} %convolution_bitcast_fusion, pred[256]{0:T(512)(128)(4,1)S(1)} %fusion.7), kind=kLoop, calls=%fused_computation.4 | loop fusion | flops 8388352 | bytes 12584192 | tf_op jit(solution)/shard_map/reduce_sum | solution.py:353
  59.4 0.0 copy-done.4
  59.4 0.0 copy-start.5
  59.4 1.2 %fusion.2.normed_ref = bf16[256,8192]{1,0:T(8,128)(2,1)S(1)} fusion(bf16[256,8192]{1,0:T(8,128)(2,1)S(1)} %get-tuple-element.10, f32[8192]{0:T(1024)S(1)} %copy-done.4, f32[256]{0:T(256)S(1)} %add_rsqrt_fusion), kind=kLoop, calls=%fused_computation.6 | loop fusion | flops 8388608 | bytes 8422400 | tf_op jit(solution)/shard_map/convert_element_type | solution.py:354
  60.6 0.0 copy-done
  60.6 0.0 copy-done.5
  60.6 0.0 copy-start.1
  60.6 0.0 copy-start.3
  60.6 1.9 %fusion.5.value_ref = bf16[256,128]{1,0:T(8,128)(2,1)} fusion(bf16[256,8192]{1,0:T(8,128)(2,1)S(1)} %fusion.2.normed_ref, bf16[8192,128]{1,0:T(8,128)(2,1)S(1)} %copy-done, f32[128]{0:T(128)S(1)} %copy-done.5), kind=kOutput, calls=%fused_computation.11 | convolution fusion | flops 536936448 | bytes 6357504 | tf_op jit(solution)/shard_map/dot_general | solution.py:356
  62.5 0.2 copy-done.1
  62.8 1.0 copy-done.3
  63.8 1.9 %convolution_convert_fusion.1.key_ref = bf16[256,128]{1,0:T(8,128)(2,1)} fusion(bf16[256,8192]{1,0:T(8,128)(2,1)S(1)} %fusion.2.normed_ref, bf16[8192,128]{1,0:T(8,128)(2,1)S(1)} %copy-done.3), kind=kOutput, calls=%fused_computation.12 | convolution fusion | flops 536903680 | bytes 6356992 | tf_op jit(solution)/shard_map/dot_general | solution.py:355
  65.7 28.0 %shard_map.110 = (bf16[4096,256]{1,0:T(8,128)(2,1)}, bf16[256,1024]{1,0:T(8,128)(2,1)}) custom-call(bf16[256,128]{1,0:T(8,128)(2,1)} %convolution_convert_fusion.1.key_ref, bf16[256,128]{1,0:T(8,128)(2,1)} %fusion.5.value_ref, bf16[256,8192]{1,0:T(8,128)(2,1)} %copy-done.1, bf16[8192,1024]{1,0:T(8,128)(2,1)} %w_ref.1, f32[1,1024]{1,0:T(1,128)} %bitcast.15), custom_call_target="tpu_custom_call" | custom-call | tf_op jit(solution)/shard_map/pallas_call | solution.py:314
  93.6 19.2 %shard_map.111 = bf16[256,1024]{1,0:T(8,128)(2,1)} custom-call(s32[4096]{0:T(1024)} %doc_ref.1, bf16[256,1024]{1,0:T(8,128)(2,1)} %get-tuple-element.7.q_ref, bf16[4096,256]{1,0:T(8,128)(2,1)} %get-tuple-element.8.k_ref.v_ref, bf16[4096,256]{1,0:T(8,128)(2,1)} %get-tuple-element.8.k_ref.v_ref, s32[1,4096]{1,0:T(1,128)} %bitcast.16, s32[1,4096]{1,0:T(1,128)} %bitcast.17), custom_call_target="tpu_custom_call" | custom-call | flops 2147483648 | bytes 3145728 | tf_op jit(solution)/shard_map/pallas_call | solution.py:459
  (5 shorter events, 0.1 us)
Async XLA Ops:
  0.0 60.6 %copy-start = (bf16[8192,128]{1,0:T(8,128)(2,1)S(1)}, bf16[8192,128]{1,0:T(8,128)(2,1)}, u32[]{:S(2)}) copy-start(bf16[8192,128]{1,0:T(8,128)(2,1)} %param.20) | copy-start | bytes 6291460
  53.3 3.8 %copy-start.2 = (bf16[256,8192]{1,0:T(8,128)(2,1)S(1)}, bf16[256,8192]{1,0:T(8,128)(2,1)}, u32[]{:S(2)}) copy-start(bf16[256,8192]{1,0:T(8,128)(2,1)} %param.11) | copy-start | bytes 12582916
  57.1 2.3 %copy-start.4 = (f32[8192]{0:T(1024)S(1)}, f32[8192]{0:T(1024)}, u32[]{:S(2)}) copy-start(f32[8192]{0:T(1024)} %param.16) | copy-start | bytes 98308
  59.4 1.2 %copy-start.5 = (f32[128]{0:T(128)S(1)}, f32[128]{0:T(128)}, u32[]{:S(2)}) copy-start(f32[128]{0:T(128)} %param.21) | copy-start | bytes 1540
  60.6 2.2 %copy-start.1 = (bf16[256,8192]{1,0:T(8,128)(2,1)}, bf16[256,8192]{1,0:T(8,128)(2,1)S(1)}, u32[]{:S(2)}) copy-start(bf16[256,8192]{1,0:T(8,128)(2,1)S(1)} %fusion.2.normed_ref) | copy-start | bytes 12582916
  60.6 3.1 %copy-start.3 = (bf16[8192,128]{1,0:T(8,128)(2,1)S(1)}, bf16[8192,128]{1,0:T(8,128)(2,1)}, u32[]{:S(2)}) copy-start(bf16[8192,128]{1,0:T(8,128)(2,1)} %param.19) | copy-start | bytes 6291460

commit v24 on v23

--- a/solution.py
+++ b/solution.py
@@ -37,7 +37,7 @@
 
 
 def place_frames(text, incoming, incoming_place, width):
-    lookup = incoming_place[None] == jnp.arange(text.shape[0], dtype=jnp.int32)[:, None, None]
+    lookup = incoming_place[None] == jnp.arange(text.shape[0], dtype=jnp.int32).astype(incoming.dtype)[:, None, None]
     covered = jnp.any(lookup, axis=(1, 2))
     placed = lax.dot_general(
         lookup.astype(incoming.dtype), incoming, (((1, 2), (0, 1)), ((), ())),
@@ -347,7 +347,7 @@
     payload = frame_slots(frames, tile_pos, frame_count, shard_rows, seq_count, capacity)
     gathered = exchange_frames(payload, vis_count)
     width = text.shape[1]
-    incoming_place = gathered[:, :, width].astype(jnp.int32)
+    incoming_place = gathered[:, :, width]
     merged = place_frames(text, gathered, incoming_place, width)
     widened = merged.astype(jnp.float32)
     mean_square = jnp.mean(widened * widened, axis=1, keepdims=True)

time: 114 us -> 114 us (level)
  no operation moved by 1% of the time
where the time goes in v24:
time: 114 us; the launch traced here: 113 us
  Pallas kernels  95 us (83%)
  matrix products  9.14 us (8%)
  other arithmetic  4.59 us (4%)
  local copies, waits for them, and re-layouts  3.3 us (3%)
    pallas_call x1, Pallas kernels, exchange_frames(): pl.pallas_call(exchange_kernel, out_shape=jax.ShapeDtypeStruct((vis_count...  47.8 us
    pallas_call x1, Pallas kernels, gather_keys(): pl.pallas_call(gather_kernel, out_shape=(jax.ShapeDtypeStruct((seq_count...  27.9 us
    pallas_call x1, Pallas kernels, flash_attention(): pl.pallas_call(flash_kernel, out_shape=jax.ShapeDtypeStruct((rows, width)...  19.2 us
    dot_general x1, matrix products, place_frames(): lax.dot_general(lookup.astype(incoming.dtype), incoming, (((1, 2), (0, 1)...  3.71 us
    reduce_sum x1, other arithmetic, on_device(): mean_square = jnp.mean(widened * widened, axis=1, keepdims=True)  2.28 us

profile of v24, /device:TPU:57, one launch (start us, length us, event | category | flops | bytes accessed | tf_op | source)
XLA Modules:
  0.0 113.0 jit_solution(2047280168427105844)
XLA Ops:
  0.0 0.0 copy-start
  0.8 0.7 multiply_subtract_fusion
  1.5 0.1 fusion.6
  1.6 0.1 select_reduce_fusion
  1.8 0.1 fusion.11
  1.9 0.1 broadcast_in_dim.30
  1.9 1.5 %convolution_convert_fusion = bf16[32,8192]{1,0:T(8,128)(2,1)S(1)} fusion(bf16[32,8192]{1,0:T(8,128)(2,1)} %param.12, s32[32]{0:T(128)S(1)} %multiply_add_fusion, pred[32]{0:T(512)(128)(4,1)S(1)} %iota_compare_fusion.5), kind=kOutput, calls=%fused_computation.3 | convolution fusion | flops 17041408 | bytes 1048736 | tf_op jit(solution)/shard_map/dot_general | solution.py:31
  3.5 1.0 reshape.37.payload_ref
  4.5 47.8 %shard_map.109 = bf16[128,2,8320]{2,1,0:T(2,128)(2,1)} custom-call(bf16[16,2,8320]{2,1,0:T(2,128)(2,1)} %reshape.37.payload_ref), custom_call_target="tpu_custom_call" | custom-call | tf_op jit(solution)/shard_map/pallas_call | solution.py:175
  52.3 0.9 slice.7
  53.2 0.1 copy.16
  53.3 0.0 copy-start.2
  53.3 3.7 %convolution_bitcast_fusion = bf16[256,8320]{1,0:T(8,128)(2,1)S(1)} fusion(bf16[128,2,8320]{2,1,0:T(2,128)(2,1)} %shard_map.109, bf16[128,2]{0,1:T(2,128)(2,1)S(1)} %bitcast.13, bf16[256]{0:T(256)(128)(2,1)S(1)} %iota_convert_fusion), kind=kOutput, calls=%fused_computation | convolution fusion | flops 1090584576 | bytes 8520704 | tf_op jit(solution)/shard_map/dot_general | solution.py:42
  57.0 0.2 compare_reduce_fusion
  57.2 0.0 copy-done.2
  57.2 0.0 copy-start.4
  57.2 2.3 %fusion = (f32[256]{0:T(256)S(1)}, bf16[256,8192]{1,0:T(8,128)(2,1)S(1)}) fusion(bf16[256,8192]{1,0:T(8,128)(2,1)S(1)} %copy-done.2, bf16[256,8320]{1,0:T(8,128)(2,1)S(1)} %convolution_bitcast_fusion, pred[256]{0:T(512)(128)(4,1)S(1)} %compare_reduce_fusion), kind=kLoop, calls=%fused_computation.4 | loop fusion | flops 8388352 | bytes 12584192 | tf_op jit(solution)/shard_map/reduce_sum | solution.py:353
  59.5 0.0 copy-done.4
  59.5 0.0 copy-start.5
  59.5 1.2 %fusion.2.normed_ref = bf16[256,8192]{1,0:T(8,128)(2,1)S(1)} fusion(bf16[256,8192]{1,0:T(8,128)(2,1)S(1)} %get-tuple-element.10, f32[8192]{0:T(1024)S(1)} %copy-done.4, f32[256]{0:T(256)S(1)} %add_rsqrt_fusion), kind=kLoop, calls=%fused_computation.6 | loop fusion | flops 8388608 | bytes 8422400 | tf_op jit(solution)/shard_map/convert_element_type | solution.py:354
  60.7 0.0 copy-done
  60.8 0.0 copy-done.5
  60.8 0.0 copy-start.1
  60.8 0.0 copy-start.3
  60.8 1.9 %fusion.5.value_ref = bf16[256,128]{1,0:T(8,128)(2,1)} fusion(bf16[256,8192]{1,0:T(8,128)(2,1)S(1)} %fusion.2.normed_ref, bf16[8192,128]{1,0:T(8,128)(2,1)S(1)} %copy-done, f32[128]{0:T(128)S(1)} %copy-done.5), kind=kOutput, calls=%fused_computation.11 | convolution fusion | flops 536936448 | bytes 6357504 | tf_op jit(solution)/shard_map/dot_general | solution.py:356
  62.7 0.2 copy-done.1
  62.9 1.0 copy-done.3
  63.9 1.9 %convolution_convert_fusion.1.key_ref = bf16[256,128]{1,0:T(8,128)(2,1)} fusion(bf16[256,8192]{1,0:T(8,128)(2,1)S(1)} %fusion.2.normed_ref, bf16[8192,128]{1,0:T(8,128)(2,1)S(1)} %copy-done.3), kind=kOutput, calls=%fused_computation.12 | convolution fusion | flops 536903680 | bytes 6356992 | tf_op jit(solution)/shard_map/dot_general | solution.py:355
  65.8 27.9 %shard_map.110 = (bf16[4096,256]{1,0:T(8,128)(2,1)}, bf16[256,1024]{1,0:T(8,128)(2,1)}) custom-call(bf16[256,128]{1,0:T(8,128)(2,1)} %convolution_convert_fusion.1.key_ref, bf16[256,128]{1,0:T(8,128)(2,1)} %fusion.5.value_ref, bf16[256,8192]{1,0:T(8,128)(2,1)} %copy-done.1, bf16[8192,1024]{1,0:T(8,128)(2,1)} %w_ref.1, f32[1,1024]{1,0:T(1,128)} %bitcast.15), custom_call_target="tpu_custom_call" | custom-call | tf_op jit(solution)/shard_map/pallas_call | solution.py:314
  93.7 19.2 %shard_map.111 = bf16[256,1024]{1,0:T(8,128)(2,1)} custom-call(s32[4096]{0:T(1024)} %doc_ref.1, bf16[256,1024]{1,0:T(8,128)(2,1)} %get-tuple-element.7.q_ref, bf16[4096,256]{1,0:T(8,128)(2,1)} %get-tuple-element.8.k_ref.v_ref, bf16[4096,256]{1,0:T(8,128)(2,1)} %get-tuple-element.8.k_ref.v_ref, s32[1,4096]{1,0:T(1,128)} %bitcast.16, s32[1,4096]{1,0:T(1,128)} %bitcast.17), custom_call_target="tpu_custom_call" | custom-call | flops 2147483648 | bytes 3145728 | tf_op jit(solution)/shard_map/pallas_call | solution.py:459
  (6 shorter events, 0.1 us)
Async XLA Ops:
  0.0 60.7 %copy-start = (bf16[8192,128]{1,0:T(8,128)(2,1)S(1)}, bf16[8192,128]{1,0:T(8,128)(2,1)}, u32[]{:S(2)}) copy-start(bf16[8192,128]{1,0:T(8,128)(2,1)} %param.20) | copy-start | bytes 6291460
  53.3 3.9 %copy-start.2 = (bf16[256,8192]{1,0:T(8,128)(2,1)S(1)}, bf16[256,8192]{1,0:T(8,128)(2,1)}, u32[]{:S(2)}) copy-start(bf16[256,8192]{1,0:T(8,128)(2,1)} %param.11) | copy-start | bytes 12582916
  57.2 2.3 %copy-start.4 = (f32[8192]{0:T(1024)S(1)}, f32[8192]{0:T(1024)}, u32[]{:S(2)}) copy-start(f32[8192]{0:T(1024)} %param.16) | copy-start | bytes 98308
  59.5 1.2 %copy-start.5 = (f32[128]{0:T(128)S(1)}, f32[128]{0:T(128)}, u32[]{:S(2)}) copy-start(f32[128]{0:T(128)} %param.21) | copy-start | bytes 1540
  60.8 2.2 %copy-start.1 = (bf16[256,8192]{1,0:T(8,128)(2,1)}, bf16[256,8192]{1,0:T(8,128)(2,1)S(1)}, u32[]{:S(2)}) copy-start(bf16[256,8192]{1,0:T(8,128)(2,1)S(1)} %fusion.2.normed_ref) | copy-start | bytes 12582916
  60.8 3.1 %copy-start.3 = (bf16[8192,128]{1,0:T(8,128)(2,1)S(1)}, bf16[8192,128]{1,0:T(8,128)(2,1)}, u32[]{:S(2)}) copy-start(bf16[8192,128]{1,0:T(8,128)(2,1)} %param.19) | copy-start | bytes 6291460

commit v25 on v23

--- a/solution.py
+++ b/solution.py
@@ -304,7 +304,7 @@
         copy.wait_send()
 
 
-PROJ_TILE = 512
+PROJ_TILE = 1024
 
 
 def gather_keys(keys, values, normed, w_query, q_bias, seq_count):

time: 114 us -> 114 us (level)
  the two profiles are of different devices: /device:TPU:57 before, /device:TPU:40 now
where the time goes in v25:
time: 114 us; the launch traced here: 113 us
  Pallas kernels  94.8 us (83%)
  matrix products  9.11 us (8%)
  other arithmetic  5.42 us (5%)
  local copies, waits for them, and re-layouts  2.4 us (2%)
    pallas_call x1, Pallas kernels, exchange_frames(): pl.pallas_call(exchange_kernel, out_shape=jax.ShapeDtypeStruct((vis_count...  48 us
    pallas_call x1, Pallas kernels, gather_keys(): pl.pallas_call(gather_kernel, out_shape=(jax.ShapeDtypeStruct((seq_count...  27.5 us
    pallas_call x1, Pallas kernels, flash_attention(): pl.pallas_call(flash_kernel, out_shape=jax.ShapeDtypeStruct((rows, width)...  19.3 us
    dot_general x1, matrix products, place_frames(): lax.dot_general(lookup.astype(incoming.dtype), incoming, (((1, 2), (0, 1)...  3.67 us
    reduce_sum x1, other arithmetic, on_device(): mean_square = jnp.mean(widened * widened, axis=1, keepdims=True)  2.28 us

profile of v25, /device:TPU:40, one launch (start us, length us, event | category | flops | bytes accessed | tf_op | source)
XLA Modules:
  0.0 112.7 jit_solution(9554646065317166936)
XLA Ops:
  0.0 0.0 copy-start
  0.8 0.7 multiply_subtract_fusion
  1.5 0.1 fusion.6
  1.6 0.1 select_reduce_fusion
  1.7 0.1 fusion.10
  1.8 0.1 broadcast_in_dim.27
  1.9 1.5 %convolution_convert_fusion = bf16[32,8192]{1,0:T(8,128)(2,1)S(1)} fusion(bf16[32,8192]{1,0:T(8,128)(2,1)} %param.12, s32[32]{0:T(128)S(1)} %multiply_add_fusion, pred[32]{0:T(512)(128)(4,1)S(1)} %iota_compare_fusion.7), kind=kOutput, calls=%fused_computation.3 | convolution fusion | flops 17041408 | bytes 1048736 | tf_op jit(solution)/shard_map/dot_general | solution.py:31
  3.4 1.0 reshape.39.payload_ref
  4.5 48.0 %shard_map.109 = bf16[128,2,8320]{2,1,0:T(2,128)(2,1)} custom-call(bf16[16,2,8320]{2,1,0:T(2,128)(2,1)} %reshape.39.payload_ref), custom_call_target="tpu_custom_call" | custom-call | tf_op jit(solution)/shard_map/pallas_call | solution.py:175
  52.5 0.9 slice_convert_fusion.1
  53.4 0.1 copy.18
  53.5 0.0 copy-start.2
  53.5 3.7 %convolution_bitcast_fusion = bf16[256,8320]{1,0:T(8,128)(2,1)S(1)} fusion(bf16[128,2,8320]{2,1,0:T(2,128)(2,1)} %shard_map.109, s32[128,2]{0,1:T(2,128)S(1)} %bitcast.13), kind=kOutput, calls=%fused_computation | convolution fusion | flops 1090584576 | bytes 8520704 | tf_op jit(solution)/shard_map/dot_general | solution.py:42
  57.2 0.1 fusion.7
  57.3 0.0 copy-done.2
  57.3 0.0 copy-start.4
  57.3 2.3 %fusion = (f32[256]{0:T(256)S(1)}, bf16[256,8192]{1,0:T(8,128)(2,1)S(1)}) fusion(bf16[256,8192]{1,0:T(8,128)(2,1)S(1)} %copy-done.2, bf16[256,8320]{1,0:T(8,128)(2,1)S(1)} %convolution_bitcast_fusion, pred[256]{0:T(512)(128)(4,1)S(1)} %fusion.7), kind=kLoop, calls=%fused_computation.4 | loop fusion | flops 8388352 | bytes 12584192 | tf_op jit(solution)/shard_map/reduce_sum | solution.py:353
  59.6 0.0 copy-done.4
  59.6 0.0 copy-start.5
  59.6 1.2 %fusion.2.normed_ref = bf16[256,8192]{1,0:T(8,128)(2,1)S(1)} fusion(bf16[256,8192]{1,0:T(8,128)(2,1)S(1)} %get-tuple-element.10, f32[8192]{0:T(1024)S(1)} %copy-done.4, f32[256]{0:T(256)S(1)} %add_rsqrt_fusion), kind=kLoop, calls=%fused_computation.6 | loop fusion | flops 8388608 | bytes 8422400 | tf_op jit(solution)/shard_map/convert_element_type | solution.py:354
  60.8 0.0 copy-done
  60.8 0.0 copy-done.5
  60.8 0.0 copy-start.1
  60.8 0.0 copy-start.3
  60.9 1.9 %fusion.5.value_ref = bf16[256,128]{1,0:T(8,128)(2,1)} fusion(bf16[256,8192]{1,0:T(8,128)(2,1)S(1)} %fusion.2.normed_ref, bf16[8192,128]{1,0:T(8,128)(2,1)S(1)} %copy-done, f32[128]{0:T(128)S(1)} %copy-done.5), kind=kOutput, calls=%fused_computation.11 | convolution fusion | flops 536936448 | bytes 6357504 | tf_op jit(solution)/shard_map/dot_general | solution.py:356
  62.8 0.2 copy-done.1
  63.0 1.0 copy-done.3
  64.0 1.9 %convolution_convert_fusion.1.key_ref = bf16[256,128]{1,0:T(8,128)(2,1)} fusion(bf16[256,8192]{1,0:T(8,128)(2,1)S(1)} %fusion.2.normed_ref, bf16[8192,128]{1,0:T(8,128)(2,1)S(1)} %copy-done.3), kind=kOutput, calls=%fused_computation.12 | convolution fusion | flops 536903680 | bytes 6356992 | tf_op jit(solution)/shard_map/dot_general | solution.py:355
  65.9 27.5 %shard_map.110 = (bf16[4096,256]{1,0:T(8,128)(2,1)}, bf16[256,1024]{1,0:T(8,128)(2,1)}) custom-call(bf16[256,128]{1,0:T(8,128)(2,1)} %convolution_convert_fusion.1.key_ref, bf16[256,128]{1,0:T(8,128)(2,1)} %fusion.5.value_ref, bf16[256,8192]{1,0:T(8,128)(2,1)} %copy-done.1, bf16[8192,1024]{1,0:T(8,128)(2,1)} %w_ref.1, f32[1,1024]{1,0:T(1,128)} %bitcast.15), custom_call_target="tpu_custom_call" | custom-call | tf_op jit(solution)/shard_map/pallas_call | solution.py:314
  93.4 19.3 %shard_map.111 = bf16[256,1024]{1,0:T(8,128)(2,1)} custom-call(s32[4096]{0:T(1024)} %doc_ref.1, bf16[256,1024]{1,0:T(8,128)(2,1)} %get-tuple-element.7.q_ref, bf16[4096,256]{1,0:T(8,128)(2,1)} %get-tuple-element.8.k_ref.v_ref, bf16[4096,256]{1,0:T(8,128)(2,1)} %get-tuple-element.8.k_ref.v_ref, s32[1,4096]{1,0:T(1,128)} %bitcast.16, s32[1,4096]{1,0:T(1,128)} %bitcast.17), custom_call_target="tpu_custom_call" | custom-call | flops 2147483648 | bytes 3145728 | tf_op jit(solution)/shard_map/pallas_call | solution.py:459
  (5 shorter events, 0.1 us)
Async XLA Ops:
  0.0 60.8 %copy-start = (bf16[8192,128]{1,0:T(8,128)(2,1)S(1)}, bf16[8192,128]{1,0:T(8,128)(2,1)}, u32[]{:S(2)}) copy-start(bf16[8192,128]{1,0:T(8,128)(2,1)} %param.20) | copy-start | bytes 6291460
  53.5 3.8 %copy-start.2 = (bf16[256,8192]{1,0:T(8,128)(2,1)S(1)}, bf16[256,8192]{1,0:T(8,128)(2,1)}, u32[]{:S(2)}) copy-start(bf16[256,8192]{1,0:T(8,128)(2,1)} %param.11) | copy-start | bytes 12582916
  57.3 2.3 %copy-start.4 = (f32[8192]{0:T(1024)S(1)}, f32[8192]{0:T(1024)}, u32[]{:S(2)}) copy-start(f32[8192]{0:T(1024)} %param.16) | copy-start | bytes 98308
  59.6 1.2 %copy-start.5 = (f32[128]{0:T(128)S(1)}, f32[128]{0:T(128)}, u32[]{:S(2)}) copy-start(f32[128]{0:T(128)} %param.21) | copy-start | bytes 1540
  60.8 2.2 %copy-start.1 = (bf16[256,8192]{1,0:T(8,128)(2,1)}, bf16[256,8192]{1,0:T(8,128)(2,1)S(1)}, u32[]{:S(2)}) copy-start(bf16[256,8192]{1,0:T(8,128)(2,1)S(1)} %fusion.2.normed_ref) | copy-start | bytes 12582916
  60.8 3.1 %copy-start.3 = (bf16[8192,128]{1,0:T(8,128)(2,1)S(1)}, bf16[8192,128]{1,0:T(8,128)(2,1)}, u32[]{:S(2)}) copy-start(bf16[8192,128]{1,0:T(8,128)(2,1)} %param.19) | copy-start | bytes 6291460
